TPU v7x, 32 devices: a whole 2x2x4 slice. The times are simulated.
32 devices in a mesh: lon: 8 (over z, x), lat: 4 (over y, core).
Axes of the slice: x: 2, y: 2, z: 4, core: 2. Of those that a mesh axis runs over, the one named last changes fastest.
Arguments:
- tokens: bfloat16 [96, 48, 512], P('lon', 'lat'), may hold values from -6 to 6
- norm_gain: float32 [512], replicated, may hold values from 0.5 to 1.5
- qkv_weight: bfloat16 [512, 1536], replicated, may hold values from -3 to 3
- bias_table: float32 [16, 529], replicated, may hold values from -8 to 260
- proj_weight: bfloat16 [512, 512], replicated, may hold values from -0.25 to 0.25
- out_grad: bfloat16 [96, 48, 512], P('lon', 'lat'), may hold values from -6 to 6
Outputs:
- token_grad: bfloat16 [96, 48, 512], P('lon', 'lat')
- qkv_grad: float32 [786432], P(('lon', 'lat'))
All inputs are finite; a program needn't handle non-finite values.
Results may differ from a plain program's by a relative error of at most 0.0092.
Values may be sent and summed in bfloat16 or wider, within the bound.
No kernel may reach another device: no remote copies, remote signals or barrier semaphores. Data moves between devices by JAX's collectives and lax.ppermute only.
A program may use at most 128 MiB of HBM per device.

v0:
```python
import math

import jax
import jax.numpy as jnp
from jax import lax
from jax.sharding import PartitionSpec as P

WIN = 12


def from_behind(block, axis, distance):
    devices = range(lax.axis_size(axis))
    route = [((i - distance) % len(devices), i) for i in devices]
    return lax.ppermute(block, axis, route)


def window_backward(
    shifted_tokens,
    shifted_grad,
    norm_gain,
    qkv_weight,
    bias_table,
    proj_weight,
    lat_start,
    lat_total,
):
    span_lon, span_lat, width = shifted_tokens.shape
    heads = bias_table.shape[0]
    head_size = width // heads
    edge = WIN // 2
    rows_lon = span_lon // WIN
    rows_lat = span_lat // WIN
    area = WIN * WIN
    factor = head_size ** (-0.5)
    inputs = shifted_tokens.astype(jnp.float32)
    centred = inputs - jnp.mean(inputs, axis=-1, keepdims=True)
    inverse = lax.rsqrt(jnp.mean(centred * centred, axis=-1, keepdims=True) + 1e-05)
    unit = centred * inverse
    normed = (unit * norm_gain).astype(jnp.bfloat16).reshape(-1, width)
    projected = jnp.dot(normed, qkv_weight, preferred_element_type=jnp.float32).astype(jnp.bfloat16)
    blocks = projected.reshape(rows_lon, WIN, rows_lat, WIN, 3, heads, head_size)
    blocks = blocks.transpose(4, 0, 2, 5, 1, 3, 6).reshape(
        3, rows_lon, rows_lat, heads, area, head_size
    )
    query = blocks[0]
    keys = blocks[1]
    values = blocks[2]
    offsets = jnp.arange(2 * WIN - 1, dtype=jnp.int32)
    places = jnp.arange(WIN, dtype=jnp.int32)
    lookup = (
        places[:, None, None] - places[None, :, None] + WIN - 1 == offsets[None, None, :]
    ).astype(jnp.float32)
    table = bias_table.reshape(heads, 2 * WIN - 1, 2 * WIN - 1)
    relative = jnp.einsum(
        "hab,ija,klb->hikjl", table, lookup, lookup, precision=lax.Precision.HIGHEST
    ).reshape(heads, area, area)
    position = lat_start + jnp.arange(span_lat, dtype=jnp.int32)
    group = (position >= lat_total - WIN).astype(jnp.int32) + (position >= lat_total - edge).astype(
        jnp.int32
    )
    group = jnp.broadcast_to(group.reshape(rows_lat, 1, WIN), (rows_lat, WIN, WIN)).reshape(
        rows_lat, area
    )
    allowed = (group[:, :, None] == group[:, None, :])[None, :, None]
    scores = (
        jnp.einsum("nmhid,nmhjd->nmhij", query, keys, preferred_element_type=jnp.float32) * factor
        + relative
    )
    scores = jnp.where(allowed, scores, -1e30)
    peak = jnp.max(scores, axis=-1, keepdims=True)
    weights = jnp.exp(scores - peak)
    probs = weights / jnp.sum(weights, axis=-1, keepdims=True)
    probs_low = probs.astype(jnp.bfloat16)
    upstream = jnp.dot(
        shifted_grad.reshape(-1, width), proj_weight.T, preferred_element_type=jnp.float32
    ).astype(jnp.bfloat16)
    upstream = upstream.reshape(rows_lon, WIN, rows_lat, WIN, heads, head_size).transpose(
        0, 2, 4, 1, 3, 5
    )
    upstream = upstream.reshape(rows_lon, rows_lat, heads, area, head_size)
    grad_values = jnp.einsum(
        "nmhij,nmhid->nmhjd", probs_low, upstream, preferred_element_type=jnp.float32
    )
    grad_probs = jnp.einsum(
        "nmhid,nmhjd->nmhij", upstream, values, preferred_element_type=jnp.float32
    )
    centre = jnp.sum(probs * grad_probs, axis=-1, keepdims=True)
    grad_scores = (probs * (grad_probs - centre) * factor).astype(jnp.bfloat16)
    grad_query = jnp.einsum(
        "nmhij,nmhjd->nmhid", grad_scores, keys, preferred_element_type=jnp.float32
    )
    grad_keys = jnp.einsum(
        "nmhij,nmhid->nmhjd", grad_scores, query, preferred_element_type=jnp.float32
    )
    stacked = jnp.stack([grad_query, grad_keys, grad_values]).astype(jnp.bfloat16)
    grad_qkv = stacked.reshape(3, rows_lon, rows_lat, heads, WIN, WIN, head_size)
    grad_qkv = grad_qkv.transpose(1, 4, 2, 5, 0, 3, 6).reshape(-1, 3 * width)
    grad_normed = jnp.dot(grad_qkv, qkv_weight.T, preferred_element_type=jnp.float32).reshape(
        span_lon, span_lat, width
    )
    scaled = grad_normed * norm_gain
    result = shifted_grad.astype(jnp.float32) + inverse * (
        scaled
        - jnp.mean(scaled, axis=-1, keepdims=True)
        - unit * jnp.mean(scaled * unit, axis=-1, keepdims=True)
    )
    weight_grad = jnp.dot(grad_qkv.T, normed, preferred_element_type=jnp.float32)
    return (result.astype(jnp.bfloat16), weight_grad)


def shards(tokens, norm_gain, qkv_weight, bias_table, proj_weight, out_grad):
    span_lon, span_lat, width = tokens.shape
    edge = WIN // 2
    arrived = from_behind((tokens[:, :edge], out_grad[:, :edge]), "lat", -1)
    lat_tokens = jnp.concatenate([tokens[:, edge:], arrived[0]], axis=1)
    lat_grad = jnp.concatenate([out_grad[:, edge:], arrived[1]], axis=1)
    landed = from_behind((lat_tokens[:edge], lat_grad[:edge]), "lon", -1)
    shifted_tokens = jnp.concatenate([lat_tokens[edge:], landed[0]], axis=0)
    shifted_grad = jnp.concatenate([lat_grad[edge:], landed[1]], axis=0)
    lat_start = lax.axis_index("lat") * span_lat
    lat_total = span_lat * lax.axis_size("lat")
    result, weight_grad = window_backward(
        shifted_tokens,
        shifted_grad,
        norm_gain,
        qkv_weight,
        bias_table,
        proj_weight,
        lat_start,
        lat_total,
    )
    trailing = from_behind(result[span_lon - edge :], "lon", 1)
    lon_back = jnp.concatenate([trailing, result[: span_lon - edge]], axis=0)
    bottom = from_behind(lon_back[:, span_lat - edge :], "lat", 1)
    token_grad = jnp.concatenate([bottom, lon_back[:, : span_lat - edge]], axis=1)
    flat_grad = weight_grad.reshape(-1)
    factor = 1.0 / math.sqrt(span_lon * lax.axis_size("lon") * span_lat * lax.axis_size("lat"))
    summed = lax.psum_scatter(flat_grad, ("lon", "lat"), scatter_dimension=0, tiled=True)
    return (token_grad, summed * factor)


def solution(mesh):
    placed = (P("lon", "lat", None), P(), P(), P(), P(), P("lon", "lat", None))
    return jax.shard_map(
        shards,
        mesh=mesh,
        in_specs=placed,
        out_specs=(P("lon", "lat", None), P(("lon", "lat"))),
        check_vma=False,
    )
```

profile of v0, /device:TPU:0, one launch (start us, length us, event | category | flops | bytes accessed | tf_op | source)
XLA Modules:
  0.0 259.0 jit_solution(11439710915390380479)
XLA Ops:
  7.2 1.1 fusion.50
  8.4 2.5 collective-permute-start.2
  10.8 1.0 fusion.51
  11.8 0.7 collective-permute-start
  12.6 0.9 reshape.355
  13.5 0.8 convolution_bitcast_fusion.2
  14.3 9.0 %convolution_bitcast_fusion = f32[16,12,12,12,12]{4,0,2,3,1:T(8,128)} fusion(f32[12,12,16,23,1]{3,1,2,0,4:T(8,128)S(1)} %convolution_bitcast_fusion.2, s32[12,12]{1,0:T(8,128)S(1)} %subtract_add_fusion), kind=kOutput, calls=%fused_computation.2 | convolution fusion | flops 91573488 | bytes 1539648 | tf_op jit(solution)/shard_map/hab,ija,klb->hikjl/dot_general | solution.py:54
  23.4 0.7 broadcast_compare_fusion
  24.1 24.3 %copy.62 = f32[16,12,12,12,12]{2,1,4,3,0:T(8,128)} copy(f32[16,12,12,12,12]{4,0,2,3,1:T(8,128)} %convolution_bitcast_fusion) | data formatting | bytes 2654208 | tf_op jit(solution)/shard_map/broadcast_in_dim;reshape | solution.py:66
  48.4 13.4 %reshape.360 = f32[16,144,144]{1,2,0:T(8,128)} reshape(f32[16,12,12,12,12]{2,1,4,3,0:T(8,128)} %copy.62) | data formatting | bytes 2654208 | tf_op jit(solution)/shard_map/broadcast_in_dim;reshape | solution.py:66
  61.9 4.6 %collective-permute-start.3 = (bf16[6,12,512]{2,1,0:T(8,128)(2,1)S(1)}, bf16[6,12,512]{2,1,0:T(8,128)(2,1)S(1)}, u32[]{:S(2)}, u32[]{:S(2)}) collective-permute-start(bf16[6,12,512]{2,1,0:T(8,128)(2,1)S(1)} %get-tuple-element.12), channel_id=1, source_target_pairs={{4,0},{8,4},{12,8},{16,12},{20,16},{24,20},{28,24},{0,28},{5,1},{9... | collective-permute-start | bytes 221192 | tf_op jit(solution)/shard_map/ppermute | solution.py:14
  66.5 0.6 collective-permute-start.1
  67.1 2.4 collective-permute-done.3
  69.6 0.1 convert_reduce_fusion
  69.7 0.2 multiply_reduce_fusion.2
  70.0 1.2 collective-permute-done.1
  71.2 0.6 copy-done.8
  71.9 0.3 convolution_convert_fusion.2
  72.3 0.3 reshape.348
  72.6 1.2 copy.41
  74.0 1.2 convolution_convert_fusion
  75.2 2.1 reshape.343
  77.3 0.5 copy.70
  77.9 0.3 fusion.48
  78.2 1.2 copy.36
  79.4 0.5 copy.37
  79.9 2.2 add_select_fusion
  82.2 2.1 fusion.52
  84.3 3.0 %convolution_convert_fusion.1 = bf16[16,144,32]{1,2,0:T(8,128)(2,1)S(1)} fusion(bf16[16,144,32]{1,2,0:T(8,128)(2,1)S(1)} %copy-done.3, f32[16,144]{1,0:T(8,128)S(1)} %get-tuple-element.19, f32[16,144,144]{1,2,0:T(8,128)} %copy-done.1), kind=kOutput, calls=%fused_computation.18 | convolution fusion | flops 22305168 | bytes 1631232 | tf_op jit(solution)/shard_map/nmhij,nmhid->nmhjd/dot_general | solution.py:81
  87.3 1.8 fusion.26
  89.2 4.5 %fusion.19 = bf16[16,144,32]{1,2,0:T(8,128)(2,1)S(1)} fusion(bf16[16,144,32]{1,2,0:T(8,128)(2,1)S(1)} %copy-done.4, f32[16,144,144]{1,2,0:T(8,128)} %fusion.26, f32[16,144,144]{1,2,0:T(8,128)} %get-tuple-element.20, f32[16,144]{1,0:T(8,128)S(1)} %get-tuple-element.19), kind=kOutput, calls=%fused_computation.20 | convolution fusion | flops 23632272 | bytes 2958336 | tf_op jit(solution)/shard_map/nmhij,nmhid->nmhjd/dot_general | solution.py:92
  93.7 5.3 %fusion.16 = bf16[16,144,32]{1,2,0:T(8,128)(2,1)} fusion(bf16[16,144,32]{1,2,0:T(8,128)(2,1)S(1)} %copy.37, f32[16,144,144]{1,2,0:T(8,128)} %fusion.26, f32[16,144,144]{1,2,0:T(8,128)} %get-tuple-element.20, f32[16,144]{1,0:T(8,128)S(1)} %get-tuple-element.19), kind=kOutput, calls=%fused_computation.19 | convolution fusion | flops 23632272 | bytes 2958336 | tf_op jit(solution)/shard_map/nmhij,nmhjd->nmhid/dot_general | solution.py:89
  99.0 0.5 copy.51
  99.5 0.5 copy.48
  100.0 1.4 copy.45
  101.4 0.4 maximum_bitcast_fusion
  101.9 0.3 copy.52
  102.2 2.4 dot_general.44
  104.6 2.4 reshape.351
  107.0 1.9 fusion.47
  108.9 0.2 multiply_convert_fusion.1
  109.2 0.6 convolution_bitcast_fusion.1
  109.8 2.5 copy.64
  112.4 7.3 %collective-permute-done.4 = bf16[6,12,512]{2,1,0:T(8,128)(2,1)S(1)} collective-permute-done((bf16[6,12,512]{2,1,0:T(8,128)(2,1)S(1)}, bf16[6,12,512]{2,1,0:T(8,128)(2,1)S(1)}, u32[]{:S(2)}, u32[]{:S(2)}) %collective-permute-start.4) | collective-permute-done | bytes 73760 | tf_op jit(solution)/shard_map/ppermute | solution.py:14
  119.8 4.3 %collective-permute-done.5 = bf16[12,6,512]{2,1,0:T(8,128)(2,1)S(1)} collective-permute-done((bf16[12,6,512]{2,1,0:T(8,128)(2,1)S(1)}, bf16[12,6,512]{2,1,0:T(8,128)(2,1)S(1)}, u32[]{:S(2)}, u32[]{:S(2)}) %collective-permute-start.5) | collective-permute-done | bytes 73760 | tf_op jit(solution)/shard_map/ppermute | solution.py:14
  124.1 0.8 fusion.28
  124.9 125.8 %all-reduce.3.cloned.1.call-done = f32[786432]{0:T(1024)} async-done(((f32[786432]{0:T(1024)}), f32[786432]{0:T(1024)}) %all-reduce.3.cloned.1.call-update) | async-done | bytes 3145744
  250.6 1.5 dynamic-slice_multiply_fusion
  (47 shorter events, 0.9 us)
Async XLA Ops:
  7.2 66.8 %copy-start = (bf16[512,1536]{1,0:T(8,128)(2,1)S(1)}, bf16[512,1536]{1,0:T(8,128)(2,1)}, u32[]{:S(2)}) copy-start(bf16[512,1536]{1,0:T(8,128)(2,1)} %param.8) | copy-start | bytes 4718596
  7.2 243.5 %all-reduce.3.cloned.1.call-start = ((), (), s32[]{:S(2)}) async-start(), calls=%async_computation | async-start | bytes 6291456
  8.4 53.4 %collective-permute-start.2 = (bf16[12,6,512]{2,1,0:T(8,128)(2,1)S(1)}, bf16[12,6,512]{2,1,0:T(8,128)(2,1)S(1)}, u32[]{:S(2)}, u32[]{:S(2)}) collective-permute-start(bf16[12,6,512]{2,1,0:T(8,128)(2,1)S(1)} %get-tuple-element.14), channel_id=1, source_target_pairs={{1,0},{2,1},{3,2},{0,3},{5,4},{6,5},{7,6},{4,7},{9,8},{10,9},{11,1... | collective-permute-start | bytes 221192 | tf_op jit(solution)/shard_map/ppermute | solution.py:14
  11.8 54.6 %collective-permute-start = (bf16[12,6,512]{2,1,0:T(8,128)(2,1)S(1)}, bf16[12,6,512]{2,1,0:T(8,128)(2,1)S(1)}, u32[]{:S(2)}, u32[]{:S(2)}) collective-permute-start(bf16[12,6,512]{2,1,0:T(8,128)(2,1)S(1)} %get-tuple-element.18), channel_id=1, source_target_pairs={{1,0},{2,1},{3,2},{0,3},{5,4},{6,5},{7,6},{4,7},{9,8},{10,9},{11,1... | collective-permute-start | bytes 221192 | tf_op jit(solution)/shard_map/ppermute | solution.py:14
  48.4 23.6 %copy-start.7 = (bf16[512,512]{1,0:T(8,128)(2,1)S(1)}, bf16[512,512]{1,0:T(8,128)(2,1)}, u32[]{:S(2)}) copy-start(bf16[512,512]{1,0:T(8,128)(2,1)} %param.10) | copy-start | bytes 1572868
  61.9 7.7 %collective-permute-start.3 = (bf16[6,12,512]{2,1,0:T(8,128)(2,1)S(1)}, bf16[6,12,512]{2,1,0:T(8,128)(2,1)S(1)}, u32[]{:S(2)}, u32[]{:S(2)}) collective-permute-start(bf16[6,12,512]{2,1,0:T(8,128)(2,1)S(1)} %get-tuple-element.12), channel_id=1, source_target_pairs={{4,0},{8,4},{12,8},{16,12},{20,16},{24,20},{28,24},{0,28},{5,1},{9... | collective-permute-start | bytes 221192 | tf_op jit(solution)/shard_map/ppermute | solution.py:14
  66.5 5.4 %copy-start.5 = (bf16[6,12,512]{2,1,0:T(8,128)(2,1)}, bf16[6,12,512]{2,1,0:T(8,128)(2,1)S(1)}, u32[]{:S(2)}) copy-start(bf16[6,12,512]{2,1,0:T(8,128)(2,1)S(1)} %get-tuple-element.15) | copy-start | bytes 221188
  66.5 4.7 %collective-permute-start.1 = (bf16[6,12,512]{2,1,0:T(8,128)(2,1)S(1)}, bf16[6,12,512]{2,1,0:T(8,128)(2,1)S(1)}, u32[]{:S(2)}, u32[]{:S(2)}) collective-permute-start(bf16[6,12,512]{2,1,0:T(8,128)(2,1)S(1)} %get-tuple-element.16), channel_id=1, source_target_pairs={{4,0},{8,4},{12,8},{16,12},{20,16},{24,20},{28,24},{0,28},{5,1},{9... | collective-permute-start | bytes 221192 | tf_op jit(solution)/shard_map/ppermute | solution.py:14
  69.7 4.3 %copy-start.10 = (f32[512]{0:T(512)S(1)}, f32[512]{0:T(512)}, u32[]{:S(2)}) copy-start(f32[512]{0:T(512)} %param.7) | copy-start | bytes 6148
  71.2 0.6 copy-start.8
  82.1 2.1 copy-start.1
  82.2 2.1 copy-start.3
  87.3 1.9 copy-start.4
  107.0 1.9 copy-start.6
  107.0 1.9 copy-start.9
  107.0 1.9 copy-start.11
  107.0 2.2 copy-start.2
  112.4 7.4 %collective-permute-start.4 = (bf16[6,12,512]{2,1,0:T(8,128)(2,1)S(1)}, bf16[6,12,512]{2,1,0:T(8,128)(2,1)S(1)}, u32[]{:S(2)}, u32[]{:S(2)}) collective-permute-start(bf16[6,12,512]{2,1,0:T(8,128)(2,1)S(1)} %get-tuple-element.9), channel_id=1, source_target_pairs={{28,0},{0,4},{4,8},{8,12},{12,16},{16,20},{20,24},{24,28},{29,1},{... | collective-permute-start | bytes 221192 | tf_op jit(solution)/shard_map/ppermute | solution.py:14
  119.8 4.4 %collective-permute-start.5 = (bf16[12,6,512]{2,1,0:T(8,128)(2,1)S(1)}, bf16[12,6,512]{2,1,0:T(8,128)(2,1)S(1)}, u32[]{:S(2)}, u32[]{:S(2)}) collective-permute-start(bf16[12,6,512]{2,1,0:T(8,128)(2,1)S(1)} %fusion.32), channel_id=1, source_target_pairs={{3,0},{0,1},{1,2},{2,3},{7,4},{4,5},{5,6},{6,7},{11,8},{8,9},{9,10... | collective-permute-start | bytes 221192 | tf_op jit(solution)/shard_map/ppermute | solution.py:14
Sparse Core Ops, SparseCore 0:
  112.5 138.1 all-reduce.2
where the time goes:
time: 260 us; the launch traced here: 259 us
  waiting for transfers between devices  141 us (54%)
  local copies, waits for them, and re-layouts  58 us (22%)
  matrix products  30.8 us (12%)
  between operations  14.4 us (6%)
  starting transfers between devices  8.51 us (3%)
  other arithmetic  6.32 us (2%)
    unnamed x2, waiting for transfers between devices  126 us
    another operation x2, local copies, waits for them, and re-layouts, window_backward(): jnp.einsum('nmhid,nmhjd->nmhij', query, keys, preferred_element_type=jnp....  37.7 us
    ppermute x6, waiting for transfers between devices, from_behind(): return lax.ppermute(block, axis, route)  15.2 us
    dot_general x2, matrix products, window_backward(): jnp.einsum('hab,ija,klb->hikjl', table, lookup, lookup, precision=lax.Pre...  9.82 us
    ppermute x6, starting transfers between devices, from_behind(): return lax.ppermute(block, axis, route)  8.47 us
    another operation x6, local copies, waits for them, and re-layouts  5.3 us
    dot_general x1, matrix products, window_backward(): jnp.einsum('nmhij,nmhjd->nmhid', grad_scores, keys, preferred_element_typ...  5.3 us
  transfers between devices with their start and end apart: 7, of which 5 were waited for; matrix products, arithmetic and copies ran while one was open for 20% of the time, Pallas kernels for 0%

commit v1 on v0

v1 whole, which is shorter than its diff:
```python
import functools
import math

import jax
import jax.numpy as jnp
from jax import lax
from jax.experimental import pallas as pl
from jax.experimental.pallas import tpu as pltpu
from jax.sharding import PartitionSpec as P

WIN = 12
EDGE = WIN // 2
AREA = WIN * WIN
QUARTER = EDGE * EDGE
SPAN = 2 * WIN - 1
LANES = 128
F32 = jnp.float32
BF16 = jnp.bfloat16
AXES = ("lon", "lat")


def dot(a, b, ca, cb):
    return lax.dot_general(a, b, (((ca,), (cb,)), ((), ())), preferred_element_type=F32)


def bias_kernel(flag_ref, table_ref, low_ref, high_ref, pad_ref):
    heads, count = table_ref.shape
    width = pad_ref.shape[1]
    pad_ref[...] = jnp.zeros_like(pad_ref)
    pad_ref[:, :count] = table_ref[...]
    flat = pad_ref[...]
    shifts = WIN + EDGE
    moved = jnp.concatenate(
        [flat] + [pltpu.roll(flat, width - b, 1) for b in range(1, shifts)], axis=0
    )
    row = lax.broadcasted_iota(jnp.int32, (width, 2 * LANES), 0)
    col = lax.broadcasted_iota(jnp.int32, (width, 2 * LANES), 1)
    place = col + (SPAN - EDGE) * ((col * 10923) >> 16)
    pick = jnp.where((row == place) & (col < SPAN * EDGE), 1.0, 0.0).astype(BF16)
    first = moved.astype(BF16)
    rest = moved - first.astype(F32)
    second = rest.astype(BF16)
    third = (rest - second.astype(F32)).astype(BF16)
    packed = dot(first, pick, 1, 0) + (dot(second, pick, 1, 0) + dot(third, pick, 1, 0))
    half = WIN * EDGE
    lane = lax.broadcasted_iota(jnp.int32, (heads, LANES), 1)
    apart = jnp.where(flag_ref[0] > 0, -1e30, 0.0).astype(F32)
    for v in range(WIN):
        b = WIN - 1 - v
        side, inner = divmod(v, EDGE)
        near = packed[heads * b : heads * (b + 1)] + (apart if side == 1 else 0.0)
        far = packed[heads * (b + EDGE) : heads * (b + EDGE + 1)] + (apart if side == 0 else 0.0)
        for u in range(WIN):
            a = EDGE * (WIN - 1 - u)
            left = pltpu.roll(near, (2 * LANES - a) % (2 * LANES), 1) if a else near
            right = pltpu.roll(far, (half - a) % (2 * LANES), 1)
            start = heads * (side * half + u * EDGE + inner)
            low_ref[start : start + heads, :] = jnp.where(
                lane < half, left[:, :LANES], right[:, :LANES]
            )
            high_ref[start : start + heads, :] = right[:, LANES:]


def relative_bias(flag, table):
    heads = table.shape[0]
    shape = jax.ShapeDtypeStruct((AREA * heads, LANES), F32)
    width = -(-table.shape[1] // LANES) * LANES
    return pl.pallas_call(
        bias_kernel,
        out_shape=(shape, shape),
        in_specs=[
            pl.BlockSpec(memory_space=pltpu.SMEM),
            pl.BlockSpec(memory_space=pltpu.VMEM),
        ],
        out_specs=(pl.BlockSpec(memory_space=pltpu.VMEM),) * 2,
        scratch_shapes=[pltpu.VMEM((heads, width), F32)],
        cost_estimate=pl.CostEstimate(
            flops=2 * 3 * 18 * heads * width * 256, bytes_accessed=2 * AREA * heads * 512, transcendentals=0
        ),
        name="relative_bias",
    )(flag, table)


def window_kernel(
    blocks,
    order_ref,
    own_ref,
    lon_ref,
    lat_ref,
    diag_ref,
    gain_ref,
    weight_ref,
    proj_ref,
    low_ref,
    high_ref,
    own_out,
    lon_out,
    lat_out,
    diag_out,
    *rest,
):
    weight_outs = rest[:-5]
    token_ref, grad_ref, qkv_ref, turned_ref, placed_ref = rest[-5:]
    width = gain_ref.shape[1]
    heads = low_ref.shape[0] // AREA
    size = width // heads
    group = LANES // size
    factor = size ** (-0.5)
    for k, ref in enumerate((own_ref, lon_ref, lat_ref, diag_ref)):
        token_ref[QUARTER * k : QUARTER * (k + 1), :] = ref[0].astype(F32)
        grad_ref[QUARTER * k : QUARTER * (k + 1), :] = ref[1].astype(F32)
    inputs = token_ref[...]
    gain = gain_ref[...]
    centred = inputs - jnp.mean(inputs, axis=-1, keepdims=True)
    inverse = lax.rsqrt(jnp.mean(centred * centred, axis=-1, keepdims=True) + 1e-05)
    unit = centred * inverse
    normed = (unit * gain).astype(BF16)
    qkv_ref[...] = dot(normed, weight_ref[...], 1, 0).astype(BF16)
    upstream = dot(grad_ref[...].astype(BF16), proj_ref[...], 1, 1).astype(BF16)
    lane = lax.broadcasted_iota(jnp.int32, (AREA, LANES), 1)
    zero = jnp.zeros((AREA, LANES), BF16)
    for g in range(width // LANES):
        cols = slice(LANES * g, LANES * (g + 1))
        query = qkv_ref[:, LANES * g : LANES * (g + 1)]
        keys = qkv_ref[:, width + LANES * g : width + LANES * (g + 1)]
        values = qkv_ref[:, 2 * width + LANES * g : 2 * width + LANES * (g + 1)]
        up = upstream[:, cols]
        keys_turned = keys.T
        here = [(lane >= size * n) & (lane < size * (n + 1)) for n in range(group)]
        all_scores = dot(
            jnp.concatenate([jnp.where(m, keys, zero) for m in here], axis=0), query, 1, 1
        )
        all_grads = dot(
            jnp.concatenate([jnp.where(m, values, zero) for m in here], axis=0), up, 1, 1
        )
        grad_values = None
        for n in range(group):
            h = g * group + n
            rows = slice(AREA * n, AREA * (n + 1))
            bias = jnp.concatenate(
                [
                    low_ref[pl.ds(h, AREA, stride=heads), :],
                    high_ref[pl.ds(h, AREA, stride=heads), :],
                ],
                axis=1,
            )[:, :AREA]
            scores = all_scores[rows] * factor + bias
            peak = jnp.max(scores, axis=0, keepdims=True)
            weights = jnp.exp(scores - peak)
            probs = weights * (1.0 / jnp.sum(weights, axis=0, keepdims=True))
            grad_probs = all_grads[rows]
            centre = jnp.sum(probs * grad_probs, axis=0, keepdims=True)
            grad_scores = (probs * (grad_probs - centre) * factor).astype(BF16)
            part_values = dot(probs.astype(BF16), jnp.where(here[n], up, zero), 1, 0)
            part_keys = dot(grad_scores, jnp.where(here[n], query, zero), 1, 0)
            part_query = dot(keys_turned[size * n : size * (n + 1)], grad_scores, 1, 0)
            turned_ref[h * size : (h + 1) * size, :] = part_query.astype(BF16)
            if grad_values is None:
                grad_values, grad_keys = part_values, part_keys
            else:
                grad_values = grad_values + part_values
                grad_keys = grad_keys + part_keys
        grad_values = grad_values.astype(BF16)
        grad_keys = grad_keys.astype(BF16)
        qkv_ref[:, LANES * g : LANES * (g + 1)] = turned_ref[cols, :].T
        qkv_ref[:, width + LANES * g : width + LANES * (g + 1)] = grad_keys
        qkv_ref[:, 2 * width + LANES * g : 2 * width + LANES * (g + 1)] = grad_values
        turned_ref[width + LANES * g : width + LANES * (g + 1), :] = grad_keys.T
        turned_ref[2 * width + LANES * g : 2 * width + LANES * (g + 1), :] = grad_values.T
    grad_normed = dot(qkv_ref[...], weight_ref[...], 1, 1)
    scaled = grad_normed * gain
    result = grad_ref[...] + inverse * (
        scaled
        - jnp.mean(scaled, axis=-1, keepdims=True)
        - unit * jnp.mean(scaled * unit, axis=-1, keepdims=True)
    )
    token_ref[...] = result
    for k, ref in enumerate((own_out, lon_out, lat_out, diag_out)):
        ref[...] = token_ref[QUARTER * k : QUARTER * (k + 1), :].astype(BF16)
    if blocks is None:
        weight_outs[0][...] = dot(turned_ref[...], normed, 1, 0)
    else:
        rows = 3 * width // len(blocks)
        for slot, offset in enumerate(blocks):
            start = pl.multiple_of((order_ref[0] ^ offset) * rows, rows)
            placed_ref[slot * rows : (slot + 1) * rows, :] = turned_ref[pl.ds(start, rows), :]
        total = 3 * width // len(weight_outs)
        for k, ref in enumerate(weight_outs):
            ref[...] = dot(placed_ref[total * k : total * (k + 1), :], normed, 1, 0).astype(BF16)


def window_backward(order, quarters, gain, weight, proj, low, high, blocks):
    width = proj.shape[0]
    piece = jax.ShapeDtypeStruct((QUARTER, width), BF16)
    if blocks is None:
        weight_shapes = (jax.ShapeDtypeStruct((3 * width, width), F32),)
    else:
        weight_shapes = (jax.ShapeDtypeStruct((3 * width // 2, width), BF16),) * 2
    vmem = pl.BlockSpec(memory_space=pltpu.VMEM)
    return pl.pallas_call(
        functools.partial(window_kernel, blocks),
        out_shape=(piece,) * 4 + weight_shapes,
        in_specs=[pl.BlockSpec(memory_space=pltpu.SMEM)] + [vmem] * 9,
        out_specs=(vmem,) * (4 + len(weight_shapes)),
        scratch_shapes=[
            pltpu.VMEM((AREA, width), F32),
            pltpu.VMEM((AREA, width), F32),
            pltpu.VMEM((AREA, 3 * width), BF16),
            pltpu.VMEM((3 * width, AREA), BF16),
            pltpu.VMEM((3 * width, AREA), BF16),
        ],
        compiler_params=pltpu.CompilerParams(vmem_limit_bytes=32 << 20),
        cost_estimate=pl.CostEstimate(
            flops=2 * AREA * width * width * 10, bytes_accessed=6 << 20, transcendentals=16 * AREA * AREA
        ),
        name="window_backward",
    )(order, *quarters, gain, weight, proj, low, high)


def exchange(block, offset, total):
    return lax.ppermute(block, AXES, [(i, i ^ offset) for i in range(total)])


def gather_sum(slots, offsets, total):
    arrived = [exchange(slots[k + 1], offset, total) for k, offset in enumerate(offsets)]
    summed = slots[0].astype(F32)
    for piece in arrived:
        summed = summed + piece.astype(F32)
    return summed


def shards(tokens, norm_gain, qkv_weight, bias_table, proj_weight, out_grad):
    span_lon, span_lat, width = tokens.shape
    lons, lats = lax.axis_size("lon"), lax.axis_size("lat")
    total = lons * lats
    place = lax.axis_index("lon") * lats + lax.axis_index("lat")

    def route(step_lon, step_lat):
        return [
            (a * lats + b, (a + step_lon) % lons * lats + (b + step_lat) % lats)
            for a in range(lons)
            for b in range(lats)
        ]

    def quarter(at_lon, at_lat):
        return jnp.stack(
            [
                x[at_lon : at_lon + EDGE, at_lat : at_lat + EDGE].reshape(QUARTER, width)
                for x in (tokens, out_grad)
            ]
        )

    quarters = [
        quarter(EDGE, EDGE),
        lax.ppermute(quarter(0, EDGE), AXES, route(-1, 0)),
        lax.ppermute(quarter(EDGE, 0), AXES, route(0, -1)),
        lax.ppermute(quarter(0, 0), AXES, route(-1, -1)),
    ]
    flag = (lax.axis_index("lat") == lats - 1).astype(jnp.int32).reshape(1)
    low, high = relative_bias(flag, bias_table)
    rows = 3 * width // total
    staged = total % 32 == 0 and 3 * width % total == 0 and rows % 16 == 0
    if staged:
        far = total // 8
        blocks = tuple(
            core + 2 * plane + 8 * line
            for core in range(2)
            for plane in range(4)
            for line in range(far)
        )
    else:
        blocks = None
    own, to_lon, to_lat, to_diag, *weight_grads = window_backward(
        place.astype(jnp.int32).reshape(1),
        quarters,
        norm_gain.reshape(1, width),
        qkv_weight,
        proj_weight,
        low,
        high,
        blocks,
    )
    factor = 1.0 / math.sqrt(span_lon * lons * span_lat * lats)
    if staged:
        keep, send = weight_grads
        shape = (4, far, rows, width)
        pair = gather_sum([keep.reshape(shape), send.reshape(shape)], [1], total).astype(BF16)
        plane = gather_sum([pair[k] for k in range(4)], [2, 4, 6], total).astype(BF16)
        line = gather_sum([plane[k] for k in range(far)], [8 * k for k in range(1, far)], total)
        summed = line.reshape(-1)
    else:
        summed = lax.psum_scatter(
            weight_grads[0].reshape(-1), AXES, scatter_dimension=0, tiled=True
        )
    from_lon = lax.ppermute(to_lon, AXES, route(1, 0))
    from_lat = lax.ppermute(to_lat, AXES, route(0, 1))
    from_diag = lax.ppermute(to_diag, AXES, route(1, 1))
    cell = (EDGE, EDGE, width)
    upper = jnp.concatenate([from_diag.reshape(cell), from_lon.reshape(cell)], axis=1)
    lower = jnp.concatenate([from_lat.reshape(cell), own.reshape(cell)], axis=1)
    token_grad = jnp.concatenate([upper, lower], axis=0)
    return (token_grad, summed * factor)


def solution(mesh):
    placed = (P("lon", "lat", None), P(), P(), P(), P(), P("lon", "lat", None))
    return jax.shard_map(
        shards,
        mesh=mesh,
        in_specs=placed,
        out_specs=(P("lon", "lat", None), P(("lon", "lat"))),
        check_vma=False,
    )
```

time: 260 us -> 50.6 us (0.19)
  waiting for transfers between devices: 141 us -> 17 us
  local copies, waits for them, and re-layouts: 58 us -> 5.64 us
  matrix products: 30.8 us -> 0 us
  between operations: 14.4 us -> 0.89 us
  Pallas kernels: 0 us -> 8.85 us
  starting transfers between devices: 8.51 us -> 16.8 us
  other arithmetic: 6.32 us -> 1.17 us
    unnamed x2 -> x0, waiting for transfers between devices: 126 us -> none
    another operation x8, local copies, waits for them, and re-layouts: 43 us -> 0.14 us  [quarter(): jnp.stack([x[at_lon:at_lon + EDGE, at_lat:at_lat + EDGE].reshape(QUARTER,...]
    dot_general x11 -> x0, matrix products: 30.8 us -> none  [the longest x2 9.82 us: window_backward(): jnp.einsum('hab,ija,klb->hikjl', table, lookup, lookup, precision=lax.Pre...]
    pallas_call x0 -> x2, Pallas kernels: none -> 8.85 us  [the longest x1 4.81 us: window_backward(): pl.pallas_call(functools.partial(window_kernel, blocks), out_shape=(piece...]
    ppermute x6 -> x13, starting transfers between devices: 8.47 us -> 16.8 us  [the longest x7 7.78 us: exchange(): return lax.ppermute(block, AXES, [(i, i ^ offset) for i in range(total)])]
    reshape x6 -> x4, local copies, waits for them, and re-layouts: 6.27 us -> 0.08 us  [the longest x2 0.04 us: shards(): lower = jnp.concatenate([from_lat.reshape(cell), own.reshape(cell)], axis=1)]
    ppermute x6 -> x13, waiting for transfers between devices: 15.2 us -> 17 us  [the longest x1 7.86 us: shards(): from_diag = lax.ppermute(to_diag, AXES, route(1, 1))]
  transfers between devices with their start and end apart: 7 -> 13, of which waited for: 5 -> 6; matrix products, arithmetic and copies ran while one was open for 20% -> 2% of each run, Pallas kernels for 0% -> 8%
where the time goes in v1:
time: 50.6 us; the launch traced here: 50.3 us
  waiting for transfers between devices  17 us (34%)
  starting transfers between devices  16.8 us (33%)
  Pallas kernels  8.85 us (17%)
  local copies, waits for them, and re-layouts  5.64 us (11%)
  other arithmetic  1.17 us (2%)
  between operations  0.89 us (2%)
    ppermute x1, waiting for transfers between devices, shards(): from_diag = lax.ppermute(to_diag, AXES, route(1, 1))  7.86 us
    ppermute x7, starting transfers between devices, exchange(): return lax.ppermute(block, AXES, [(i, i ^ offset) for i in range(total)])  7.78 us
    ppermute x7, waiting for transfers between devices, exchange(): return lax.ppermute(block, AXES, [(i, i ^ offset) for i in range(total)])  5.78 us
    pallas_call x1, Pallas kernels, window_backward(): pl.pallas_call(functools.partial(window_kernel, blocks), out_shape=(piece...  4.81 us
    ppermute x1, starting transfers between devices, shards(): lax.ppermute(quarter(0, EDGE), AXES, route(-1, 0))  4.58 us
    pallas_call x1, Pallas kernels, relative_bias(): pl.pallas_call(bias_kernel, out_shape=(shape, shape), in_specs=[pl.BlockS...  4.04 us
    unnamed x11, local copies, waits for them, and re-layouts  3.21 us
    ppermute x1, waiting for transfers between devices, shards(): from_lat = lax.ppermute(to_lat, AXES, route(0, 1))  2.97 us
  transfers between devices with their start and end apart: 13, of which 6 were waited for; matrix products, arithmetic and copies ran while one was open for 2% of the time, Pallas kernels for 8%

profile of v1, /device:TPU:0, one launch (start us, length us, event | category | flops | bytes accessed | tf_op | source)
XLA Modules:
  0.0 50.3 jit_solution(12268340680249149179)
XLA Ops:
  0.6 0.0 copy-start.3
  0.6 0.0 copy-start
  0.7 0.0 copy-start.4
  0.7 1.1 %fusion.8 = (bf16[6,6,512]{2,1,0:T(8,128)(2,1)S(1)}, bf16[6,6,512]{2,1,0:T(8,128)(2,1)S(1)}, bf16[6,6,512]{2,1,0:T(8,128)(2,1)S(1)}, bf16[6,6,512]{2,1,0:T(8,128)(2,1)S(1)}) fusion(bf16[12,12,512]{2,1,0:T(8,128)(2,1)} %param.6), kind=kLoop, calls=%fused_computation.24 | loop fusion | bytes 294912 | tf_op jit(solution)/shard_map/slice | solution.py:248
  1.8 1.0 %fusion.9 = (bf16[6,6,512]{2,1,0:T(8,128)(2,1)S(1)}, bf16[6,6,512]{2,1,0:T(8,128)(2,1)S(1)}, bf16[6,6,512]{2,1,0:T(8,128)(2,1)S(1)}, bf16[6,6,512]{2,1,0:T(8,128)(2,1)S(1)}) fusion(bf16[12,12,512]{2,1,0:T(8,128)(2,1)} %param.11), kind=kLoop, calls=%fused_computation.25 | loop fusion | bytes 294912 | tf_op jit(solution)/shard_map/slice | solution.py:248
  2.9 2.5 %collective-permute-start.1 = (bf16[2,36,512]{2,1,0:T(8,128)(2,1)S(1)}, bf16[2,36,512]{2,1,0:T(8,128)(2,1)S(1)}, u32[]{:S(2)}, u32[]{:S(2)}) collective-permute-start(bf16[2,36,512]{2,1,0:T(8,128)(2,1)S(1)} %pad_maximum_fusion.2), channel_id=1, source_target_pairs={{0,3},{1,0},{2,1},{3,2},{4,7},{5,4},{6,5},{7,6},{8,11},{9,8},{10,9... | collective-permute-start | bytes 221192 | tf_op jit(solution)/shard_map/ppermute | solution.py:256
  5.4 4.6 %collective-permute-start = (bf16[2,36,512]{2,1,0:T(8,128)(2,1)S(1)}, bf16[2,36,512]{2,1,0:T(8,128)(2,1)S(1)}, u32[]{:S(2)}, u32[]{:S(2)}) collective-permute-start(bf16[2,36,512]{2,1,0:T(8,128)(2,1)S(1)} %pad_maximum_fusion.1), channel_id=1, source_target_pairs={{0,28},{1,29},{2,30},{3,31},{4,0},{5,1},{6,2},{7,3},{8,4},{9,5},{1... | collective-permute-start | bytes 221192 | tf_op jit(solution)/shard_map/ppermute | solution.py:255
  10.1 0.4 collective-permute-start.2
  10.5 4.0 %relative_bias.1 = (f32[2304,128]{1,0:T(8,128)}, f32[2304,128]{1,0:T(8,128)}) custom-call(s32[1]{0:T(128)} %bitcast.2.flag_ref, f32[16,529]{1,0:T(8,128)} %table_ref.1), custom_call_target="tpu_custom_call" | custom-call | flops 283115520 | bytes 2359296 | tf_op jit(solution)/shard_map/relative_bias/pallas_call | solution.py:68
  14.6 0.0 collective-permute-done.1.lat_ref
  14.6 0.0 collective-permute-done.lon_ref
  14.6 0.0 collective-permute-done.2.diag_ref
  14.6 0.0 copy-done.3
  14.6 0.0 copy-done
  14.6 0.0 copy-done.4
  14.7 0.0 copy-start.1
  14.7 1.3 %copy-done.1 = f32[2304,128]{1,0:T(8,128)S(1)} copy-done((f32[2304,128]{1,0:T(8,128)S(1)}, f32[2304,128]{1,0:T(8,128)}, u32[]{:S(2)}) %copy-start.1) | copy-done | bytes 1179672
  15.9 0.0 copy-start.2
  15.9 1.3 %copy-done.2 = f32[2304,128]{1,0:T(8,128)S(1)} copy-done((f32[2304,128]{1,0:T(8,128)S(1)}, f32[2304,128]{1,0:T(8,128)}, u32[]{:S(2)}) %copy-start.2) | copy-done | bytes 1179672
  17.2 4.8 %window_backward.1 = (bf16[36,512]{1,0:T(8,128)(2,1)S(1)}, bf16[36,512]{1,0:T(8,128)(2,1)S(1)}, bf16[36,512]{1,0:T(8,128)(2,1)S(1)}, bf16[36,512]{1,0:T(8,128)(2...) custom-call(s32[1]{0:T(128)} %bitcast.order_ref, bf16[2,36,512]{2,1,0:T(8,128)(2,1)S(1)} %pad_maximum_fusion.own_ref, ...), custom_call_target="tpu_custom_call" | custom-call | flops 754974720 | bytes 6291456 | tf_op jit(solution)/shard_map/window_backward/pallas_call | solution.py:200
  22.0 0.3 collective-permute-start.6
  22.4 2.0 %collective-permute-done.6 = bf16[4,4,48,512]{3,2,1,0:T(8,128)(2,1)S(1)} collective-permute-done((bf16[4,4,48,512]{3,2,1,0:T(8,128)(2,1)S(1)}, bf16[4,4,48,512]{3,2,1,0:T(8,128)(2,1)S(1)}, u32[]{:S(2)}, u32[]{:S(2)}) %collective-permute-start.6) | collective-permute-done | bytes 786464 | tf_op jit(solution)/shard_map/ppermute | solution.py:221
  24.4 0.2 fusion
  24.7 1.2 %collective-permute-start.7 = (bf16[4,48,512]{2,1,0:T(8,128)(2,1)S(1)}, bf16[4,48,512]{2,1,0:T(8,128)(2,1)S(1)}, u32[]{:S(2)}, u32[]{:S(2)}) collective-permute-start(bf16[4,48,512]{2,1,0:T(8,128)(2,1)S(1)} %get-tuple-element.18), channel_id=1, source_target_pairs={{0,2},{1,3},{2,0},{3,1},{4,6},{5,7},{6,4},{7,5},{8,10},{9,11},{10,... | collective-permute-start | bytes 589832 | tf_op jit(solution)/shard_map/ppermute | solution.py:221
  25.9 1.8 %collective-permute-start.9 = (bf16[4,48,512]{2,1,0:T(8,128)(2,1)S(1)}, bf16[4,48,512]{2,1,0:T(8,128)(2,1)S(1)}, u32[]{:S(2)}, u32[]{:S(2)}) collective-permute-start(bf16[4,48,512]{2,1,0:T(8,128)(2,1)S(1)} %get-tuple-element.19), channel_id=1, source_target_pairs={{0,6},{1,7},{2,4},{3,5},{4,2},{5,3},{6,0},{7,1},{8,14},{9,15},{10,... | collective-permute-start | bytes 589832 | tf_op jit(solution)/shard_map/ppermute | solution.py:221
  27.7 0.5 %collective-permute-start.8 = (bf16[4,48,512]{2,1,0:T(8,128)(2,1)S(1)}, bf16[4,48,512]{2,1,0:T(8,128)(2,1)S(1)}, u32[]{:S(2)}, u32[]{:S(2)}) collective-permute-start(bf16[4,48,512]{2,1,0:T(8,128)(2,1)S(1)} %get-tuple-element.20), channel_id=1, source_target_pairs={{0,4},{1,5},{2,6},{3,7},{4,0},{5,1},{6,2},{7,3},{8,12},{9,13},{10,... | collective-permute-start | bytes 589832 | tf_op jit(solution)/shard_map/ppermute | solution.py:221
  28.2 0.5 %collective-permute-start.3 = (bf16[36,512]{1,0:T(8,128)(2,1)S(1)}, bf16[36,512]{1,0:T(8,128)(2,1)S(1)}, u32[]{:S(2)}, u32[]{:S(2)}) collective-permute-start(bf16[36,512]{1,0:T(8,128)(2,1)S(1)} %get-tuple-element.12), channel_id=1, source_target_pairs={{0,5},{1,6},{2,7},{3,4},{4,9},{5,10},{6,11},{7,8},{8,13},{9,14},{1... | collective-permute-start | bytes 110600 | tf_op jit(solution)/shard_map/ppermute | solution.py:297
  28.8 1.0 %collective-permute-start.4 = (bf16[36,512]{1,0:T(8,128)(2,1)S(1)}, bf16[36,512]{1,0:T(8,128)(2,1)S(1)}, u32[]{:S(2)}, u32[]{:S(2)}) collective-permute-start(bf16[36,512]{1,0:T(8,128)(2,1)S(1)} %get-tuple-element.13), channel_id=1, source_target_pairs={{0,4},{1,5},{2,6},{3,7},{4,8},{5,9},{6,10},{7,11},{8,12},{9,13},{1... | collective-permute-start | bytes 110600 | tf_op jit(solution)/shard_map/ppermute | solution.py:295
  29.7 7.9 %collective-permute-done.3 = bf16[36,512]{1,0:T(8,128)(2,1)S(1)} collective-permute-done((bf16[36,512]{1,0:T(8,128)(2,1)S(1)}, bf16[36,512]{1,0:T(8,128)(2,1)S(1)}, u32[]{:S(2)}, u32[]{:S(2)}) %collective-permute-start.3) | collective-permute-done | bytes 36896 | tf_op jit(solution)/shard_map/ppermute | solution.py:297
  37.6 0.0 collective-permute-start.5
  37.6 0.4 collective-permute-done.4
  38.0 3.0 %collective-permute-done.5 = bf16[36,512]{1,0:T(8,128)(2,1)S(1)} collective-permute-done((bf16[36,512]{1,0:T(8,128)(2,1)S(1)}, bf16[36,512]{1,0:T(8,128)(2,1)S(1)}, u32[]{:S(2)}, u32[]{:S(2)}) %collective-permute-start.5) | collective-permute-done | bytes 36896 | tf_op jit(solution)/shard_map/ppermute | solution.py:296
  41.0 0.0 collective-permute-done.7
  41.0 0.0 collective-permute-done.9
  41.1 0.0 collective-permute-done.8
  41.1 0.1 fusion.3
  41.2 0.1 collective-permute-start.10
  41.3 3.3 %collective-permute-start.12 = (bf16[48,512]{1,0:T(8,128)(2,1)S(1)}, bf16[48,512]{1,0:T(8,128)(2,1)S(1)}, u32[]{:S(2)}, u32[]{:S(2)}) collective-permute-start(bf16[48,512]{1,0:T(8,128)(2,1)S(1)} %get-tuple-element.22), channel_id=1, source_target_pairs={{0,24},{1,25},{2,26},{3,27},{4,28},{5,29},{6,30},{7,31},{8,16},{9,... | collective-permute-start | bytes 147464 | tf_op jit(solution)/shard_map/ppermute | solution.py:221
  44.6 0.5 collective-permute-start.11
  45.1 0.7 %maximum_maximum_fusion = bf16[12,12,512]{2,1,0:T(8,128)(2,1)} fusion(bf16[6,6,512]{2,1,0:T(8,128)(2,1)S(1)} %reshape.47, bf16[6,6,512]{2,1,0:T(8,128)(2,1)S(1)} %reshape.46, bf16[6,6,512]{2,1,0:T(8,128)(2,1)S(1)} %reshape.45, bf16[6,6,512]{2,1,0:T(8,128)(2,1)S(1)} %reshape.44), kind=kLoop, calls=%fused_computation.10 | loop fusion | flops 589824 | bytes 294912 | tf_op jit(solution)/shard_map/concatenate | solution.py:301
  45.8 0.0 collective-permute-done.10
  45.9 1.8 %collective-permute-done.12 = bf16[48,512]{1,0:T(8,128)(2,1)S(1)} collective-permute-done((bf16[48,512]{1,0:T(8,128)(2,1)S(1)}, bf16[48,512]{1,0:T(8,128)(2,1)S(1)}, u32[]{:S(2)}, u32[]{:S(2)}) %collective-permute-start.12) | collective-permute-done | bytes 49184 | tf_op jit(solution)/shard_map/ppermute | solution.py:221
  47.7 1.9 %collective-permute-done.11 = bf16[48,512]{1,0:T(8,128)(2,1)S(1)} collective-permute-done((bf16[48,512]{1,0:T(8,128)(2,1)S(1)}, bf16[48,512]{1,0:T(8,128)(2,1)S(1)}, u32[]{:S(2)}, u32[]{:S(2)}) %collective-permute-start.11) | collective-permute-done | bytes 49184 | tf_op jit(solution)/shard_map/ppermute | solution.py:221
  49.6 0.7 %copy.8 = f32[6,4,8,128]{3,1,2,0:T(4,128)} copy(f32[6,4,8,128]{3,2,1,0:T(8,128)S(1)} %fusion.7) | data formatting | bytes 196608
  (19 shorter events, 0.4 us)
Async XLA Ops:
  0.6 14.0 %copy-start.3 = (bf16[512,512]{1,0:T(8,128)(2,1)S(1)}, bf16[512,512]{1,0:T(8,128)(2,1)}, u32[]{:S(2)}) copy-start(bf16[512,512]{1,0:T(8,128)(2,1)} %proj_ref.1) | copy-start | bytes 1572868
  0.6 14.0 %copy-start = (bf16[512,1536]{1,0:T(8,128)(2,1)S(1)}, bf16[512,1536]{1,0:T(8,128)(2,1)}, u32[]{:S(2)}) copy-start(bf16[512,1536]{1,0:T(8,128)(2,1)} %weight_ref.1) | copy-start | bytes 4718596
  0.7 14.0 %copy-start.4 = (f32[512]{0:T(512)S(1)}, f32[512]{0:T(512)}, u32[]{:S(2)}) copy-start(f32[512]{0:T(512)} %param.7) | copy-start | bytes 6148
  2.9 11.7 %collective-permute-start.1 = (bf16[2,36,512]{2,1,0:T(8,128)(2,1)S(1)}, bf16[2,36,512]{2,1,0:T(8,128)(2,1)S(1)}, u32[]{:S(2)}, u32[]{:S(2)}) collective-permute-start(bf16[2,36,512]{2,1,0:T(8,128)(2,1)S(1)} %pad_maximum_fusion.2), channel_id=1, source_target_pairs={{0,3},{1,0},{2,1},{3,2},{4,7},{5,4},{6,5},{7,6},{8,11},{9,8},{10,9... | collective-permute-start | bytes 221192 | tf_op jit(solution)/shard_map/ppermute | solution.py:256
  5.4 9.2 %collective-permute-start = (bf16[2,36,512]{2,1,0:T(8,128)(2,1)S(1)}, bf16[2,36,512]{2,1,0:T(8,128)(2,1)S(1)}, u32[]{:S(2)}, u32[]{:S(2)}) collective-permute-start(bf16[2,36,512]{2,1,0:T(8,128)(2,1)S(1)} %pad_maximum_fusion.1), channel_id=1, source_target_pairs={{0,28},{1,29},{2,30},{3,31},{4,0},{5,1},{6,2},{7,3},{8,4},{9,5},{1... | collective-permute-start | bytes 221192 | tf_op jit(solution)/shard_map/ppermute | solution.py:255
  10.1 4.5 %collective-permute-start.2 = (bf16[2,36,512]{2,1,0:T(8,128)(2,1)S(1)}, bf16[2,36,512]{2,1,0:T(8,128)(2,1)S(1)}, u32[]{:S(2)}, u32[]{:S(2)}) collective-permute-start(bf16[2,36,512]{2,1,0:T(8,128)(2,1)S(1)} %pad_maximum_fusion.3), channel_id=1, source_target_pairs={{0,31},{1,28},{2,29},{3,30},{4,3},{5,0},{6,1},{7,2},{8,7},{9,4},{1... | collective-permute-start | bytes 221192 | tf_op jit(solution)/shard_map/ppermute | solution.py:257
  14.7 1.3 %copy-start.1 = (f32[2304,128]{1,0:T(8,128)S(1)}, f32[2304,128]{1,0:T(8,128)}, u32[]{:S(2)}) copy-start(f32[2304,128]{1,0:T(8,128)} %get-tuple-element.10.low_ref) | copy-start | bytes 3538948
  15.9 1.3 %copy-start.2 = (f32[2304,128]{1,0:T(8,128)S(1)}, f32[2304,128]{1,0:T(8,128)}, u32[]{:S(2)}) copy-start(f32[2304,128]{1,0:T(8,128)} %get-tuple-element.11.high_ref) | copy-start | bytes 3538948
  22.0 2.4 %collective-permute-start.6 = (bf16[4,4,48,512]{3,2,1,0:T(8,128)(2,1)S(1)}, bf16[4,4,48,512]{3,2,1,0:T(8,128)(2,1)S(1)}, u32[]{:S(2)}, u32[]{:S(2)}) collective-permute-start(bf16[4,4,48,512]{3,2,1,0:T(8,128)(2,1)S(1)} %bitcast.33), channel_id=1, source_target_pairs={{0,1},{1,0},{2,3},{3,2},{4,5},{5,4},{6,7},{7,6},{8,9},{9,8},{10,11... | collective-permute-start | bytes 2359304 | tf_op jit(solution)/shard_map/ppermute | solution.py:221
  24.7 16.4 %collective-permute-start.7 = (bf16[4,48,512]{2,1,0:T(8,128)(2,1)S(1)}, bf16[4,48,512]{2,1,0:T(8,128)(2,1)S(1)}, u32[]{:S(2)}, u32[]{:S(2)}) collective-permute-start(bf16[4,48,512]{2,1,0:T(8,128)(2,1)S(1)} %get-tuple-element.18), channel_id=1, source_target_pairs={{0,2},{1,3},{2,0},{3,1},{4,6},{5,7},{6,4},{7,5},{8,10},{9,11},{10,... | collective-permute-start | bytes 589832 | tf_op jit(solution)/shard_map/ppermute | solution.py:221
  25.9 15.2 %collective-permute-start.9 = (bf16[4,48,512]{2,1,0:T(8,128)(2,1)S(1)}, bf16[4,48,512]{2,1,0:T(8,128)(2,1)S(1)}, u32[]{:S(2)}, u32[]{:S(2)}) collective-permute-start(bf16[4,48,512]{2,1,0:T(8,128)(2,1)S(1)} %get-tuple-element.19), channel_id=1, source_target_pairs={{0,6},{1,7},{2,4},{3,5},{4,2},{5,3},{6,0},{7,1},{8,14},{9,15},{10,... | collective-permute-start | bytes 589832 | tf_op jit(solution)/shard_map/ppermute | solution.py:221
  27.7 13.4 %collective-permute-start.8 = (bf16[4,48,512]{2,1,0:T(8,128)(2,1)S(1)}, bf16[4,48,512]{2,1,0:T(8,128)(2,1)S(1)}, u32[]{:S(2)}, u32[]{:S(2)}) collective-permute-start(bf16[4,48,512]{2,1,0:T(8,128)(2,1)S(1)} %get-tuple-element.20), channel_id=1, source_target_pairs={{0,4},{1,5},{2,6},{3,7},{4,0},{5,1},{6,2},{7,3},{8,12},{9,13},{10,... | collective-permute-start | bytes 589832 | tf_op jit(solution)/shard_map/ppermute | solution.py:221
  28.2 9.4 %collective-permute-start.3 = (bf16[36,512]{1,0:T(8,128)(2,1)S(1)}, bf16[36,512]{1,0:T(8,128)(2,1)S(1)}, u32[]{:S(2)}, u32[]{:S(2)}) collective-permute-start(bf16[36,512]{1,0:T(8,128)(2,1)S(1)} %get-tuple-element.12), channel_id=1, source_target_pairs={{0,5},{1,6},{2,7},{3,4},{4,9},{5,10},{6,11},{7,8},{8,13},{9,14},{1... | collective-permute-start | bytes 110600 | tf_op jit(solution)/shard_map/ppermute | solution.py:297
  28.8 9.3 %collective-permute-start.4 = (bf16[36,512]{1,0:T(8,128)(2,1)S(1)}, bf16[36,512]{1,0:T(8,128)(2,1)S(1)}, u32[]{:S(2)}, u32[]{:S(2)}) collective-permute-start(bf16[36,512]{1,0:T(8,128)(2,1)S(1)} %get-tuple-element.13), channel_id=1, source_target_pairs={{0,4},{1,5},{2,6},{3,7},{4,8},{5,9},{6,10},{7,11},{8,12},{9,13},{1... | collective-permute-start | bytes 110600 | tf_op jit(solution)/shard_map/ppermute | solution.py:295
  37.6 3.4 %collective-permute-start.5 = (bf16[36,512]{1,0:T(8,128)(2,1)S(1)}, bf16[36,512]{1,0:T(8,128)(2,1)S(1)}, u32[]{:S(2)}, u32[]{:S(2)}) collective-permute-start(bf16[36,512]{1,0:T(8,128)(2,1)S(1)} %get-tuple-element.14), channel_id=1, source_target_pairs={{0,1},{1,2},{2,3},{3,0},{4,5},{5,6},{6,7},{7,4},{8,9},{9,10},{10,1... | collective-permute-start | bytes 110600 | tf_op jit(solution)/shard_map/ppermute | solution.py:296
  41.2 4.7 %collective-permute-start.10 = (bf16[48,512]{1,0:T(8,128)(2,1)S(1)}, bf16[48,512]{1,0:T(8,128)(2,1)S(1)}, u32[]{:S(2)}, u32[]{:S(2)}) collective-permute-start(bf16[48,512]{1,0:T(8,128)(2,1)S(1)} %get-tuple-element.21), channel_id=1, source_target_pairs={{0,8},{1,9},{2,10},{3,11},{4,12},{5,13},{6,14},{7,15},{8,0},{9,1},... | collective-permute-start | bytes 147464 | tf_op jit(solution)/shard_map/ppermute | solution.py:221
  41.3 6.4 %collective-permute-start.12 = (bf16[48,512]{1,0:T(8,128)(2,1)S(1)}, bf16[48,512]{1,0:T(8,128)(2,1)S(1)}, u32[]{:S(2)}, u32[]{:S(2)}) collective-permute-start(bf16[48,512]{1,0:T(8,128)(2,1)S(1)} %get-tuple-element.22), channel_id=1, source_target_pairs={{0,24},{1,25},{2,26},{3,27},{4,28},{5,29},{6,30},{7,31},{8,16},{9,... | collective-permute-start | bytes 147464 | tf_op jit(solution)/shard_map/ppermute | solution.py:221
  44.6 5.0 %collective-permute-start.11 = (bf16[48,512]{1,0:T(8,128)(2,1)S(1)}, bf16[48,512]{1,0:T(8,128)(2,1)S(1)}, u32[]{:S(2)}, u32[]{:S(2)}) collective-permute-start(bf16[48,512]{1,0:T(8,128)(2,1)S(1)} %get-tuple-element.23), channel_id=1, source_target_pairs={{0,16},{1,17},{2,18},{3,19},{4,20},{5,21},{6,22},{7,23},{8,24},{9,... | collective-permute-start | bytes 147464 | tf_op jit(solution)/shard_map/ppermute | solution.py:221

commit v2 on v1

--- a/solution.py
+++ b/solution.py
@@ -23,7 +23,59 @@
     return lax.dot_general(a, b, (((ca,), (cb,)), ((), ())), preferred_element_type=F32)
 
 
-def bias_kernel(flag_ref, table_ref, low_ref, high_ref, pad_ref):
+def pack_kernel(
+    tokens_hbm, grad_hbm, table_hbm, own_ref, lon_ref, lat_ref, diag_ref, table_ref, here_ref, stage_ref, sems
+):
+    copies = [
+        pltpu.make_async_copy(tokens_hbm, here_ref.at[0], sems.at[0]),
+        pltpu.make_async_copy(grad_hbm, here_ref.at[1], sems.at[1]),
+        pltpu.make_async_copy(table_hbm, table_ref, sems.at[2]),
+    ]
+    for copy in copies:
+        copy.start()
+    for k in range(2):
+        copies[k].wait()
+        for u in range(WIN):
+            line = here_ref[k, u].astype(F32)
+            row = u % EDGE * EDGE
+            early = u < EDGE
+            stage_ref[k, 2 if early else 3, row : row + EDGE, :] = line[:EDGE]
+            stage_ref[k, 0 if early else 1, row : row + EDGE, :] = line[EDGE:]
+        for n, out in enumerate((own_ref, lon_ref, lat_ref, diag_ref)):
+            out[k] = stage_ref[k, n].astype(BF16)
+    copies[2].wait()
+
+
+def pack(tokens, grad, table):
+    width = tokens.shape[2]
+    shape = jax.ShapeDtypeStruct((2, QUARTER, width), BF16)
+    hbm = pl.BlockSpec(memory_space=pltpu.HBM)
+    vmem = pl.BlockSpec(memory_space=pltpu.VMEM)
+    return pl.pallas_call(
+        pack_kernel,
+        out_shape=(shape,) * 4 + (jax.ShapeDtypeStruct(table.shape, F32),),
+        in_specs=[hbm] * 3,
+        out_specs=(vmem,) * 5,
+        scratch_shapes=[
+            pltpu.VMEM((2,) + tokens.shape, BF16),
+            pltpu.VMEM((2, 4, QUARTER, width), F32),
+            pltpu.SemaphoreType.DMA((3,)),
+        ],
+        compiler_params=pltpu.CompilerParams(vmem_limit_bytes=8 << 20),
+        cost_estimate=pl.CostEstimate(flops=0, bytes_accessed=1 << 20, transcendentals=0),
+        name="pack",
+    )(*(pltpu.with_memory_space_constraint(x, pltpu.HBM) for x in (tokens, grad, table)))
+
+
+def bias_kernel(
+    flag_ref, table_ref, weight_hbm, proj_hbm, low_ref, high_ref, weight_ref, proj_ref, pad_ref, sems
+):
+    copies = [
+        pltpu.make_async_copy(weight_hbm, weight_ref, sems.at[0]),
+        pltpu.make_async_copy(proj_hbm, proj_ref, sems.at[1]),
+    ]
+    for copy in copies:
+        copy.start()
     heads, count = table_ref.shape
     width = pad_ref.shape[1]
     pad_ref[...] = jnp.zeros_like(pad_ref)
@@ -59,26 +111,33 @@
                 lane < half, left[:, :LANES], right[:, :LANES]
             )
             high_ref[start : start + heads, :] = right[:, LANES:]
-
-
-def relative_bias(flag, table):
+    for copy in copies:
+        copy.wait()
+
+
+def relative_bias(flag, table, weight, proj):
     heads = table.shape[0]
     shape = jax.ShapeDtypeStruct((AREA * heads, LANES), F32)
     width = -(-table.shape[1] // LANES) * LANES
+    hbm = pl.BlockSpec(memory_space=pltpu.HBM)
+    vmem = pl.BlockSpec(memory_space=pltpu.VMEM)
     return pl.pallas_call(
         bias_kernel,
-        out_shape=(shape, shape),
-        in_specs=[
-            pl.BlockSpec(memory_space=pltpu.SMEM),
-            pl.BlockSpec(memory_space=pltpu.VMEM),
-        ],
-        out_specs=(pl.BlockSpec(memory_space=pltpu.VMEM),) * 2,
-        scratch_shapes=[pltpu.VMEM((heads, width), F32)],
+        out_shape=(
+            shape,
+            shape,
+            jax.ShapeDtypeStruct(weight.shape, BF16),
+            jax.ShapeDtypeStruct(proj.shape, BF16),
+        ),
+        in_specs=[pl.BlockSpec(memory_space=pltpu.SMEM), vmem, hbm, hbm],
+        out_specs=(vmem,) * 4,
+        scratch_shapes=[pltpu.VMEM((heads, width), F32), pltpu.SemaphoreType.DMA((2,))],
+        compiler_params=pltpu.CompilerParams(vmem_limit_bytes=16 << 20),
         cost_estimate=pl.CostEstimate(
-            flops=2 * 3 * 18 * heads * width * 256, bytes_accessed=2 * AREA * heads * 512, transcendentals=0
+            flops=6 * 18 * heads * width * 256, bytes_accessed=6 << 20, transcendentals=0
         ),
         name="relative_bias",
-    )(flag, table)
+    )(flag, table, *(pltpu.with_memory_space_constraint(x, pltpu.HBM) for x in (weight, proj)))
 
 
 def window_kernel(
@@ -106,7 +165,7 @@
     size = width // heads
     group = LANES // size
     factor = size ** (-0.5)
-    for k, ref in enumerate((own_ref, lon_ref, lat_ref, diag_ref)):
+    for k, ref in enumerate((lon_ref, own_ref, diag_ref, lat_ref)):
         token_ref[QUARTER * k : QUARTER * (k + 1), :] = ref[0].astype(F32)
         grad_ref[QUARTER * k : QUARTER * (k + 1), :] = ref[1].astype(F32)
     inputs = token_ref[...]
@@ -175,7 +234,7 @@
         - unit * jnp.mean(scaled * unit, axis=-1, keepdims=True)
     )
     token_ref[...] = result
-    for k, ref in enumerate((own_out, lon_out, lat_out, diag_out)):
+    for k, ref in enumerate((lon_out, own_out, diag_out, lat_out)):
         ref[...] = token_ref[QUARTER * k : QUARTER * (k + 1), :].astype(BF16)
     if blocks is None:
         weight_outs[0][...] = dot(turned_ref[...], normed, 1, 0)
@@ -221,9 +280,12 @@
     return lax.ppermute(block, AXES, [(i, i ^ offset) for i in range(total)])
 
 
-def gather_sum(slots, offsets, total):
-    arrived = [exchange(slots[k + 1], offset, total) for k, offset in enumerate(offsets)]
-    summed = slots[0].astype(F32)
+def send_slots(slots, offsets, total):
+    return [exchange(slots[k + 1], offset, total) for k, offset in enumerate(offsets)]
+
+
+def add_slots(own, arrived):
+    summed = own.astype(F32)
     for piece in arrived:
         summed = summed + piece.astype(F32)
     return summed
@@ -242,22 +304,15 @@
             for b in range(lats)
         ]
 
-    def quarter(at_lon, at_lat):
-        return jnp.stack(
-            [
-                x[at_lon : at_lon + EDGE, at_lat : at_lat + EDGE].reshape(QUARTER, width)
-                for x in (tokens, out_grad)
-            ]
-        )
-
+    own, lon_start, lat_start, diag_start, table = pack(tokens, out_grad, bias_table)
     quarters = [
-        quarter(EDGE, EDGE),
-        lax.ppermute(quarter(0, EDGE), AXES, route(-1, 0)),
-        lax.ppermute(quarter(EDGE, 0), AXES, route(0, -1)),
-        lax.ppermute(quarter(0, 0), AXES, route(-1, -1)),
+        own,
+        lax.ppermute(lon_start, AXES, route(1, 0)),
+        lax.ppermute(lat_start, AXES, route(0, -1)),
+        lax.ppermute(diag_start, AXES, route(1, -1)),
     ]
     flag = (lax.axis_index("lat") == lats - 1).astype(jnp.int32).reshape(1)
-    low, high = relative_bias(flag, bias_table)
+    low, high, weight, proj = relative_bias(flag, table, qkv_weight, proj_weight)
     rows = 3 * width // total
     staged = total % 32 == 0 and 3 * width % total == 0 and rows % 16 == 0
     if staged:
@@ -274,30 +329,32 @@
         place.astype(jnp.int32).reshape(1),
         quarters,
         norm_gain.reshape(1, width),
-        qkv_weight,
-        proj_weight,
+        weight,
+        proj,
         low,
         high,
         blocks,
     )
     factor = 1.0 / math.sqrt(span_lon * lons * span_lat * lats)
+    from_lon = lax.ppermute(to_lon, AXES, route(-1, 0))
+    from_diag = lax.ppermute(to_diag, AXES, route(-1, 1))
     if staged:
         keep, send = weight_grads
         shape = (4, far, rows, width)
-        pair = gather_sum([keep.reshape(shape), send.reshape(shape)], [1], total).astype(BF16)
-        plane = gather_sum([pair[k] for k in range(4)], [2, 4, 6], total).astype(BF16)
-        line = gather_sum([plane[k] for k in range(far)], [8 * k for k in range(1, far)], total)
-        summed = line.reshape(-1)
+        pair = add_slots(keep.reshape(shape), [exchange(send.reshape(shape), 1, total)]).astype(BF16)
+        plane = add_slots(pair[0], send_slots(pair, [2, 4, 6], total)).astype(BF16)
+        plane, to_lat = lax.optimization_barrier((plane, to_lat))
+        from_lat = lax.ppermute(to_lat, AXES, route(0, 1))
+        arrived = send_slots(plane, [8 * k for k in range(1, far)], total)
+        summed = add_slots(plane[0], arrived).reshape(-1)
     else:
+        from_lat = lax.ppermute(to_lat, AXES, route(0, 1))
         summed = lax.psum_scatter(
             weight_grads[0].reshape(-1), AXES, scatter_dimension=0, tiled=True
         )
-    from_lon = lax.ppermute(to_lon, AXES, route(1, 0))
-    from_lat = lax.ppermute(to_lat, AXES, route(0, 1))
-    from_diag = lax.ppermute(to_diag, AXES, route(1, 1))
     cell = (EDGE, EDGE, width)
-    upper = jnp.concatenate([from_diag.reshape(cell), from_lon.reshape(cell)], axis=1)
-    lower = jnp.concatenate([from_lat.reshape(cell), own.reshape(cell)], axis=1)
+    upper = jnp.concatenate([from_lat.reshape(cell), own.reshape(cell)], axis=1)
+    lower = jnp.concatenate([from_diag.reshape(cell), from_lon.reshape(cell)], axis=1)
     token_grad = jnp.concatenate([upper, lower], axis=0)
     return (token_grad, summed * factor)
 

time: 50.6 us -> 44.8 us (0.89)
  local copies, waits for them, and re-layouts: 5.64 us -> 0.8 us
  starting transfers between devices: 16.8 us -> 16.2 us
    ppermute x1, waiting for transfers between devices: 2.97 us -> 0.01 us  [shards(): from_lat = lax.ppermute(to_lat, AXES, route(0, 1))]
    unnamed x11 -> x3, local copies, waits for them, and re-layouts: 3.21 us -> 0.67 us
    slice x2 -> x0, local copies, waits for them, and re-layouts: 2.15 us -> none  [quarter(): x[at_lon:at_lon + EDGE, at_lat:at_lat + EDGE].reshape(QUARTER, width)]
    ppermute x5, waiting for transfers between devices: 8.25 us -> 9.75 us  [the longest x1 7.42 us: shards(): from_diag = lax.ppermute(to_diag, AXES, route(-1, 1))]
    ppermute x7, waiting for transfers between devices: 5.78 us -> 6.77 us  [exchange(): return lax.ppermute(block, AXES, [(i, i ^ offset) for i in range(total)])]
    ppermute x5, starting transfers between devices: 8.97 us -> 8 us  [the longest x1 2.99 us: shards(): lax.ppermute(lon_start, AXES, route(1, 0))]
    pallas_call x1 -> x2, Pallas kernels: 4.04 us -> 4.4 us  [the longest x1 3.29 us: relative_bias(): pl.pallas_call(bias_kernel, out_shape=(shape, shape, jax.ShapeDtypeStruct...]
  transfers between devices with their start and end apart: 13 -> 13, of which waited for: 6 -> 6; matrix products, arithmetic and copies ran while one was open for 2% -> 2% of each run, Pallas kernels for 8% -> 7%
where the time goes in v2:
time: 44.8 us; the launch traced here: 44.6 us
  waiting for transfers between devices  16.5 us (37%)
  starting transfers between devices  16.2 us (36%)
  Pallas kernels  9.2 us (21%)
  other arithmetic  1.11 us (2%)
  local copies, waits for them, and re-layouts  0.8 us (2%)
  between operations  0.77 us (2%)
    ppermute x7, starting transfers between devices, exchange(): return lax.ppermute(block, AXES, [(i, i ^ offset) for i in range(total)])  8.14 us
    ppermute x1, waiting for transfers between devices, shards(): from_diag = lax.ppermute(to_diag, AXES, route(-1, 1))  7.42 us
    ppermute x7, waiting for transfers between devices, exchange(): return lax.ppermute(block, AXES, [(i, i ^ offset) for i in range(total)])  6.77 us
    pallas_call x1, Pallas kernels, window_backward(): pl.pallas_call(functools.partial(window_kernel, blocks), out_shape=(piece...  4.81 us
    pallas_call x1, Pallas kernels, relative_bias(): pl.pallas_call(bias_kernel, out_shape=(shape, shape, jax.ShapeDtypeStruct...  3.29 us
    ppermute x1, starting transfers between devices, shards(): lax.ppermute(lon_start, AXES, route(1, 0))  2.99 us
    ppermute x1, starting transfers between devices, shards(): lax.ppermute(diag_start, AXES, route(1, -1))  1.94 us
    ppermute x1, starting transfers between devices, shards(): from_lon = lax.ppermute(to_lon, AXES, route(-1, 0))  1.65 us
  transfers between devices with their start and end apart: 13, of which 6 were waited for; matrix products, arithmetic and copies ran while one was open for 2% of the time, Pallas kernels for 7%

profile of v2, /device:TPU:0, one launch (start us, length us, event | category | flops | bytes accessed | tf_op | source)
XLA Modules:
  0.0 44.6 jit_solution(15871305783420836962)
XLA Ops:
  0.6 0.0 copy-start
  0.6 1.1 %pack.1 = (bf16[2,36,512]{2,1,0:T(8,128)(2,1)S(1)}, bf16[2,36,512]{2,1,0:T(8,128)(2,1)S(1)}, bf16[2,36,512]{2,1,0:T(8,128)(2,1)S(1)}, bf16[2,36,512]{2,1,0:T(8,128)(2,1)S(1)}, f32[16,529]{1,0:T(8,128)S(1)}) custom-call(bf16[12,12,512]{2,1,0:T(8,128)(2,1)} %tokens_hbm.1, bf16[12,12,512]{2,1,0:T(8,128)(2,1)} %grad_hbm.1, f32[16,529]{1,0:T(8,128)} %table_hbm.1), custom_call_target="tpu_custom_call" | custom-call | bytes 1048576 | tf_op jit(solution)/shard_map/pack/pallas_call | solution.py:54
  1.8 3.0 %collective-permute-start = (bf16[2,36,512]{2,1,0:T(8,128)(2,1)S(1)}, bf16[2,36,512]{2,1,0:T(8,128)(2,1)S(1)}, u32[]{:S(2)}, u32[]{:S(2)}) collective-permute-start(bf16[2,36,512]{2,1,0:T(8,128)(2,1)S(1)} %get-tuple-element.20), channel_id=1, source_target_pairs={{0,4},{1,5},{2,6},{3,7},{4,8},{5,9},{6,10},{7,11},{8,12},{9,13},{1... | collective-permute-start | bytes 221192 | tf_op jit(solution)/shard_map/ppermute | solution.py:310
  4.7 0.7 %collective-permute-start.1 = (bf16[2,36,512]{2,1,0:T(8,128)(2,1)S(1)}, bf16[2,36,512]{2,1,0:T(8,128)(2,1)S(1)}, u32[]{:S(2)}, u32[]{:S(2)}) collective-permute-start(bf16[2,36,512]{2,1,0:T(8,128)(2,1)S(1)} %get-tuple-element.21), channel_id=1, source_target_pairs={{0,3},{1,0},{2,1},{3,2},{4,7},{5,4},{6,5},{7,6},{8,11},{9,8},{10,9... | collective-permute-start | bytes 221192 | tf_op jit(solution)/shard_map/ppermute | solution.py:311
  5.4 1.9 %collective-permute-start.2 = (bf16[2,36,512]{2,1,0:T(8,128)(2,1)S(1)}, bf16[2,36,512]{2,1,0:T(8,128)(2,1)S(1)}, u32[]{:S(2)}, u32[]{:S(2)}) collective-permute-start(bf16[2,36,512]{2,1,0:T(8,128)(2,1)S(1)} %get-tuple-element.22), channel_id=1, source_target_pairs={{0,7},{1,4},{2,5},{3,6},{4,11},{5,8},{6,9},{7,10},{8,15},{9,12},{1... | collective-permute-start | bytes 221192 | tf_op jit(solution)/shard_map/ppermute | solution.py:312
  7.4 3.3 %relative_bias.1 = (f32[2304,128]{1,0:T(8,128)S(1)}, f32[2304,128]{1,0:T(8,128)S(1)}, bf16[512,1536]{1,0:T(8,128)(2,1)S(1)}, bf16[512,512]{1,0:T(8,128)(2,1)S(1)}) custom-call(s32[1]{0:T(128)} %bitcast.2.flag_ref, f32[16,529]{1,0:T(8,128)S(1)} %get-tuple-element.23.table_ref, bf16[512,1536]{1,0:T(8,128)(2,1)} %weight_hbm.1, bf16[512,512]{1,0:T(8,128)(2,1)} %proj_hbm.1), custom_call_target="tpu_custom_call" | custom-call | flops 283115520 | bytes 6291456 | tf_op jit(solution)/shard_map/relative_bias/pallas_call | solution.py:124
  10.7 0.0 collective-permute-done.lon_ref
  10.7 0.0 collective-permute-done.1.lat_ref
  10.7 1.3 %collective-permute-done.2.diag_ref = bf16[2,36,512]{2,1,0:T(8,128)(2,1)S(1)} collective-permute-done((bf16[2,36,512]{2,1,0:T(8,128)(2,1)S(1)}, bf16[2,36,512]{2,1,0:T(8,128)(2,1)S(1)}, u32[]{:S(2)}, u32[]{:S(2)}) %collective-permute-start.2) | collective-permute-done | bytes 73760 | tf_op jit(solution)/shard_map/ppermute | solution.py:312
  12.0 0.0 copy-done
  12.0 4.8 %window_backward.1 = (bf16[36,512]{1,0:T(8,128)(2,1)S(1)}, bf16[36,512]{1,0:T(8,128)(2,1)S(1)}, bf16[36,512]{1,0:T(8,128)(2,1)S(1)}, bf16[36,512]{1,0:T(8,128)(2...) custom-call(s32[1]{0:T(128)} %bitcast.order_ref, bf16[2,36,512]{2,1,0:T(8,128)(2,1)S(1)} %get-tuple-element.19.own_ref, ...), custom_call_target="tpu_custom_call" | custom-call | flops 754974720 | bytes 6291456 | tf_op jit(solution)/shard_map/window_backward/pallas_call | solution.py:259
  16.8 1.0 %collective-permute-start.3 = (bf16[4,4,48,512]{3,2,1,0:T(8,128)(2,1)S(1)}, bf16[4,4,48,512]{3,2,1,0:T(8,128)(2,1)S(1)}, u32[]{:S(2)}, u32[]{:S(2)}) collective-permute-start(bf16[4,4,48,512]{3,2,1,0:T(8,128)(2,1)S(1)} %bitcast.31), channel_id=1, source_target_pairs={{0,1},{1,0},{2,3},{3,2},{4,5},{5,4},{6,7},{7,6},{8,9},{9,8},{10,11... | collective-permute-start | bytes 2359304 | tf_op jit(solution)/shard_map/ppermute | solution.py:280
  17.8 1.9 %collective-permute-done.3 = bf16[4,4,48,512]{3,2,1,0:T(8,128)(2,1)S(1)} collective-permute-done((bf16[4,4,48,512]{3,2,1,0:T(8,128)(2,1)S(1)}, bf16[4,4,48,512]{3,2,1,0:T(8,128)(2,1)S(1)}, u32[]{:S(2)}, u32[]{:S(2)}) %collective-permute-start.3) | collective-permute-done | bytes 786464 | tf_op jit(solution)/shard_map/ppermute | solution.py:280
  19.8 0.2 fusion
  20.0 1.4 %collective-permute-start.4 = (bf16[4,48,512]{2,1,0:T(8,128)(2,1)S(1)}, bf16[4,48,512]{2,1,0:T(8,128)(2,1)S(1)}, u32[]{:S(2)}, u32[]{:S(2)}) collective-permute-start(bf16[4,48,512]{2,1,0:T(8,128)(2,1)S(1)} %get-tuple-element.36), channel_id=1, source_target_pairs={{0,2},{1,3},{2,0},{3,1},{4,6},{5,7},{6,4},{7,5},{8,10},{9,11},{10,... | collective-permute-start | bytes 589832 | tf_op jit(solution)/shard_map/ppermute | solution.py:280
  21.4 0.0 collective-permute-start.6
  21.4 2.2 %collective-permute-start.5 = (bf16[4,48,512]{2,1,0:T(8,128)(2,1)S(1)}, bf16[4,48,512]{2,1,0:T(8,128)(2,1)S(1)}, u32[]{:S(2)}, u32[]{:S(2)}) collective-permute-start(bf16[4,48,512]{2,1,0:T(8,128)(2,1)S(1)} %get-tuple-element.38), channel_id=1, source_target_pairs={{0,4},{1,5},{2,6},{3,7},{4,0},{5,1},{6,2},{7,3},{8,12},{9,13},{10,... | collective-permute-start | bytes 589832 | tf_op jit(solution)/shard_map/ppermute | solution.py:280
  23.6 0.7 %collective-permute-start.8 = (bf16[36,512]{1,0:T(8,128)(2,1)S(1)}, bf16[36,512]{1,0:T(8,128)(2,1)S(1)}, u32[]{:S(2)}, u32[]{:S(2)}) collective-permute-start(bf16[36,512]{1,0:T(8,128)(2,1)S(1)} %get-tuple-element.33), channel_id=1, source_target_pairs={{0,29},{1,30},{2,31},{3,28},{4,1},{5,2},{6,3},{7,0},{8,5},{9,6},{1... | collective-permute-start | bytes 110600 | tf_op jit(solution)/shard_map/ppermute | solution.py:340
  24.4 1.6 %collective-permute-start.9 = (bf16[36,512]{1,0:T(8,128)(2,1)S(1)}, bf16[36,512]{1,0:T(8,128)(2,1)S(1)}, u32[]{:S(2)}, u32[]{:S(2)}) collective-permute-start(bf16[36,512]{1,0:T(8,128)(2,1)S(1)} %get-tuple-element.34), channel_id=1, source_target_pairs={{0,28},{1,29},{2,30},{3,31},{4,0},{5,1},{6,2},{7,3},{8,4},{9,5},{1... | collective-permute-start | bytes 110600 | tf_op jit(solution)/shard_map/ppermute | solution.py:339
  26.0 7.4 %collective-permute-done.8 = bf16[36,512]{1,0:T(8,128)(2,1)S(1)} collective-permute-done((bf16[36,512]{1,0:T(8,128)(2,1)S(1)}, bf16[36,512]{1,0:T(8,128)(2,1)S(1)}, u32[]{:S(2)}, u32[]{:S(2)}) %collective-permute-start.8) | collective-permute-done | bytes 36896 | tf_op jit(solution)/shard_map/ppermute | solution.py:340
  33.5 1.0 %collective-permute-done.9 = bf16[36,512]{1,0:T(8,128)(2,1)S(1)} collective-permute-done((bf16[36,512]{1,0:T(8,128)(2,1)S(1)}, bf16[36,512]{1,0:T(8,128)(2,1)S(1)}, u32[]{:S(2)}, u32[]{:S(2)}) %collective-permute-start.9) | collective-permute-done | bytes 36896 | tf_op jit(solution)/shard_map/ppermute | solution.py:339
  34.5 0.0 collective-permute-done.4
  34.5 0.0 collective-permute-done.6
  34.5 0.0 collective-permute-done.5
  34.5 0.1 fusion.3
  34.6 0.1 collective-permute-start.7
  34.7 0.1 collective-permute-start.10
  34.8 2.2 %collective-permute-start.12 = (bf16[48,512]{1,0:T(8,128)(2,1)S(1)}, bf16[48,512]{1,0:T(8,128)(2,1)S(1)}, u32[]{:S(2)}, u32[]{:S(2)}) collective-permute-start(bf16[48,512]{1,0:T(8,128)(2,1)S(1)} %get-tuple-element.40), channel_id=1, source_target_pairs={{0,24},{1,25},{2,26},{3,27},{4,28},{5,29},{6,30},{7,31},{8,16},{9,... | collective-permute-start | bytes 147464 | tf_op jit(solution)/shard_map/ppermute | solution.py:280
  37.1 1.2 %collective-permute-start.11 = (bf16[48,512]{1,0:T(8,128)(2,1)S(1)}, bf16[48,512]{1,0:T(8,128)(2,1)S(1)}, u32[]{:S(2)}, u32[]{:S(2)}) collective-permute-start(bf16[48,512]{1,0:T(8,128)(2,1)S(1)} %get-tuple-element.41), channel_id=1, source_target_pairs={{0,16},{1,17},{2,18},{3,19},{4,20},{5,21},{6,22},{7,23},{8,24},{9,... | collective-permute-start | bytes 147464 | tf_op jit(solution)/shard_map/ppermute | solution.py:280
  38.3 0.0 collective-permute-done.7
  38.3 0.7 %maximum_maximum_fusion = bf16[12,12,512]{2,1,0:T(8,128)(2,1)} fusion(bf16[6,6,512]{2,1,0:T(8,128)(2,1)S(1)} %reshape.48, bf16[6,6,512]{2,1,0:T(8,128)(2,1)S(1)} %reshape.47, bf16[6,6,512]{2,1,0:T(8,128)(2,1)S(1)} %reshape.46, bf16[6,6,512]{2,1,0:T(8,128)(2,1)S(1)} %reshape.45), kind=kLoop, calls=%fused_computation.10 | loop fusion | flops 589824 | bytes 294912 | tf_op jit(solution)/shard_map/concatenate | solution.py:358
  39.1 0.0 collective-permute-done.10
  39.1 2.0 %collective-permute-done.12 = bf16[48,512]{1,0:T(8,128)(2,1)S(1)} collective-permute-done((bf16[48,512]{1,0:T(8,128)(2,1)S(1)}, bf16[48,512]{1,0:T(8,128)(2,1)S(1)}, u32[]{:S(2)}, u32[]{:S(2)}) %collective-permute-start.12) | collective-permute-done | bytes 49184 | tf_op jit(solution)/shard_map/ppermute | solution.py:280
  41.1 2.8 %collective-permute-done.11 = bf16[48,512]{1,0:T(8,128)(2,1)S(1)} collective-permute-done((bf16[48,512]{1,0:T(8,128)(2,1)S(1)}, bf16[48,512]{1,0:T(8,128)(2,1)S(1)}, u32[]{:S(2)}, u32[]{:S(2)}) %collective-permute-start.11) | collective-permute-done | bytes 49184 | tf_op jit(solution)/shard_map/ppermute | solution.py:280
  43.9 0.7 %copy.8 = f32[6,4,8,128]{3,1,2,0:T(4,128)} copy(f32[6,4,8,128]{3,2,1,0:T(8,128)S(1)} %fusion.7) | data formatting | bytes 196608
  (7 shorter events, 0.2 us)
Async XLA Ops:
  0.6 11.4 %copy-start = (f32[512]{0:T(512)S(1)}, f32[512]{0:T(512)}, u32[]{:S(2)}) copy-start(f32[512]{0:T(512)} %param.7) | copy-start | bytes 6148
  1.8 8.9 %collective-permute-start = (bf16[2,36,512]{2,1,0:T(8,128)(2,1)S(1)}, bf16[2,36,512]{2,1,0:T(8,128)(2,1)S(1)}, u32[]{:S(2)}, u32[]{:S(2)}) collective-permute-start(bf16[2,36,512]{2,1,0:T(8,128)(2,1)S(1)} %get-tuple-element.20), channel_id=1, source_target_pairs={{0,4},{1,5},{2,6},{3,7},{4,8},{5,9},{6,10},{7,11},{8,12},{9,13},{1... | collective-permute-start | bytes 221192 | tf_op jit(solution)/shard_map/ppermute | solution.py:310
  4.7 5.9 %collective-permute-start.1 = (bf16[2,36,512]{2,1,0:T(8,128)(2,1)S(1)}, bf16[2,36,512]{2,1,0:T(8,128)(2,1)S(1)}, u32[]{:S(2)}, u32[]{:S(2)}) collective-permute-start(bf16[2,36,512]{2,1,0:T(8,128)(2,1)S(1)} %get-tuple-element.21), channel_id=1, source_target_pairs={{0,3},{1,0},{2,1},{3,2},{4,7},{5,4},{6,5},{7,6},{8,11},{9,8},{10,9... | collective-permute-start | bytes 221192 | tf_op jit(solution)/shard_map/ppermute | solution.py:311
  5.4 6.6 %collective-permute-start.2 = (bf16[2,36,512]{2,1,0:T(8,128)(2,1)S(1)}, bf16[2,36,512]{2,1,0:T(8,128)(2,1)S(1)}, u32[]{:S(2)}, u32[]{:S(2)}) collective-permute-start(bf16[2,36,512]{2,1,0:T(8,128)(2,1)S(1)} %get-tuple-element.22), channel_id=1, source_target_pairs={{0,7},{1,4},{2,5},{3,6},{4,11},{5,8},{6,9},{7,10},{8,15},{9,12},{1... | collective-permute-start | bytes 221192 | tf_op jit(solution)/shard_map/ppermute | solution.py:312
  16.8 2.9 %collective-permute-start.3 = (bf16[4,4,48,512]{3,2,1,0:T(8,128)(2,1)S(1)}, bf16[4,4,48,512]{3,2,1,0:T(8,128)(2,1)S(1)}, u32[]{:S(2)}, u32[]{:S(2)}) collective-permute-start(bf16[4,4,48,512]{3,2,1,0:T(8,128)(2,1)S(1)} %bitcast.31), channel_id=1, source_target_pairs={{0,1},{1,0},{2,3},{3,2},{4,5},{5,4},{6,7},{7,6},{8,9},{9,8},{10,11... | collective-permute-start | bytes 2359304 | tf_op jit(solution)/shard_map/ppermute | solution.py:280
  20.0 14.5 %collective-permute-start.4 = (bf16[4,48,512]{2,1,0:T(8,128)(2,1)S(1)}, bf16[4,48,512]{2,1,0:T(8,128)(2,1)S(1)}, u32[]{:S(2)}, u32[]{:S(2)}) collective-permute-start(bf16[4,48,512]{2,1,0:T(8,128)(2,1)S(1)} %get-tuple-element.36), channel_id=1, source_target_pairs={{0,2},{1,3},{2,0},{3,1},{4,6},{5,7},{6,4},{7,5},{8,10},{9,11},{10,... | collective-permute-start | bytes 589832 | tf_op jit(solution)/shard_map/ppermute | solution.py:280
  21.4 13.1 %collective-permute-start.6 = (bf16[4,48,512]{2,1,0:T(8,128)(2,1)S(1)}, bf16[4,48,512]{2,1,0:T(8,128)(2,1)S(1)}, u32[]{:S(2)}, u32[]{:S(2)}) collective-permute-start(bf16[4,48,512]{2,1,0:T(8,128)(2,1)S(1)} %get-tuple-element.37), channel_id=1, source_target_pairs={{0,6},{1,7},{2,4},{3,5},{4,2},{5,3},{6,0},{7,1},{8,14},{9,15},{10,... | collective-permute-start | bytes 589832 | tf_op jit(solution)/shard_map/ppermute | solution.py:280
  21.4 13.1 %collective-permute-start.5 = (bf16[4,48,512]{2,1,0:T(8,128)(2,1)S(1)}, bf16[4,48,512]{2,1,0:T(8,128)(2,1)S(1)}, u32[]{:S(2)}, u32[]{:S(2)}) collective-permute-start(bf16[4,48,512]{2,1,0:T(8,128)(2,1)S(1)} %get-tuple-element.38), channel_id=1, source_target_pairs={{0,4},{1,5},{2,6},{3,7},{4,0},{5,1},{6,2},{7,3},{8,12},{9,13},{10,... | collective-permute-start | bytes 589832 | tf_op jit(solution)/shard_map/ppermute | solution.py:280
  23.6 9.8 %collective-permute-start.8 = (bf16[36,512]{1,0:T(8,128)(2,1)S(1)}, bf16[36,512]{1,0:T(8,128)(2,1)S(1)}, u32[]{:S(2)}, u32[]{:S(2)}) collective-permute-start(bf16[36,512]{1,0:T(8,128)(2,1)S(1)} %get-tuple-element.33), channel_id=1, source_target_pairs={{0,29},{1,30},{2,31},{3,28},{4,1},{5,2},{6,3},{7,0},{8,5},{9,6},{1... | collective-permute-start | bytes 110600 | tf_op jit(solution)/shard_map/ppermute | solution.py:340
  24.4 10.1 %collective-permute-start.9 = (bf16[36,512]{1,0:T(8,128)(2,1)S(1)}, bf16[36,512]{1,0:T(8,128)(2,1)S(1)}, u32[]{:S(2)}, u32[]{:S(2)}) collective-permute-start(bf16[36,512]{1,0:T(8,128)(2,1)S(1)} %get-tuple-element.34), channel_id=1, source_target_pairs={{0,28},{1,29},{2,30},{3,31},{4,0},{5,1},{6,2},{7,3},{8,4},{9,5},{1... | collective-permute-start | bytes 110600 | tf_op jit(solution)/shard_map/ppermute | solution.py:339
  34.6 3.6 %collective-permute-start.7 = (bf16[36,512]{1,0:T(8,128)(2,1)S(1)}, bf16[36,512]{1,0:T(8,128)(2,1)S(1)}, u32[]{:S(2)}, u32[]{:S(2)}) collective-permute-start(bf16[36,512]{1,0:T(8,128)(2,1)S(1)} %get-tuple-element.31), channel_id=1, source_target_pairs={{0,1},{1,2},{2,3},{3,0},{4,5},{5,6},{6,7},{7,4},{8,9},{9,10},{10,1... | collective-permute-start | bytes 110600 | tf_op jit(solution)/shard_map/ppermute | solution.py:347
  34.7 4.4 %collective-permute-start.10 = (bf16[48,512]{1,0:T(8,128)(2,1)S(1)}, bf16[48,512]{1,0:T(8,128)(2,1)S(1)}, u32[]{:S(2)}, u32[]{:S(2)}) collective-permute-start(bf16[48,512]{1,0:T(8,128)(2,1)S(1)} %get-tuple-element.39), channel_id=1, source_target_pairs={{0,8},{1,9},{2,10},{3,11},{4,12},{5,13},{6,14},{7,15},{8,0},{9,1},... | collective-permute-start | bytes 147464 | tf_op jit(solution)/shard_map/ppermute | solution.py:280
  34.8 6.3 %collective-permute-start.12 = (bf16[48,512]{1,0:T(8,128)(2,1)S(1)}, bf16[48,512]{1,0:T(8,128)(2,1)S(1)}, u32[]{:S(2)}, u32[]{:S(2)}) collective-permute-start(bf16[48,512]{1,0:T(8,128)(2,1)S(1)} %get-tuple-element.40), channel_id=1, source_target_pairs={{0,24},{1,25},{2,26},{3,27},{4,28},{5,29},{6,30},{7,31},{8,16},{9,... | collective-permute-start | bytes 147464 | tf_op jit(solution)/shard_map/ppermute | solution.py:280
  37.1 6.9 %collective-permute-start.11 = (bf16[48,512]{1,0:T(8,128)(2,1)S(1)}, bf16[48,512]{1,0:T(8,128)(2,1)S(1)}, u32[]{:S(2)}, u32[]{:S(2)}) collective-permute-start(bf16[48,512]{1,0:T(8,128)(2,1)S(1)} %get-tuple-element.41), channel_id=1, source_target_pairs={{0,16},{1,17},{2,18},{3,19},{4,20},{5,21},{6,22},{7,23},{8,24},{9,... | collective-permute-start | bytes 147464 | tf_op jit(solution)/shard_map/ppermute | solution.py:280

commit v3 on v2

--- a/solution.py
+++ b/solution.py
@@ -17,6 +17,11 @@
 F32 = jnp.float32
 BF16 = jnp.bfloat16
 AXES = ("lon", "lat")
+PLANE = (0, 2, 1, 3)
+
+
+def line_order(far):
+    return [0] + sorted(range(1, far), key=lambda k: (k != far // 2, k))
 
 
 def dot(a, b, ca, cb):
@@ -39,16 +44,17 @@
             line = here_ref[k, u].astype(F32)
             row = u % EDGE * EDGE
             early = u < EDGE
-            stage_ref[k, 2 if early else 3, row : row + EDGE, :] = line[:EDGE]
-            stage_ref[k, 0 if early else 1, row : row + EDGE, :] = line[EDGE:]
-        for n, out in enumerate((own_ref, lon_ref, lat_ref, diag_ref)):
-            out[k] = stage_ref[k, n].astype(BF16)
+            row += k * QUARTER
+            stage_ref[2 if early else 3, row : row + EDGE, :] = line[:EDGE]
+            stage_ref[0 if early else 1, row : row + EDGE, :] = line[EDGE:]
+    for n, out in enumerate((own_ref, lon_ref, lat_ref, diag_ref)):
+        out[...] = stage_ref[n].astype(BF16)
     copies[2].wait()
 
 
 def pack(tokens, grad, table):
     width = tokens.shape[2]
-    shape = jax.ShapeDtypeStruct((2, QUARTER, width), BF16)
+    shape = jax.ShapeDtypeStruct((2 * QUARTER, width), BF16)
     hbm = pl.BlockSpec(memory_space=pltpu.HBM)
     vmem = pl.BlockSpec(memory_space=pltpu.VMEM)
     return pl.pallas_call(
@@ -58,7 +64,7 @@
         out_specs=(vmem,) * 5,
         scratch_shapes=[
             pltpu.VMEM((2,) + tokens.shape, BF16),
-            pltpu.VMEM((2, 4, QUARTER, width), F32),
+            pltpu.VMEM((4, 2 * QUARTER, width), F32),
             pltpu.SemaphoreType.DMA((3,)),
         ],
         compiler_params=pltpu.CompilerParams(vmem_limit_bytes=8 << 20),
@@ -70,10 +76,14 @@
 def bias_kernel(
     flag_ref, table_ref, weight_hbm, proj_hbm, low_ref, high_ref, weight_ref, proj_ref, pad_ref, sems
 ):
-    copies = [
-        pltpu.make_async_copy(weight_hbm, weight_ref, sems.at[0]),
-        pltpu.make_async_copy(proj_hbm, proj_ref, sems.at[1]),
-    ]
+    copies = []
+    for source, target, chunks in ((weight_hbm, weight_ref, 6), (proj_hbm, proj_ref, 2)):
+        step = source.shape[1] // chunks
+        for k in range(chunks):
+            part = pl.ds(k * step, step)
+            copies.append(
+                pltpu.make_async_copy(source.at[:, part], target.at[:, part], sems.at[len(copies)])
+            )
     for copy in copies:
         copy.start()
     heads, count = table_ref.shape
@@ -131,7 +141,7 @@
         ),
         in_specs=[pl.BlockSpec(memory_space=pltpu.SMEM), vmem, hbm, hbm],
         out_specs=(vmem,) * 4,
-        scratch_shapes=[pltpu.VMEM((heads, width), F32), pltpu.SemaphoreType.DMA((2,))],
+        scratch_shapes=[pltpu.VMEM((heads, width), F32), pltpu.SemaphoreType.DMA((8,))],
         compiler_params=pltpu.CompilerParams(vmem_limit_bytes=16 << 20),
         cost_estimate=pl.CostEstimate(
             flops=6 * 18 * heads * width * 256, bytes_accessed=6 << 20, transcendentals=0
@@ -145,8 +155,8 @@
     order_ref,
     own_ref,
     lon_ref,
+    diag_ref,
     lat_ref,
-    diag_ref,
     gain_ref,
     weight_ref,
     proj_ref,
@@ -166,8 +176,9 @@
     group = LANES // size
     factor = size ** (-0.5)
     for k, ref in enumerate((lon_ref, own_ref, diag_ref, lat_ref)):
-        token_ref[QUARTER * k : QUARTER * (k + 1), :] = ref[0].astype(F32)
-        grad_ref[QUARTER * k : QUARTER * (k + 1), :] = ref[1].astype(F32)
+        both = ref[...].astype(F32)
+        token_ref[QUARTER * k : QUARTER * (k + 1), :] = both[:QUARTER]
+        grad_ref[QUARTER * k : QUARTER * (k + 1), :] = both[QUARTER:]
     inputs = token_ref[...]
     gain = gain_ref[...]
     centred = inputs - jnp.mean(inputs, axis=-1, keepdims=True)
@@ -192,7 +203,7 @@
         all_grads = dot(
             jnp.concatenate([jnp.where(m, values, zero) for m in here], axis=0), up, 1, 1
         )
-        grad_values = None
+        low_probs, low_scores = [], []
         for n in range(group):
             h = g * group + n
             rows = slice(AREA * n, AREA * (n + 1))
@@ -210,15 +221,17 @@
             grad_probs = all_grads[rows]
             centre = jnp.sum(probs * grad_probs, axis=0, keepdims=True)
             grad_scores = (probs * (grad_probs - centre) * factor).astype(BF16)
-            part_values = dot(probs.astype(BF16), jnp.where(here[n], up, zero), 1, 0)
-            part_keys = dot(grad_scores, jnp.where(here[n], query, zero), 1, 0)
+            low_probs.append(probs.astype(BF16))
+            low_scores.append(grad_scores)
             part_query = dot(keys_turned[size * n : size * (n + 1)], grad_scores, 1, 0)
             turned_ref[h * size : (h + 1) * size, :] = part_query.astype(BF16)
-            if grad_values is None:
-                grad_values, grad_keys = part_values, part_keys
-            else:
-                grad_values = grad_values + part_values
-                grad_keys = grad_keys + part_keys
+        all_values = dot(jnp.concatenate(low_probs, axis=0), up, 1, 0)
+        all_keys = dot(jnp.concatenate(low_scores, axis=0), query, 1, 0)
+        grad_values, grad_keys = all_values[:AREA], all_keys[:AREA]
+        for n in range(1, group):
+            rows = slice(AREA * n, AREA * (n + 1))
+            grad_values = jnp.where(here[n], all_values[rows], grad_values)
+            grad_keys = jnp.where(here[n], all_keys[rows], grad_keys)
         grad_values = grad_values.astype(BF16)
         grad_keys = grad_keys.astype(BF16)
         qkv_ref[:, LANES * g : LANES * (g + 1)] = turned_ref[cols, :].T
@@ -240,8 +253,11 @@
         weight_outs[0][...] = dot(turned_ref[...], normed, 1, 0)
     else:
         rows = 3 * width // len(blocks)
-        for slot, offset in enumerate(blocks):
-            start = pl.multiple_of((order_ref[0] ^ offset) * rows, rows)
+        place = order_ref[0]
+        odd = place % 2 == 1
+        for slot, (even_offset, odd_offset) in enumerate(blocks):
+            offset = jnp.where(odd, odd_offset, even_offset)
+            start = pl.multiple_of((place ^ offset) * rows, rows)
             placed_ref[slot * rows : (slot + 1) * rows, :] = turned_ref[pl.ds(start, rows), :]
         total = 3 * width // len(weight_outs)
         for k, ref in enumerate(weight_outs):
@@ -276,12 +292,13 @@
     )(order, *quarters, gain, weight, proj, low, high)
 
 
-def exchange(block, offset, total):
-    return lax.ppermute(block, AXES, [(i, i ^ offset) for i in range(total)])
+def exchange(block, even, odd, total):
+    pairs = [(i, i ^ (odd if i % 2 else even)) for i in range(total)]
+    return lax.ppermute(block, AXES, pairs)
 
 
 def send_slots(slots, offsets, total):
-    return [exchange(slots[k + 1], offset, total) for k, offset in enumerate(offsets)]
+    return [exchange(slots[k + 1], *offset, total) for k, offset in enumerate(offsets)]
 
 
 def add_slots(own, arrived):
@@ -305,12 +322,10 @@
         ]
 
     own, lon_start, lat_start, diag_start, table = pack(tokens, out_grad, bias_table)
-    quarters = [
-        own,
-        lax.ppermute(lon_start, AXES, route(1, 0)),
-        lax.ppermute(lat_start, AXES, route(0, -1)),
-        lax.ppermute(diag_start, AXES, route(1, -1)),
-    ]
+    at_lon = lax.ppermute(lon_start, AXES, route(1, 0))
+    at_diag = lax.ppermute(diag_start, AXES, route(1, -1))
+    at_lat = lax.ppermute(lat_start, AXES, route(0, -1))
+    quarters = [own, at_lon, at_diag, at_lat]
     flag = (lax.axis_index("lat") == lats - 1).astype(jnp.int32).reshape(1)
     low, high, weight, proj = relative_bias(flag, table, qkv_weight, proj_weight)
     rows = 3 * width // total
@@ -318,10 +333,10 @@
     if staged:
         far = total // 8
         blocks = tuple(
-            core + 2 * plane + 8 * line
+            (core + 2 * (k if core else PLANE[k]) + 8 * line, core + 2 * (PLANE[k] if core else k) + 8 * line)
             for core in range(2)
-            for plane in range(4)
-            for line in range(far)
+            for k in range(4)
+            for line in line_order(far)
         )
     else:
         blocks = None
@@ -341,11 +356,10 @@
     if staged:
         keep, send = weight_grads
         shape = (4, far, rows, width)
-        pair = add_slots(keep.reshape(shape), [exchange(send.reshape(shape), 1, total)]).astype(BF16)
-        plane = add_slots(pair[0], send_slots(pair, [2, 4, 6], total)).astype(BF16)
-        plane, to_lat = lax.optimization_barrier((plane, to_lat))
+        pair = add_slots(keep.reshape(shape), [exchange(send.reshape(shape), 1, 1, total)]).astype(BF16)
+        plane = add_slots(pair[0], send_slots(pair, [(2 * PLANE[k], 2 * k) for k in range(1, 4)], total)).astype(BF16)
         from_lat = lax.ppermute(to_lat, AXES, route(0, 1))
-        arrived = send_slots(plane, [8 * k for k in range(1, far)], total)
+        arrived = send_slots(plane, [(8 * k, 8 * k) for k in line_order(far)[1:]], total)
         summed = add_slots(plane[0], arrived).reshape(-1)
     else:
         from_lat = lax.ppermute(to_lat, AXES, route(0, 1))

time: 44.8 us -> 42.1 us (0.940)
  waiting for transfers between devices: 16.5 us -> 10.4 us
  starting transfers between devices: 16.2 us -> 19.7 us
    ppermute x1, waiting for transfers between devices: 7.42 us -> 2.24 us  [shards(): from_diag = lax.ppermute(to_diag, AXES, route(-1, 1))]
    ppermute x1, waiting for transfers between devices: 0.01 us -> 2.24 us  [shards(): from_lat = lax.ppermute(to_lat, AXES, route(0, 1))]
    ppermute x10, waiting for transfers between devices: 8.08 us -> 5.88 us  [the longest x7 5.45 us: exchange(): return lax.ppermute(block, AXES, pairs)]
    ppermute x1, starting transfers between devices: 0.74 us -> 2.62 us  [shards(): from_diag = lax.ppermute(to_diag, AXES, route(-1, 1))]
    ppermute x1, starting transfers between devices: 1.65 us -> 2.9 us  [shards(): from_lon = lax.ppermute(to_lon, AXES, route(-1, 0))]
    ppermute x1, waiting for transfers between devices: 1.02 us -> 0.01 us  [shards(): from_lon = lax.ppermute(to_lon, AXES, route(-1, 0))]
  transfers between devices with their start and end apart: 13 -> 13, of which waited for: 6 -> 7; matrix products, arithmetic and copies ran while one was open for 2% -> 2% of each run, Pallas kernels for 7% -> 8%
where the time goes in v3:
time: 42.1 us; the launch traced here: 41.9 us
  starting transfers between devices  19.7 us (47%)
  waiting for transfers between devices  10.4 us (25%)
  Pallas kernels  9.24 us (22%)
  other arithmetic  1.11 us (3%)
  local copies, waits for them, and re-layouts  0.8 us (2%)
  between operations  0.76 us (2%)
    ppermute x7, starting transfers between devices, exchange(): return lax.ppermute(block, AXES, pairs)  8.35 us
    ppermute x7, waiting for transfers between devices, exchange(): return lax.ppermute(block, AXES, pairs)  5.45 us
    pallas_call x1, Pallas kernels, window_backward(): pl.pallas_call(functools.partial(window_kernel, blocks), out_shape=(piece...  4.73 us
    pallas_call x1, Pallas kernels, relative_bias(): pl.pallas_call(bias_kernel, out_shape=(shape, shape, jax.ShapeDtypeStruct...  3.38 us
    ppermute x1, starting transfers between devices, shards(): at_lon = lax.ppermute(lon_start, AXES, route(1, 0))  2.99 us
    ppermute x1, starting transfers between devices, shards(): from_lon = lax.ppermute(to_lon, AXES, route(-1, 0))  2.9 us
    ppermute x1, starting transfers between devices, shards(): from_diag = lax.ppermute(to_diag, AXES, route(-1, 1))  2.62 us
    ppermute x1, waiting for transfers between devices, shards(): from_lat = lax.ppermute(to_lat, AXES, route(0, 1))  2.24 us
  transfers between devices with their start and end apart: 13, of which 7 were waited for; matrix products, arithmetic and copies ran while one was open for 2% of the time, Pallas kernels for 8%

profile of v3, /device:TPU:0, one launch (start us, length us, event | category | flops | bytes accessed | tf_op | source)
XLA Modules:
  0.0 41.9 jit_solution(1930350828034347399)
XLA Ops:
  0.6 0.0 copy-start
  0.6 1.1 %pack.1 = (bf16[72,512]{1,0:T(8,128)(2,1)S(1)}, bf16[72,512]{1,0:T(8,128)(2,1)S(1)}, bf16[72,512]{1,0:T(8,128)(2,1)S(1)}, bf16[72,512]{1,0:T(8,128)(2,1)S(1)}, f32[16,529]{1,0:T(8,128)S(1)}) custom-call(bf16[12,12,512]{2,1,0:T(8,128)(2,1)} %tokens_hbm.1, bf16[12,12,512]{2,1,0:T(8,128)(2,1)} %grad_hbm.1, f32[16,529]{1,0:T(8,128)} %table_hbm.1), custom_call_target="tpu_custom_call" | custom-call | bytes 1048576 | tf_op jit(solution)/shard_map/pack/pallas_call | solution.py:60
  1.8 3.0 %collective-permute-start = (bf16[72,512]{1,0:T(8,128)(2,1)S(1)}, bf16[72,512]{1,0:T(8,128)(2,1)S(1)}, u32[]{:S(2)}, u32[]{:S(2)}) collective-permute-start(bf16[72,512]{1,0:T(8,128)(2,1)S(1)} %get-tuple-element.18), channel_id=1, source_target_pairs={{0,4},{1,5},{2,6},{3,7},{4,8},{5,9},{6,10},{7,11},{8,12},{9,13},{1... | collective-permute-start | bytes 221192 | tf_op jit(solution)/shard_map/ppermute | solution.py:325
  4.8 1.7 %collective-permute-start.1 = (bf16[72,512]{1,0:T(8,128)(2,1)S(1)}, bf16[72,512]{1,0:T(8,128)(2,1)S(1)}, u32[]{:S(2)}, u32[]{:S(2)}) collective-permute-start(bf16[72,512]{1,0:T(8,128)(2,1)S(1)} %get-tuple-element.19), channel_id=1, source_target_pairs={{0,7},{1,4},{2,5},{3,6},{4,11},{5,8},{6,9},{7,10},{8,15},{9,12},{1... | collective-permute-start | bytes 221192 | tf_op jit(solution)/shard_map/ppermute | solution.py:326
  6.4 1.1 %collective-permute-start.2 = (bf16[72,512]{1,0:T(8,128)(2,1)S(1)}, bf16[72,512]{1,0:T(8,128)(2,1)S(1)}, u32[]{:S(2)}, u32[]{:S(2)}) collective-permute-start(bf16[72,512]{1,0:T(8,128)(2,1)S(1)} %get-tuple-element.20), channel_id=1, source_target_pairs={{0,3},{1,0},{2,1},{3,2},{4,7},{5,4},{6,5},{7,6},{8,11},{9,8},{10,9... | collective-permute-start | bytes 221192 | tf_op jit(solution)/shard_map/ppermute | solution.py:327
  7.6 3.4 %relative_bias.1 = (f32[2304,128]{1,0:T(8,128)S(1)}, f32[2304,128]{1,0:T(8,128)S(1)}, bf16[512,1536]{1,0:T(8,128)(2,1)S(1)}, bf16[512,512]{1,0:T(8,128)(2,1)S(1)}) custom-call(s32[1]{0:T(128)} %bitcast.2.flag_ref, f32[16,529]{1,0:T(8,128)S(1)} %get-tuple-element.21.table_ref, bf16[512,1536]{1,0:T(8,128)(2,1)} %weight_hbm.1, bf16[512,512]{1,0:T(8,128)(2,1)} %proj_hbm.1), custom_call_target="tpu_custom_call" | custom-call | flops 283115520 | bytes 6291456 | tf_op jit(solution)/shard_map/relative_bias/pallas_call | solution.py:134
  10.9 0.0 collective-permute-done.lon_ref
  11.0 0.4 %collective-permute-done.1.diag_ref = bf16[72,512]{1,0:T(8,128)(2,1)S(1)} collective-permute-done((bf16[72,512]{1,0:T(8,128)(2,1)S(1)}, bf16[72,512]{1,0:T(8,128)(2,1)S(1)}, u32[]{:S(2)}, u32[]{:S(2)}) %collective-permute-start.1) | collective-permute-done | bytes 73760 | tf_op jit(solution)/shard_map/ppermute | solution.py:326
  11.4 0.0 collective-permute-done.2.lat_ref
  11.4 0.0 copy-done
  11.4 4.7 %window_backward.1 = (bf16[36,512]{1,0:T(8,128)(2,1)S(1)}, bf16[36,512]{1,0:T(8,128)(2,1)S(1)}, bf16[36,512]{1,0:T(8,128)(2,1)S(1)}, bf16[36,512]{1,0:T(8,128)(2...) custom-call(s32[1]{0:T(128)} %bitcast.order_ref, bf16[72,512]{1,0:T(8,128)(2,1)S(1)} %get-tuple-element.17.own_ref, ...), custom_call_target="tpu_custom_call" | custom-call | flops 754974720 | bytes 6291456 | tf_op jit(solution)/shard_map/window_backward/pallas_call | solution.py:275
  16.1 1.2 %collective-permute-start.6 = (bf16[4,4,48,512]{3,2,1,0:T(8,128)(2,1)S(1)}, bf16[4,4,48,512]{3,2,1,0:T(8,128)(2,1)S(1)}, u32[]{:S(2)}, u32[]{:S(2)}) collective-permute-start(bf16[4,4,48,512]{3,2,1,0:T(8,128)(2,1)S(1)} %bitcast.33), channel_id=1, source_target_pairs={{0,1},{1,0},{2,3},{3,2},{4,5},{5,4},{6,7},{7,6},{8,9},{9,8},{10,11... | collective-permute-start | bytes 2359304 | tf_op jit(solution)/shard_map/ppermute | solution.py:297
  17.4 1.9 %collective-permute-done.6 = bf16[4,4,48,512]{3,2,1,0:T(8,128)(2,1)S(1)} collective-permute-done((bf16[4,4,48,512]{3,2,1,0:T(8,128)(2,1)S(1)}, bf16[4,4,48,512]{3,2,1,0:T(8,128)(2,1)S(1)}, u32[]{:S(2)}, u32[]{:S(2)}) %collective-permute-start.6) | collective-permute-done | bytes 786464 | tf_op jit(solution)/shard_map/ppermute | solution.py:297
  19.3 0.2 fusion
  19.6 0.4 collective-permute-start.7
  19.9 2.4 %collective-permute-start.9 = (bf16[4,48,512]{2,1,0:T(8,128)(2,1)S(1)}, bf16[4,48,512]{2,1,0:T(8,128)(2,1)S(1)}, u32[]{:S(2)}, u32[]{:S(2)}) collective-permute-start(bf16[4,48,512]{2,1,0:T(8,128)(2,1)S(1)} %get-tuple-element.33), channel_id=1, source_target_pairs={{0,6},{1,7},{2,4},{3,5},{4,2},{5,3},{6,0},{7,1},{8,14},{9,15},{10,... | collective-permute-start | bytes 589832 | tf_op jit(solution)/shard_map/ppermute | solution.py:297
  22.3 0.8 %collective-permute-start.8 = (bf16[4,48,512]{2,1,0:T(8,128)(2,1)S(1)}, bf16[4,48,512]{2,1,0:T(8,128)(2,1)S(1)}, u32[]{:S(2)}, u32[]{:S(2)}) collective-permute-start(bf16[4,48,512]{2,1,0:T(8,128)(2,1)S(1)} %get-tuple-element.34), channel_id=1, source_target_pairs={{0,2},{1,5},{2,0},{3,7},{4,6},{5,1},{6,4},{7,3},{8,10},{9,13},{10,... | collective-permute-start | bytes 589832 | tf_op jit(solution)/shard_map/ppermute | solution.py:297
  23.1 0.0 collective-permute-start.3
  23.1 2.6 %collective-permute-start.4 = (bf16[36,512]{1,0:T(8,128)(2,1)S(1)}, bf16[36,512]{1,0:T(8,128)(2,1)S(1)}, u32[]{:S(2)}, u32[]{:S(2)}) collective-permute-start(bf16[36,512]{1,0:T(8,128)(2,1)S(1)} %get-tuple-element.28), channel_id=1, source_target_pairs={{0,29},{1,30},{2,31},{3,28},{4,1},{5,2},{6,3},{7,0},{8,5},{9,6},{1... | collective-permute-start | bytes 110600 | tf_op jit(solution)/shard_map/ppermute | solution.py:355
  25.7 2.2 %collective-permute-done.3 = bf16[36,512]{1,0:T(8,128)(2,1)S(1)} collective-permute-done((bf16[36,512]{1,0:T(8,128)(2,1)S(1)}, bf16[36,512]{1,0:T(8,128)(2,1)S(1)}, u32[]{:S(2)}, u32[]{:S(2)}) %collective-permute-start.3) | collective-permute-done | bytes 36896 | tf_op jit(solution)/shard_map/ppermute | solution.py:361
  28.0 2.9 %collective-permute-start.5 = (bf16[36,512]{1,0:T(8,128)(2,1)S(1)}, bf16[36,512]{1,0:T(8,128)(2,1)S(1)}, u32[]{:S(2)}, u32[]{:S(2)}) collective-permute-start(bf16[36,512]{1,0:T(8,128)(2,1)S(1)} %get-tuple-element.29), channel_id=1, source_target_pairs={{0,28},{1,29},{2,30},{3,31},{4,0},{5,1},{6,2},{7,3},{8,4},{9,5},{1... | collective-permute-start | bytes 110600 | tf_op jit(solution)/shard_map/ppermute | solution.py:354
  30.9 2.2 %collective-permute-done.4 = bf16[36,512]{1,0:T(8,128)(2,1)S(1)} collective-permute-done((bf16[36,512]{1,0:T(8,128)(2,1)S(1)}, bf16[36,512]{1,0:T(8,128)(2,1)S(1)}, u32[]{:S(2)}, u32[]{:S(2)}) %collective-permute-start.4) | collective-permute-done | bytes 36896 | tf_op jit(solution)/shard_map/ppermute | solution.py:355
  33.2 0.0 collective-permute-done.5
  33.2 0.0 collective-permute-done.7
  33.2 0.0 collective-permute-done.9
  33.3 0.0 collective-permute-done.8
  33.3 0.1 fusion.3
  33.4 1.6 %collective-permute-start.10 = (bf16[48,512]{1,0:T(8,128)(2,1)S(1)}, bf16[48,512]{1,0:T(8,128)(2,1)S(1)}, u32[]{:S(2)}, u32[]{:S(2)}) collective-permute-start(bf16[48,512]{1,0:T(8,128)(2,1)S(1)} %get-tuple-element.35), channel_id=1, source_target_pairs={{0,16},{1,17},{2,18},{3,19},{4,20},{5,21},{6,22},{7,23},{8,24},{9,... | collective-permute-start | bytes 147464 | tf_op jit(solution)/shard_map/ppermute | solution.py:297
  35.0 1.3 %collective-permute-start.12 = (bf16[48,512]{1,0:T(8,128)(2,1)S(1)}, bf16[48,512]{1,0:T(8,128)(2,1)S(1)}, u32[]{:S(2)}, u32[]{:S(2)}) collective-permute-start(bf16[48,512]{1,0:T(8,128)(2,1)S(1)} %get-tuple-element.36), channel_id=1, source_target_pairs={{0,24},{1,25},{2,26},{3,27},{4,28},{5,29},{6,30},{7,31},{8,16},{9,... | collective-permute-start | bytes 147464 | tf_op jit(solution)/shard_map/ppermute | solution.py:297
  36.4 0.6 %collective-permute-start.11 = (bf16[48,512]{1,0:T(8,128)(2,1)S(1)}, bf16[48,512]{1,0:T(8,128)(2,1)S(1)}, u32[]{:S(2)}, u32[]{:S(2)}) collective-permute-start(bf16[48,512]{1,0:T(8,128)(2,1)S(1)} %get-tuple-element.37), channel_id=1, source_target_pairs={{0,8},{1,9},{2,10},{3,11},{4,12},{5,13},{6,14},{7,15},{8,0},{9,1},... | collective-permute-start | bytes 147464 | tf_op jit(solution)/shard_map/ppermute | solution.py:297
  37.0 0.7 %maximum_maximum_fusion = bf16[12,12,512]{2,1,0:T(8,128)(2,1)} fusion(bf16[6,6,512]{2,1,0:T(8,128)(2,1)S(1)} %reshape.47, bf16[6,6,512]{2,1,0:T(8,128)(2,1)S(1)} %reshape.46, bf16[6,6,512]{2,1,0:T(8,128)(2,1)S(1)} %reshape.45, bf16[6,6,512]{2,1,0:T(8,128)(2,1)S(1)} %reshape.44), kind=kLoop, calls=%fused_computation.10 | loop fusion | flops 589824 | bytes 294912 | tf_op jit(solution)/shard_map/concatenate | solution.py:372
  37.7 2.3 %collective-permute-done.10 = bf16[48,512]{1,0:T(8,128)(2,1)S(1)} collective-permute-done((bf16[48,512]{1,0:T(8,128)(2,1)S(1)}, bf16[48,512]{1,0:T(8,128)(2,1)S(1)}, u32[]{:S(2)}, u32[]{:S(2)}) %collective-permute-start.10) | collective-permute-done | bytes 49184 | tf_op jit(solution)/shard_map/ppermute | solution.py:297
  40.0 1.1 %collective-permute-done.12 = bf16[48,512]{1,0:T(8,128)(2,1)S(1)} collective-permute-done((bf16[48,512]{1,0:T(8,128)(2,1)S(1)}, bf16[48,512]{1,0:T(8,128)(2,1)S(1)}, u32[]{:S(2)}, u32[]{:S(2)}) %collective-permute-start.12) | collective-permute-done | bytes 49184 | tf_op jit(solution)/shard_map/ppermute | solution.py:297
  41.1 0.2 collective-permute-done.11
  41.3 0.7 %copy.8 = f32[6,4,8,128]{3,1,2,0:T(4,128)} copy(f32[6,4,8,128]{3,2,1,0:T(8,128)S(1)} %fusion.7) | data formatting | bytes 196608
  (7 shorter events, 0.2 us)
Async XLA Ops:
  0.6 10.8 %copy-start = (f32[512]{0:T(512)S(1)}, f32[512]{0:T(512)}, u32[]{:S(2)}) copy-start(f32[512]{0:T(512)} %param.7) | copy-start | bytes 6148
  1.8 9.2 %collective-permute-start = (bf16[72,512]{1,0:T(8,128)(2,1)S(1)}, bf16[72,512]{1,0:T(8,128)(2,1)S(1)}, u32[]{:S(2)}, u32[]{:S(2)}) collective-permute-start(bf16[72,512]{1,0:T(8,128)(2,1)S(1)} %get-tuple-element.18), channel_id=1, source_target_pairs={{0,4},{1,5},{2,6},{3,7},{4,8},{5,9},{6,10},{7,11},{8,12},{9,13},{1... | collective-permute-start | bytes 221192 | tf_op jit(solution)/shard_map/ppermute | solution.py:325
  4.8 6.6 %collective-permute-start.1 = (bf16[72,512]{1,0:T(8,128)(2,1)S(1)}, bf16[72,512]{1,0:T(8,128)(2,1)S(1)}, u32[]{:S(2)}, u32[]{:S(2)}) collective-permute-start(bf16[72,512]{1,0:T(8,128)(2,1)S(1)} %get-tuple-element.19), channel_id=1, source_target_pairs={{0,7},{1,4},{2,5},{3,6},{4,11},{5,8},{6,9},{7,10},{8,15},{9,12},{1... | collective-permute-start | bytes 221192 | tf_op jit(solution)/shard_map/ppermute | solution.py:326
  6.4 5.0 %collective-permute-start.2 = (bf16[72,512]{1,0:T(8,128)(2,1)S(1)}, bf16[72,512]{1,0:T(8,128)(2,1)S(1)}, u32[]{:S(2)}, u32[]{:S(2)}) collective-permute-start(bf16[72,512]{1,0:T(8,128)(2,1)S(1)} %get-tuple-element.20), channel_id=1, source_target_pairs={{0,3},{1,0},{2,1},{3,2},{4,7},{5,4},{6,5},{7,6},{8,11},{9,8},{10,9... | collective-permute-start | bytes 221192 | tf_op jit(solution)/shard_map/ppermute | solution.py:327
  16.1 3.2 %collective-permute-start.6 = (bf16[4,4,48,512]{3,2,1,0:T(8,128)(2,1)S(1)}, bf16[4,4,48,512]{3,2,1,0:T(8,128)(2,1)S(1)}, u32[]{:S(2)}, u32[]{:S(2)}) collective-permute-start(bf16[4,4,48,512]{3,2,1,0:T(8,128)(2,1)S(1)} %bitcast.33), channel_id=1, source_target_pairs={{0,1},{1,0},{2,3},{3,2},{4,5},{5,4},{6,7},{7,6},{8,9},{9,8},{10,11... | collective-permute-start | bytes 2359304 | tf_op jit(solution)/shard_map/ppermute | solution.py:297
  19.6 13.7 %collective-permute-start.7 = (bf16[4,48,512]{2,1,0:T(8,128)(2,1)S(1)}, bf16[4,48,512]{2,1,0:T(8,128)(2,1)S(1)}, u32[]{:S(2)}, u32[]{:S(2)}) collective-permute-start(bf16[4,48,512]{2,1,0:T(8,128)(2,1)S(1)} %get-tuple-element.32), channel_id=1, source_target_pairs={{0,4},{1,3},{2,6},{3,1},{4,0},{5,7},{6,2},{7,5},{8,12},{9,11},{10,... | collective-permute-start | bytes 589832 | tf_op jit(solution)/shard_map/ppermute | solution.py:297
  19.9 13.3 %collective-permute-start.9 = (bf16[4,48,512]{2,1,0:T(8,128)(2,1)S(1)}, bf16[4,48,512]{2,1,0:T(8,128)(2,1)S(1)}, u32[]{:S(2)}, u32[]{:S(2)}) collective-permute-start(bf16[4,48,512]{2,1,0:T(8,128)(2,1)S(1)} %get-tuple-element.33), channel_id=1, source_target_pairs={{0,6},{1,7},{2,4},{3,5},{4,2},{5,3},{6,0},{7,1},{8,14},{9,15},{10,... | collective-permute-start | bytes 589832 | tf_op jit(solution)/shard_map/ppermute | solution.py:297
  22.3 10.9 %collective-permute-start.8 = (bf16[4,48,512]{2,1,0:T(8,128)(2,1)S(1)}, bf16[4,48,512]{2,1,0:T(8,128)(2,1)S(1)}, u32[]{:S(2)}, u32[]{:S(2)}) collective-permute-start(bf16[4,48,512]{2,1,0:T(8,128)(2,1)S(1)} %get-tuple-element.34), channel_id=1, source_target_pairs={{0,2},{1,5},{2,0},{3,7},{4,6},{5,1},{6,4},{7,3},{8,10},{9,13},{10,... | collective-permute-start | bytes 589832 | tf_op jit(solution)/shard_map/ppermute | solution.py:297
  23.1 4.9 %collective-permute-start.3 = (bf16[36,512]{1,0:T(8,128)(2,1)S(1)}, bf16[36,512]{1,0:T(8,128)(2,1)S(1)}, u32[]{:S(2)}, u32[]{:S(2)}) collective-permute-start(bf16[36,512]{1,0:T(8,128)(2,1)S(1)} %get-tuple-element.26), channel_id=1, source_target_pairs={{0,1},{1,2},{2,3},{3,0},{4,5},{5,6},{6,7},{7,4},{8,9},{9,10},{10,1... | collective-permute-start | bytes 110600 | tf_op jit(solution)/shard_map/ppermute | solution.py:361
  23.1 10.0 %collective-permute-start.4 = (bf16[36,512]{1,0:T(8,128)(2,1)S(1)}, bf16[36,512]{1,0:T(8,128)(2,1)S(1)}, u32[]{:S(2)}, u32[]{:S(2)}) collective-permute-start(bf16[36,512]{1,0:T(8,128)(2,1)S(1)} %get-tuple-element.28), channel_id=1, source_target_pairs={{0,29},{1,30},{2,31},{3,28},{4,1},{5,2},{6,3},{7,0},{8,5},{9,6},{1... | collective-permute-start | bytes 110600 | tf_op jit(solution)/shard_map/ppermute | solution.py:355
  28.0 5.2 %collective-permute-start.5 = (bf16[36,512]{1,0:T(8,128)(2,1)S(1)}, bf16[36,512]{1,0:T(8,128)(2,1)S(1)}, u32[]{:S(2)}, u32[]{:S(2)}) collective-permute-start(bf16[36,512]{1,0:T(8,128)(2,1)S(1)} %get-tuple-element.29), channel_id=1, source_target_pairs={{0,28},{1,29},{2,30},{3,31},{4,0},{5,1},{6,2},{7,3},{8,4},{9,5},{1... | collective-permute-start | bytes 110600 | tf_op jit(solution)/shard_map/ppermute | solution.py:354
  33.4 6.6 %collective-permute-start.10 = (bf16[48,512]{1,0:T(8,128)(2,1)S(1)}, bf16[48,512]{1,0:T(8,128)(2,1)S(1)}, u32[]{:S(2)}, u32[]{:S(2)}) collective-permute-start(bf16[48,512]{1,0:T(8,128)(2,1)S(1)} %get-tuple-element.35), channel_id=1, source_target_pairs={{0,16},{1,17},{2,18},{3,19},{4,20},{5,21},{6,22},{7,23},{8,24},{9,... | collective-permute-start | bytes 147464 | tf_op jit(solution)/shard_map/ppermute | solution.py:297
  35.0 6.0 %collective-permute-start.12 = (bf16[48,512]{1,0:T(8,128)(2,1)S(1)}, bf16[48,512]{1,0:T(8,128)(2,1)S(1)}, u32[]{:S(2)}, u32[]{:S(2)}) collective-permute-start(bf16[48,512]{1,0:T(8,128)(2,1)S(1)} %get-tuple-element.36), channel_id=1, source_target_pairs={{0,24},{1,25},{2,26},{3,27},{4,28},{5,29},{6,30},{7,31},{8,16},{9,... | collective-permute-start | bytes 147464 | tf_op jit(solution)/shard_map/ppermute | solution.py:297
  36.4 4.9 %collective-permute-start.11 = (bf16[48,512]{1,0:T(8,128)(2,1)S(1)}, bf16[48,512]{1,0:T(8,128)(2,1)S(1)}, u32[]{:S(2)}, u32[]{:S(2)}) collective-permute-start(bf16[48,512]{1,0:T(8,128)(2,1)S(1)} %get-tuple-element.37), channel_id=1, source_target_pairs={{0,8},{1,9},{2,10},{3,11},{4,12},{5,13},{6,14},{7,15},{8,0},{9,1},... | collective-permute-start | bytes 147464 | tf_op jit(solution)/shard_map/ppermute | solution.py:297

commit v4 on v3

--- a/solution.py
+++ b/solution.py
@@ -162,14 +162,14 @@
     proj_ref,
     low_ref,
     high_ref,
-    own_out,
-    lon_out,
-    lat_out,
-    diag_out,
+    qkv_ref,
+    unit_ref,
+    inverse_ref,
+    grad_ref,
     *rest,
 ):
-    weight_outs = rest[:-5]
-    token_ref, grad_ref, qkv_ref, turned_ref, placed_ref = rest[-5:]
+    weight_outs = rest[:-3]
+    token_ref, turned_ref, placed_ref = rest[-3:]
     width = gain_ref.shape[1]
     heads = low_ref.shape[0] // AREA
     size = width // heads
@@ -184,6 +184,8 @@
     centred = inputs - jnp.mean(inputs, axis=-1, keepdims=True)
     inverse = lax.rsqrt(jnp.mean(centred * centred, axis=-1, keepdims=True) + 1e-05)
     unit = centred * inverse
+    unit_ref[...] = unit
+    inverse_ref[...] = jnp.broadcast_to(inverse, inverse_ref.shape)
     normed = (unit * gain).astype(BF16)
     qkv_ref[...] = dot(normed, weight_ref[...], 1, 0).astype(BF16)
     upstream = dot(grad_ref[...].astype(BF16), proj_ref[...], 1, 1).astype(BF16)
@@ -239,16 +241,6 @@
         qkv_ref[:, 2 * width + LANES * g : 2 * width + LANES * (g + 1)] = grad_values
         turned_ref[width + LANES * g : width + LANES * (g + 1), :] = grad_keys.T
         turned_ref[2 * width + LANES * g : 2 * width + LANES * (g + 1), :] = grad_values.T
-    grad_normed = dot(qkv_ref[...], weight_ref[...], 1, 1)
-    scaled = grad_normed * gain
-    result = grad_ref[...] + inverse * (
-        scaled
-        - jnp.mean(scaled, axis=-1, keepdims=True)
-        - unit * jnp.mean(scaled * unit, axis=-1, keepdims=True)
-    )
-    token_ref[...] = result
-    for k, ref in enumerate((lon_out, own_out, diag_out, lat_out)):
-        ref[...] = token_ref[QUARTER * k : QUARTER * (k + 1), :].astype(BF16)
     if blocks is None:
         weight_outs[0][...] = dot(turned_ref[...], normed, 1, 0)
     else:
@@ -266,7 +258,6 @@
 
 def window_backward(order, quarters, gain, weight, proj, low, high, blocks):
     width = proj.shape[0]
-    piece = jax.ShapeDtypeStruct((QUARTER, width), BF16)
     if blocks is None:
         weight_shapes = (jax.ShapeDtypeStruct((3 * width, width), F32),)
     else:
@@ -274,22 +265,83 @@
     vmem = pl.BlockSpec(memory_space=pltpu.VMEM)
     return pl.pallas_call(
         functools.partial(window_kernel, blocks),
-        out_shape=(piece,) * 4 + weight_shapes,
+        out_shape=(
+            jax.ShapeDtypeStruct((AREA, 3 * width), BF16),
+            jax.ShapeDtypeStruct((AREA, width), F32),
+            jax.ShapeDtypeStruct((AREA, LANES), F32),
+            jax.ShapeDtypeStruct((AREA, width), F32),
+        )
+        + weight_shapes,
         in_specs=[pl.BlockSpec(memory_space=pltpu.SMEM)] + [vmem] * 9,
         out_specs=(vmem,) * (4 + len(weight_shapes)),
         scratch_shapes=[
             pltpu.VMEM((AREA, width), F32),
-            pltpu.VMEM((AREA, width), F32),
-            pltpu.VMEM((AREA, 3 * width), BF16),
             pltpu.VMEM((3 * width, AREA), BF16),
             pltpu.VMEM((3 * width, AREA), BF16),
         ],
         compiler_params=pltpu.CompilerParams(vmem_limit_bytes=32 << 20),
         cost_estimate=pl.CostEstimate(
-            flops=2 * AREA * width * width * 10, bytes_accessed=6 << 20, transcendentals=16 * AREA * AREA
+            flops=2 * AREA * width * width * 7, bytes_accessed=6 << 20, transcendentals=16 * AREA * AREA
         ),
         name="window_backward",
     )(order, *quarters, gain, weight, proj, low, high)
+
+
+def norm_kernel(
+    qkv_ref, weight_ref, gain_ref, unit_ref, inverse_ref, grad_ref, own_out, lon_out, side_out, token_ref
+):
+    unit = unit_ref[...]
+    scaled = dot(qkv_ref[...], weight_ref[...], 1, 1) * gain_ref[...]
+    result = grad_ref[...] + inverse_ref[:, :1] * (
+        scaled
+        - jnp.mean(scaled, axis=-1, keepdims=True)
+        - unit * jnp.mean(scaled * unit, axis=-1, keepdims=True)
+    )
+    token_ref[...] = result
+    for k, ref in enumerate((lon_out, own_out, side_out.at[1], side_out.at[0])):
+        ref[...] = token_ref[QUARTER * k : QUARTER * (k + 1), :].astype(BF16)
+
+
+def norm_backward(qkv, weight, gain, unit, inverse, grad):
+    width = unit.shape[1]
+    piece = jax.ShapeDtypeStruct((QUARTER, width), BF16)
+    vmem = pl.BlockSpec(memory_space=pltpu.VMEM)
+    return pl.pallas_call(
+        norm_kernel,
+        out_shape=(piece, piece, jax.ShapeDtypeStruct((2, QUARTER, width), BF16)),
+        in_specs=[vmem] * 6,
+        out_specs=(vmem,) * 3,
+        scratch_shapes=[pltpu.VMEM((AREA, width), F32)],
+        compiler_params=pltpu.CompilerParams(vmem_limit_bytes=16 << 20),
+        cost_estimate=pl.CostEstimate(
+            flops=6 * AREA * width * width, bytes_accessed=3 << 20, transcendentals=0
+        ),
+        name="norm_backward",
+    )(qkv, weight, gain, unit, inverse, grad)
+
+
+def unpack_kernel(lon_ref, side_ref, own_ref, out_ref, line_ref):
+    for u in range(WIN):
+        left, right = (side_ref[0], own_ref[...]) if u < EDGE else (lon_ref[1], lon_ref[0])
+        rows = slice(u % EDGE * EDGE, u % EDGE * EDGE + EDGE)
+        line_ref[u, :EDGE, :] = left.astype(F32)[rows]
+        line_ref[u, EDGE:, :] = right.astype(F32)[rows]
+    out_ref[...] = line_ref[...].astype(BF16)
+
+
+def unpack(lon, side, own):
+    width = own.shape[1]
+    vmem = pl.BlockSpec(memory_space=pltpu.VMEM)
+    return pl.pallas_call(
+        unpack_kernel,
+        out_shape=jax.ShapeDtypeStruct((WIN, WIN, width), BF16),
+        in_specs=[vmem] * 3,
+        out_specs=vmem,
+        scratch_shapes=[pltpu.VMEM((WIN, WIN, width), F32)],
+        compiler_params=pltpu.CompilerParams(vmem_limit_bytes=8 << 20),
+        cost_estimate=pl.CostEstimate(flops=0, bytes_accessed=1 << 19, transcendentals=0),
+        name="unpack",
+    )(lon, side, own)
 
 
 def exchange(block, even, odd, total):
@@ -340,36 +392,35 @@
         )
     else:
         blocks = None
-    own, to_lon, to_lat, to_diag, *weight_grads = window_backward(
+    gain = norm_gain.reshape(1, width)
+    grad_qkv, unit, inverse, grad, *weight_grads = window_backward(
         place.astype(jnp.int32).reshape(1),
         quarters,
-        norm_gain.reshape(1, width),
+        gain,
         weight,
         proj,
         low,
         high,
         blocks,
     )
+    own, to_lon, to_side = norm_backward(grad_qkv, weight, gain, unit, inverse, grad)
     factor = 1.0 / math.sqrt(span_lon * lons * span_lat * lats)
-    from_lon = lax.ppermute(to_lon, AXES, route(-1, 0))
-    from_diag = lax.ppermute(to_diag, AXES, route(-1, 1))
     if staged:
         keep, send = weight_grads
+        keep, to_lon, to_side = lax.optimization_barrier((keep, to_lon, to_side))
         shape = (4, far, rows, width)
         pair = add_slots(keep.reshape(shape), [exchange(send.reshape(shape), 1, 1, total)]).astype(BF16)
-        plane = add_slots(pair[0], send_slots(pair, [(2 * PLANE[k], 2 * k) for k in range(1, 4)], total)).astype(BF16)
-        from_lat = lax.ppermute(to_lat, AXES, route(0, 1))
+        planes = [(2 * PLANE[k], 2 * k) for k in range(1, 4)]
+        plane = add_slots(pair[0], send_slots(pair, planes, total)).astype(BF16)
         arrived = send_slots(plane, [(8 * k, 8 * k) for k in line_order(far)[1:]], total)
         summed = add_slots(plane[0], arrived).reshape(-1)
     else:
-        from_lat = lax.ppermute(to_lat, AXES, route(0, 1))
         summed = lax.psum_scatter(
             weight_grads[0].reshape(-1), AXES, scatter_dimension=0, tiled=True
         )
-    cell = (EDGE, EDGE, width)
-    upper = jnp.concatenate([from_lat.reshape(cell), own.reshape(cell)], axis=1)
-    lower = jnp.concatenate([from_diag.reshape(cell), from_lon.reshape(cell)], axis=1)
-    token_grad = jnp.concatenate([upper, lower], axis=0)
+    from_side = lax.ppermute(to_side, AXES, route(0, 1))
+    from_lon = lax.ppermute(jnp.stack([to_lon, from_side[1]]), AXES, route(-1, 0))
+    token_grad = unpack(from_lon, from_side, own)
     return (token_grad, summed * factor)
 
 

time: 42.1 us -> 40.5 us (0.962)
  starting transfers between devices: 19.7 us -> 16.7 us
  Pallas kernels: 9.24 us -> 10.6 us
  waiting for transfers between devices: 10.4 us -> 11.2 us
  other arithmetic: 1.11 us -> 0.39 us
    ppermute x3 -> x2, starting transfers between devices: 5.52 us -> 2.57 us  [the longest x1 2.56 us: shards(): lax.ppermute(jnp.stack([to_lon, from_side[1]]), AXES, route(-1, 0))]
    ppermute x3 -> x2, waiting for transfers between devices: 4.48 us -> 7 us  [the longest x1 7 us: shards(): from_side = lax.ppermute(to_side, AXES, route(0, 1))]
    ppermute x7, waiting for transfers between devices: 5.45 us -> 3.78 us  [exchange(): return lax.ppermute(block, AXES, pairs)]
    pallas_call x1 -> x3, Pallas kernels: 4.73 us -> 6.07 us  [the longest x1 4.56 us: window_backward(): pl.pallas_call(functools.partial(window_kernel, blocks), out_shape=(jax.S...]
    concatenate x1 -> x0, other arithmetic: 0.74 us -> none  [shards(): token_grad = jnp.concatenate([upper, lower], axis=0)]
  transfers between devices with their start and end apart: 13 -> 12, of which waited for: 7 -> 6; matrix products, arithmetic and copies ran while one was open for 2% -> 0% of each run, Pallas kernels for 8% -> 12%
where the time goes in v4:
time: 40.5 us; the launch traced here: 40.3 us
  starting transfers between devices  16.7 us (41%)
  waiting for transfers between devices  11.2 us (28%)
  Pallas kernels  10.6 us (26%)
  local copies, waits for them, and re-layouts  0.73 us (2%)
  between operations  0.73 us (2%)
    ppermute x7, starting transfers between devices, exchange(): return lax.ppermute(block, AXES, pairs)  8.36 us
    ppermute x1, waiting for transfers between devices, shards(): from_side = lax.ppermute(to_side, AXES, route(0, 1))  7 us
    pallas_call x1, Pallas kernels, window_backward(): pl.pallas_call(functools.partial(window_kernel, blocks), out_shape=(jax.S...  4.56 us
    ppermute x7, waiting for transfers between devices, exchange(): return lax.ppermute(block, AXES, pairs)  3.78 us
    pallas_call x1, Pallas kernels, relative_bias(): pl.pallas_call(bias_kernel, out_shape=(shape, shape, jax.ShapeDtypeStruct...  3.38 us
    ppermute x1, starting transfers between devices, shards(): at_lon = lax.ppermute(lon_start, AXES, route(1, 0))  2.99 us
    ppermute x1, starting transfers between devices, shards(): lax.ppermute(jnp.stack([to_lon, from_side[1]]), AXES, route(-1, 0))  2.56 us
    ppermute x1, starting transfers between devices, shards(): at_diag = lax.ppermute(diag_start, AXES, route(1, -1))  1.66 us
  transfers between devices with their start and end apart: 12, of which 6 were waited for; matrix products, arithmetic and copies ran while one was open for 0% of the time, Pallas kernels for 12%

profile of v4, /device:TPU:0, one launch (start us, length us, event | category | flops | bytes accessed | tf_op | source)
XLA Modules:
  0.0 40.3 jit_solution(2110709047365025235)
XLA Ops:
  0.6 0.0 copy-start
  0.6 1.1 %pack.1 = (bf16[72,512]{1,0:T(8,128)(2,1)S(1)}, bf16[72,512]{1,0:T(8,128)(2,1)S(1)}, bf16[72,512]{1,0:T(8,128)(2,1)S(1)}, bf16[72,512]{1,0:T(8,128)(2,1)S(1)}, f32[16,529]{1,0:T(8,128)S(1)}) custom-call(bf16[12,12,512]{2,1,0:T(8,128)(2,1)} %tokens_hbm.1, bf16[12,12,512]{2,1,0:T(8,128)(2,1)} %grad_hbm.1, f32[16,529]{1,0:T(8,128)} %table_hbm.1), custom_call_target="tpu_custom_call" | custom-call | bytes 1048576 | tf_op jit(solution)/shard_map/pack/pallas_call | solution.py:60
  1.8 3.0 %collective-permute-start = (bf16[72,512]{1,0:T(8,128)(2,1)S(1)}, bf16[72,512]{1,0:T(8,128)(2,1)S(1)}, u32[]{:S(2)}, u32[]{:S(2)}) collective-permute-start(bf16[72,512]{1,0:T(8,128)(2,1)S(1)} %get-tuple-element.24), channel_id=1, source_target_pairs={{0,4},{1,5},{2,6},{3,7},{4,8},{5,9},{6,10},{7,11},{8,12},{9,13},{1... | collective-permute-start | bytes 221192 | tf_op jit(solution)/shard_map/ppermute | solution.py:377
  4.8 1.7 %collective-permute-start.1 = (bf16[72,512]{1,0:T(8,128)(2,1)S(1)}, bf16[72,512]{1,0:T(8,128)(2,1)S(1)}, u32[]{:S(2)}, u32[]{:S(2)}) collective-permute-start(bf16[72,512]{1,0:T(8,128)(2,1)S(1)} %get-tuple-element.25), channel_id=1, source_target_pairs={{0,7},{1,4},{2,5},{3,6},{4,11},{5,8},{6,9},{7,10},{8,15},{9,12},{1... | collective-permute-start | bytes 221192 | tf_op jit(solution)/shard_map/ppermute | solution.py:378
  6.4 1.1 %collective-permute-start.2 = (bf16[72,512]{1,0:T(8,128)(2,1)S(1)}, bf16[72,512]{1,0:T(8,128)(2,1)S(1)}, u32[]{:S(2)}, u32[]{:S(2)}) collective-permute-start(bf16[72,512]{1,0:T(8,128)(2,1)S(1)} %get-tuple-element.26), channel_id=1, source_target_pairs={{0,3},{1,0},{2,1},{3,2},{4,7},{5,4},{6,5},{7,6},{8,11},{9,8},{10,9... | collective-permute-start | bytes 221192 | tf_op jit(solution)/shard_map/ppermute | solution.py:379
  7.6 3.4 %relative_bias.1 = (f32[2304,128]{1,0:T(8,128)S(1)}, f32[2304,128]{1,0:T(8,128)S(1)}, bf16[512,1536]{1,0:T(8,128)(2,1)S(1)}, bf16[512,512]{1,0:T(8,128)(2,1)S(1)}) custom-call(s32[1]{0:T(128)} %bitcast.2.flag_ref, f32[16,529]{1,0:T(8,128)S(1)} %get-tuple-element.27.table_ref, bf16[512,1536]{1,0:T(8,128)(2,1)} %weight_hbm.1, bf16[512,512]{1,0:T(8,128)(2,1)} %proj_hbm.1), custom_call_target="tpu_custom_call" | custom-call | flops 283115520 | bytes 6291456 | tf_op jit(solution)/shard_map/relative_bias/pallas_call | solution.py:134
  10.9 0.0 collective-permute-done.lon_ref
  11.0 0.4 %collective-permute-done.1.diag_ref = bf16[72,512]{1,0:T(8,128)(2,1)S(1)} collective-permute-done((bf16[72,512]{1,0:T(8,128)(2,1)S(1)}, bf16[72,512]{1,0:T(8,128)(2,1)S(1)}, u32[]{:S(2)}, u32[]{:S(2)}) %collective-permute-start.1) | collective-permute-done | bytes 73760 | tf_op jit(solution)/shard_map/ppermute | solution.py:378
  11.4 0.0 collective-permute-done.2.lat_ref
  11.4 0.0 copy-done
  11.4 4.6 %window_backward.1 = (bf16[144,1536]{1,0:T(8,128)(2,1)S(1)}, f32[144,512]{1,0:T(8,128)S(1)}, f32[144,128]{1,0:T(8,128)S(1)}, f32[144,512]{1,0:T(8,128)S(1)}, bf1...) custom-call(s32[1]{0:T(128)} %bitcast.order_ref, bf16[72,512]{1,0:T(8,128)(2,1)S(1)} %get-tuple-element.23.own_ref, ...), custom_call_target="tpu_custom_call" | custom-call | flops 528482304 | bytes 6291456 | tf_op jit(solution)/shard_map/window_backward/pallas_call | solution.py:266
  16.0 1.3 %collective-permute-start.5 = (bf16[4,4,48,512]{3,2,1,0:T(8,128)(2,1)S(1)}, bf16[4,4,48,512]{3,2,1,0:T(8,128)(2,1)S(1)}, u32[]{:S(2)}, u32[]{:S(2)}) collective-permute-start(bf16[4,4,48,512]{3,2,1,0:T(8,128)(2,1)S(1)} %bitcast.36), channel_id=1, source_target_pairs={{0,1},{1,0},{2,3},{3,2},{4,5},{5,4},{6,7},{7,6},{8,9},{9,8},{10,11... | collective-permute-start | bytes 2359304 | tf_op jit(solution)/shard_map/ppermute | solution.py:349
  17.2 0.8 %norm_backward.1 = (bf16[36,512]{1,0:T(8,128)(2,1)S(1)}, bf16[36,512]{1,0:T(8,128)(2,1)S(1)}, bf16[2,36,512]{2,1,0:T(8,128)(2,1)S(1)}) custom-call(bf16[144,1536]{1,0:T(8,128)(2,1)S(1)} %get-tuple-element.33.qkv_ref, bf16[512,1536]{1,0:T(8,128)(2,1)S(1)} %get-tuple-element.28.weight_ref, f32[1,512]{1,0:T(1,128)S(1)} %bitcast.35, ...), custom_call_target="tpu_custom_call" | custom-call | flops 226492416 | bytes 3145728 | tf_op jit(solution)/shard_map/norm_backward/pallas_call | solution.py:309
  18.0 1.1 %collective-permute-done.5 = bf16[4,4,48,512]{3,2,1,0:T(8,128)(2,1)S(1)} collective-permute-done((bf16[4,4,48,512]{3,2,1,0:T(8,128)(2,1)S(1)}, bf16[4,4,48,512]{3,2,1,0:T(8,128)(2,1)S(1)}, u32[]{:S(2)}, u32[]{:S(2)}) %collective-permute-start.5) | collective-permute-done | bytes 786464 | tf_op jit(solution)/shard_map/ppermute | solution.py:349
  19.1 0.2 fusion
  19.4 0.3 collective-permute-start.6
  19.8 2.4 %collective-permute-start.8 = (bf16[4,48,512]{2,1,0:T(8,128)(2,1)S(1)}, bf16[4,48,512]{2,1,0:T(8,128)(2,1)S(1)}, u32[]{:S(2)}, u32[]{:S(2)}) collective-permute-start(bf16[4,48,512]{2,1,0:T(8,128)(2,1)S(1)} %get-tuple-element.45), channel_id=1, source_target_pairs={{0,6},{1,7},{2,4},{3,5},{4,2},{5,3},{6,0},{7,1},{8,14},{9,15},{10,... | collective-permute-start | bytes 589832 | tf_op jit(solution)/shard_map/ppermute | solution.py:349
  22.2 0.8 %collective-permute-start.7 = (bf16[4,48,512]{2,1,0:T(8,128)(2,1)S(1)}, bf16[4,48,512]{2,1,0:T(8,128)(2,1)S(1)}, u32[]{:S(2)}, u32[]{:S(2)}) collective-permute-start(bf16[4,48,512]{2,1,0:T(8,128)(2,1)S(1)} %get-tuple-element.46), channel_id=1, source_target_pairs={{0,2},{1,5},{2,0},{3,7},{4,6},{5,1},{6,4},{7,3},{8,10},{9,13},{10,... | collective-permute-start | bytes 589832 | tf_op jit(solution)/shard_map/ppermute | solution.py:349
  23.0 0.0 collective-permute-start.3
  23.0 7.0 %collective-permute-done.3.side_ref = bf16[2,36,512]{2,1,0:T(8,128)(2,1)S(1)} collective-permute-done((bf16[2,36,512]{2,1,0:T(8,128)(2,1)S(1)}, bf16[2,36,512]{2,1,0:T(8,128)(2,1)S(1)}, u32[]{:S(2)}, u32[]{:S(2)}) %collective-permute-start.3) | collective-permute-done | bytes 73760 | tf_op jit(solution)/shard_map/ppermute | solution.py:421
  30.0 2.6 %collective-permute-start.4 = (bf16[2,36,512]{2,1,0:T(8,128)(2,1)S(1)}, bf16[2,36,512]{2,1,0:T(8,128)(2,1)S(1)}, u32[]{:S(2)}, u32[]{:S(2)}) collective-permute-start(bf16[2,36,512]{2,1,0:T(8,128)(2,1)S(1)} %pad_maximum_fusion), channel_id=1, source_target_pairs={{0,28},{1,29},{2,30},{3,31},{4,0},{5,1},{6,2},{7,3},{8,4},{9,5},{1... | collective-permute-start | bytes 221192 | tf_op jit(solution)/shard_map/ppermute | solution.py:422
  32.6 0.0 collective-permute-done.6
  32.6 0.0 collective-permute-done.8
  32.6 0.0 collective-permute-done.7
  32.6 0.1 fusion.3
  32.7 0.8 %collective-permute-start.9 = (bf16[48,512]{1,0:T(8,128)(2,1)S(1)}, bf16[48,512]{1,0:T(8,128)(2,1)S(1)}, u32[]{:S(2)}, u32[]{:S(2)}) collective-permute-start(bf16[48,512]{1,0:T(8,128)(2,1)S(1)} %get-tuple-element.47), channel_id=1, source_target_pairs={{0,16},{1,17},{2,18},{3,19},{4,20},{5,21},{6,22},{7,23},{8,24},{9,... | collective-permute-start | bytes 147464 | tf_op jit(solution)/shard_map/ppermute | solution.py:349
  33.5 1.3 %collective-permute-start.11 = (bf16[48,512]{1,0:T(8,128)(2,1)S(1)}, bf16[48,512]{1,0:T(8,128)(2,1)S(1)}, u32[]{:S(2)}, u32[]{:S(2)}) collective-permute-start(bf16[48,512]{1,0:T(8,128)(2,1)S(1)} %get-tuple-element.48), channel_id=1, source_target_pairs={{0,24},{1,25},{2,26},{3,27},{4,28},{5,29},{6,30},{7,31},{8,16},{9,... | collective-permute-start | bytes 147464 | tf_op jit(solution)/shard_map/ppermute | solution.py:349
  34.8 1.4 %collective-permute-start.10 = (bf16[48,512]{1,0:T(8,128)(2,1)S(1)}, bf16[48,512]{1,0:T(8,128)(2,1)S(1)}, u32[]{:S(2)}, u32[]{:S(2)}) collective-permute-start(bf16[48,512]{1,0:T(8,128)(2,1)S(1)} %get-tuple-element.49), channel_id=1, source_target_pairs={{0,8},{1,9},{2,10},{3,11},{4,12},{5,13},{6,14},{7,15},{8,0},{9,1},... | collective-permute-start | bytes 147464 | tf_op jit(solution)/shard_map/ppermute | solution.py:349
  36.3 0.0 collective-permute-done.4.lon_ref
  36.3 0.7 %unpack.1 = bf16[12,12,512]{2,1,0:T(8,128)(2,1)} custom-call(bf16[2,36,512]{2,1,0:T(8,128)(2,1)S(1)} %collective-permute-done.4.lon_ref, bf16[2,36,512]{2,1,0:T(8,128)(2,1)S(1)} %collective-permute-done.3.side_ref, bf16[36,512]{1,0:T(8,128)(2,1)S(1)} %get-tuple-element.41.own_ref), custom_call_target="tpu_custom_call" | custom-call | bytes 524288 | tf_op jit(solution)/shard_map/unpack/pallas_call | solution.py:335
  37.0 1.6 %collective-permute-done.9 = bf16[48,512]{1,0:T(8,128)(2,1)S(1)} collective-permute-done((bf16[48,512]{1,0:T(8,128)(2,1)S(1)}, bf16[48,512]{1,0:T(8,128)(2,1)S(1)}, u32[]{:S(2)}, u32[]{:S(2)}) %collective-permute-start.9) | collective-permute-done | bytes 49184 | tf_op jit(solution)/shard_map/ppermute | solution.py:349
  38.6 0.9 %collective-permute-done.11 = bf16[48,512]{1,0:T(8,128)(2,1)S(1)} collective-permute-done((bf16[48,512]{1,0:T(8,128)(2,1)S(1)}, bf16[48,512]{1,0:T(8,128)(2,1)S(1)}, u32[]{:S(2)}, u32[]{:S(2)}) %collective-permute-start.11) | collective-permute-done | bytes 49184 | tf_op jit(solution)/shard_map/ppermute | solution.py:349
  39.5 0.1 collective-permute-done.10
  39.7 0.7 %copy.8 = f32[6,4,8,128]{3,1,2,0:T(4,128)} copy(f32[6,4,8,128]{3,2,1,0:T(8,128)S(1)} %fusion.7) | data formatting | bytes 196608
  (5 shorter events, 0.1 us)
Async XLA Ops:
  0.6 10.8 %copy-start = (f32[512]{0:T(512)S(1)}, f32[512]{0:T(512)}, u32[]{:S(2)}) copy-start(f32[512]{0:T(512)} %param.7) | copy-start | bytes 6148
  1.8 9.2 %collective-permute-start = (bf16[72,512]{1,0:T(8,128)(2,1)S(1)}, bf16[72,512]{1,0:T(8,128)(2,1)S(1)}, u32[]{:S(2)}, u32[]{:S(2)}) collective-permute-start(bf16[72,512]{1,0:T(8,128)(2,1)S(1)} %get-tuple-element.24), channel_id=1, source_target_pairs={{0,4},{1,5},{2,6},{3,7},{4,8},{5,9},{6,10},{7,11},{8,12},{9,13},{1... | collective-permute-start | bytes 221192 | tf_op jit(solution)/shard_map/ppermute | solution.py:377
  4.8 6.6 %collective-permute-start.1 = (bf16[72,512]{1,0:T(8,128)(2,1)S(1)}, bf16[72,512]{1,0:T(8,128)(2,1)S(1)}, u32[]{:S(2)}, u32[]{:S(2)}) collective-permute-start(bf16[72,512]{1,0:T(8,128)(2,1)S(1)} %get-tuple-element.25), channel_id=1, source_target_pairs={{0,7},{1,4},{2,5},{3,6},{4,11},{5,8},{6,9},{7,10},{8,15},{9,12},{1... | collective-permute-start | bytes 221192 | tf_op jit(solution)/shard_map/ppermute | solution.py:378
  6.4 5.0 %collective-permute-start.2 = (bf16[72,512]{1,0:T(8,128)(2,1)S(1)}, bf16[72,512]{1,0:T(8,128)(2,1)S(1)}, u32[]{:S(2)}, u32[]{:S(2)}) collective-permute-start(bf16[72,512]{1,0:T(8,128)(2,1)S(1)} %get-tuple-element.26), channel_id=1, source_target_pairs={{0,3},{1,0},{2,1},{3,2},{4,7},{5,4},{6,5},{7,6},{8,11},{9,8},{10,9... | collective-permute-start | bytes 221192 | tf_op jit(solution)/shard_map/ppermute | solution.py:379
  16.0 3.2 %collective-permute-start.5 = (bf16[4,4,48,512]{3,2,1,0:T(8,128)(2,1)S(1)}, bf16[4,4,48,512]{3,2,1,0:T(8,128)(2,1)S(1)}, u32[]{:S(2)}, u32[]{:S(2)}) collective-permute-start(bf16[4,4,48,512]{3,2,1,0:T(8,128)(2,1)S(1)} %bitcast.36), channel_id=1, source_target_pairs={{0,1},{1,0},{2,3},{3,2},{4,5},{5,4},{6,7},{7,6},{8,9},{9,8},{10,11... | collective-permute-start | bytes 2359304 | tf_op jit(solution)/shard_map/ppermute | solution.py:349
  19.4 13.1 %collective-permute-start.6 = (bf16[4,48,512]{2,1,0:T(8,128)(2,1)S(1)}, bf16[4,48,512]{2,1,0:T(8,128)(2,1)S(1)}, u32[]{:S(2)}, u32[]{:S(2)}) collective-permute-start(bf16[4,48,512]{2,1,0:T(8,128)(2,1)S(1)} %get-tuple-element.44), channel_id=1, source_target_pairs={{0,4},{1,3},{2,6},{3,1},{4,0},{5,7},{6,2},{7,5},{8,12},{9,11},{10,... | collective-permute-start | bytes 589832 | tf_op jit(solution)/shard_map/ppermute | solution.py:349
  19.8 12.8 %collective-permute-start.8 = (bf16[4,48,512]{2,1,0:T(8,128)(2,1)S(1)}, bf16[4,48,512]{2,1,0:T(8,128)(2,1)S(1)}, u32[]{:S(2)}, u32[]{:S(2)}) collective-permute-start(bf16[4,48,512]{2,1,0:T(8,128)(2,1)S(1)} %get-tuple-element.45), channel_id=1, source_target_pairs={{0,6},{1,7},{2,4},{3,5},{4,2},{5,3},{6,0},{7,1},{8,14},{9,15},{10,... | collective-permute-start | bytes 589832 | tf_op jit(solution)/shard_map/ppermute | solution.py:349
  22.2 10.4 %collective-permute-start.7 = (bf16[4,48,512]{2,1,0:T(8,128)(2,1)S(1)}, bf16[4,48,512]{2,1,0:T(8,128)(2,1)S(1)}, u32[]{:S(2)}, u32[]{:S(2)}) collective-permute-start(bf16[4,48,512]{2,1,0:T(8,128)(2,1)S(1)} %get-tuple-element.46), channel_id=1, source_target_pairs={{0,2},{1,5},{2,0},{3,7},{4,6},{5,1},{6,4},{7,3},{8,10},{9,13},{10,... | collective-permute-start | bytes 589832 | tf_op jit(solution)/shard_map/ppermute | solution.py:349
  23.0 7.0 %collective-permute-start.3 = (bf16[2,36,512]{2,1,0:T(8,128)(2,1)S(1)}, bf16[2,36,512]{2,1,0:T(8,128)(2,1)S(1)}, u32[]{:S(2)}, u32[]{:S(2)}) collective-permute-start(bf16[2,36,512]{2,1,0:T(8,128)(2,1)S(1)} %get-tuple-element.40), channel_id=1, source_target_pairs={{0,1},{1,2},{2,3},{3,0},{4,5},{5,6},{6,7},{7,4},{8,9},{9,10},{10,1... | collective-permute-start | bytes 221192 | tf_op jit(solution)/shard_map/ppermute | solution.py:421
  30.0 6.3 %collective-permute-start.4 = (bf16[2,36,512]{2,1,0:T(8,128)(2,1)S(1)}, bf16[2,36,512]{2,1,0:T(8,128)(2,1)S(1)}, u32[]{:S(2)}, u32[]{:S(2)}) collective-permute-start(bf16[2,36,512]{2,1,0:T(8,128)(2,1)S(1)} %pad_maximum_fusion), channel_id=1, source_target_pairs={{0,28},{1,29},{2,30},{3,31},{4,0},{5,1},{6,2},{7,3},{8,4},{9,5},{1... | collective-permute-start | bytes 221192 | tf_op jit(solution)/shard_map/ppermute | solution.py:422
  32.7 5.9 %collective-permute-start.9 = (bf16[48,512]{1,0:T(8,128)(2,1)S(1)}, bf16[48,512]{1,0:T(8,128)(2,1)S(1)}, u32[]{:S(2)}, u32[]{:S(2)}) collective-permute-start(bf16[48,512]{1,0:T(8,128)(2,1)S(1)} %get-tuple-element.47), channel_id=1, source_target_pairs={{0,16},{1,17},{2,18},{3,19},{4,20},{5,21},{6,22},{7,23},{8,24},{9,... | collective-permute-start | bytes 147464 | tf_op jit(solution)/shard_map/ppermute | solution.py:349
  33.5 6.0 %collective-permute-start.11 = (bf16[48,512]{1,0:T(8,128)(2,1)S(1)}, bf16[48,512]{1,0:T(8,128)(2,1)S(1)}, u32[]{:S(2)}, u32[]{:S(2)}) collective-permute-start(bf16[48,512]{1,0:T(8,128)(2,1)S(1)} %get-tuple-element.48), channel_id=1, source_target_pairs={{0,24},{1,25},{2,26},{3,27},{4,28},{5,29},{6,30},{7,31},{8,16},{9,... | collective-permute-start | bytes 147464 | tf_op jit(solution)/shard_map/ppermute | solution.py:349
  34.8 4.8 %collective-permute-start.10 = (bf16[48,512]{1,0:T(8,128)(2,1)S(1)}, bf16[48,512]{1,0:T(8,128)(2,1)S(1)}, u32[]{:S(2)}, u32[]{:S(2)}) collective-permute-start(bf16[48,512]{1,0:T(8,128)(2,1)S(1)} %get-tuple-element.49), channel_id=1, source_target_pairs={{0,8},{1,9},{2,10},{3,11},{4,12},{5,13},{6,14},{7,15},{8,0},{9,1},... | collective-permute-start | bytes 147464 | tf_op jit(solution)/shard_map/ppermute | solution.py:349

commit v5 on v4

--- a/solution.py
+++ b/solution.py
@@ -191,56 +191,88 @@
     upstream = dot(grad_ref[...].astype(BF16), proj_ref[...], 1, 1).astype(BF16)
     lane = lax.broadcasted_iota(jnp.int32, (AREA, LANES), 1)
     zero = jnp.zeros((AREA, LANES), BF16)
-    for g in range(width // LANES):
-        cols = slice(LANES * g, LANES * (g + 1))
-        query = qkv_ref[:, LANES * g : LANES * (g + 1)]
-        keys = qkv_ref[:, width + LANES * g : width + LANES * (g + 1)]
-        values = qkv_ref[:, 2 * width + LANES * g : 2 * width + LANES * (g + 1)]
-        up = upstream[:, cols]
-        keys_turned = keys.T
-        here = [(lane >= size * n) & (lane < size * (n + 1)) for n in range(group)]
-        all_scores = dot(
-            jnp.concatenate([jnp.where(m, keys, zero) for m in here], axis=0), query, 1, 1
+    here = [(lane >= size * n) & (lane < size * (n + 1)) for n in range(group)]
+    left = AREA - LANES
+    packed = LANES // left
+    span = packed * size
+    row = lax.broadcasted_iota(jnp.int32, (LANES, span), 0)
+    col = lax.broadcasted_iota(jnp.int32, (LANES, span), 1)
+    own_block = row // left == col // size
+
+    def diagonal(block):
+        return jnp.where(own_block, jnp.concatenate([block] * packed, axis=0), jnp.zeros((LANES, span), BF16))
+
+    def attend(scores, grad_probs, bias):
+        scores = scores * factor + bias
+        weights = jnp.exp(scores - jnp.max(scores, axis=0, keepdims=True))
+        probs = weights * (1.0 / jnp.sum(weights, axis=0, keepdims=True))
+        centre = jnp.sum(probs * grad_probs, axis=0, keepdims=True)
+        return probs.astype(BF16), (probs * (grad_probs - centre) * factor).astype(BF16)
+
+    for f in range(width // span):
+        base = span * f
+        query_all = qkv_ref[:, base : base + span]
+        keys_all = qkv_ref[:, width + base : width + base + span]
+        values_all = qkv_ref[:, 2 * width + base : 2 * width + base + span]
+        up_all = upstream[:, base : base + span]
+        keys_turned = keys_all.T
+        query_left = diagonal(query_all[LANES:])
+        up_left = diagonal(up_all[LANES:])
+        bias = None
+        for n in range(packed):
+            part = high_ref[pl.ds(f * packed + n, AREA, stride=heads), :]
+            if n == 0:
+                bias = part
+            else:
+                bias = jnp.where(lane >= left * n, pltpu.roll(part, left * n, 1), bias)
+        probs, grad_scores = attend(
+            dot(keys_all, query_left, 1, 1), dot(values_all, up_left, 1, 1), bias
         )
-        all_grads = dot(
-            jnp.concatenate([jnp.where(m, values, zero) for m in here], axis=0), up, 1, 1
-        )
-        low_probs, low_scores = [], []
-        for n in range(group):
-            h = g * group + n
-            rows = slice(AREA * n, AREA * (n + 1))
-            bias = jnp.concatenate(
-                [
-                    low_ref[pl.ds(h, AREA, stride=heads), :],
-                    high_ref[pl.ds(h, AREA, stride=heads), :],
-                ],
-                axis=1,
-            )[:, :AREA]
-            scores = all_scores[rows] * factor + bias
-            peak = jnp.max(scores, axis=0, keepdims=True)
-            weights = jnp.exp(scores - peak)
-            probs = weights * (1.0 / jnp.sum(weights, axis=0, keepdims=True))
-            grad_probs = all_grads[rows]
-            centre = jnp.sum(probs * grad_probs, axis=0, keepdims=True)
-            grad_scores = (probs * (grad_probs - centre) * factor).astype(BF16)
-            low_probs.append(probs.astype(BF16))
-            low_scores.append(grad_scores)
-            part_query = dot(keys_turned[size * n : size * (n + 1)], grad_scores, 1, 0)
-            turned_ref[h * size : (h + 1) * size, :] = part_query.astype(BF16)
-        all_values = dot(jnp.concatenate(low_probs, axis=0), up, 1, 0)
-        all_keys = dot(jnp.concatenate(low_scores, axis=0), query, 1, 0)
-        grad_values, grad_keys = all_values[:AREA], all_keys[:AREA]
-        for n in range(1, group):
-            rows = slice(AREA * n, AREA * (n + 1))
-            grad_values = jnp.where(here[n], all_values[rows], grad_values)
-            grad_keys = jnp.where(here[n], all_keys[rows], grad_keys)
-        grad_values = grad_values.astype(BF16)
-        grad_keys = grad_keys.astype(BF16)
-        qkv_ref[:, LANES * g : LANES * (g + 1)] = turned_ref[cols, :].T
-        qkv_ref[:, width + LANES * g : width + LANES * (g + 1)] = grad_keys
-        qkv_ref[:, 2 * width + LANES * g : 2 * width + LANES * (g + 1)] = grad_values
-        turned_ref[width + LANES * g : width + LANES * (g + 1), :] = grad_keys.T
-        turned_ref[2 * width + LANES * g : 2 * width + LANES * (g + 1), :] = grad_values.T
+        left_values = dot(probs, up_left, 1, 0)
+        left_keys = dot(grad_scores, query_left, 1, 0)
+        left_query = dot(keys_turned, grad_scores, 1, 0)
+        for n in range(packed):
+            part = left_query[size * n : size * (n + 1)]
+            if n:
+                part = pltpu.roll(part, LANES - left * n, 1)
+            turned_ref[base + size * n : base + size * (n + 1), LANES:] = part[:, :left].astype(BF16)
+        for g in range(span // LANES):
+            inner = slice(LANES * g, LANES * (g + 1))
+            start = base + LANES * g
+            query = query_all[:LANES, inner]
+            keys = keys_all[:, inner]
+            values = values_all[:, inner]
+            up = up_all[:LANES, inner]
+            all_scores = dot(
+                jnp.concatenate([jnp.where(m, keys, zero) for m in here], axis=0), query, 1, 1
+            )
+            all_grads = dot(
+                jnp.concatenate([jnp.where(m, values, zero) for m in here], axis=0), up, 1, 1
+            )
+            low_probs, low_scores = [], []
+            for n in range(group):
+                first = start + size * n
+                rows = slice(AREA * n, AREA * (n + 1))
+                bias = low_ref[pl.ds(first // size, AREA, stride=heads), :]
+                probs, grad_scores = attend(all_scores[rows], all_grads[rows], bias)
+                low_probs.append(probs)
+                low_scores.append(grad_scores)
+                part = dot(keys_turned[LANES * g + size * n : LANES * g + size * (n + 1)], grad_scores, 1, 0)
+                turned_ref[first : first + size, :LANES] = part.astype(BF16)
+            all_values = dot(jnp.concatenate(low_probs, axis=0), up, 1, 0)
+            all_keys = dot(jnp.concatenate(low_scores, axis=0), query, 1, 0)
+            grad_values, grad_keys = all_values[:AREA], all_keys[:AREA]
+            for n in range(1, group):
+                rows = slice(AREA * n, AREA * (n + 1))
+                grad_values = jnp.where(here[n], all_values[rows], grad_values)
+                grad_keys = jnp.where(here[n], all_keys[rows], grad_keys)
+            grad_values = (grad_values + left_values[:, inner]).astype(BF16)
+            grad_keys = (grad_keys + left_keys[:, inner]).astype(BF16)
+            qkv_ref[:, start : start + LANES] = turned_ref[start : start + LANES, :].T
+            qkv_ref[:, width + start : width + start + LANES] = grad_keys
+            qkv_ref[:, 2 * width + start : 2 * width + start + LANES] = grad_values
+            turned_ref[width + start : width + start + LANES, :] = grad_keys.T
+            turned_ref[2 * width + start : 2 * width + start + LANES, :] = grad_values.T
     if blocks is None:
         weight_outs[0][...] = dot(turned_ref[...], normed, 1, 0)
     else:

time: 40.5 us -> 39.7 us (0.980)
  Pallas kernels: 10.6 us -> 9.81 us
    pallas_call x1, Pallas kernels: 4.56 us -> 3.79 us  [window_backward(): pl.pallas_call(functools.partial(window_kernel, blocks), out_shape=(jax.S...]
where the time goes in v5:
time: 39.7 us; the launch traced here: 39.6 us
  starting transfers between devices  16.7 us (42%)
  waiting for transfers between devices  11.2 us (28%)
  Pallas kernels  9.81 us (25%)
  local copies, waits for them, and re-layouts  0.73 us (2%)
  between operations  0.73 us (2%)
    ppermute x7, starting transfers between devices, exchange(): return lax.ppermute(block, AXES, pairs)  8.35 us
    ppermute x1, waiting for transfers between devices, shards(): from_side = lax.ppermute(to_side, AXES, route(0, 1))  6.99 us
    pallas_call x1, Pallas kernels, window_backward(): pl.pallas_call(functools.partial(window_kernel, blocks), out_shape=(jax.S...  3.79 us
    ppermute x7, waiting for transfers between devices, exchange(): return lax.ppermute(block, AXES, pairs)  3.77 us
    pallas_call x1, Pallas kernels, relative_bias(): pl.pallas_call(bias_kernel, out_shape=(shape, shape, jax.ShapeDtypeStruct...  3.38 us
    ppermute x1, starting transfers between devices, shards(): at_lon = lax.ppermute(lon_start, AXES, route(1, 0))  2.99 us
    ppermute x1, starting transfers between devices, shards(): lax.ppermute(jnp.stack([to_lon, from_side[1]]), AXES, route(-1, 0))  2.57 us
    ppermute x1, starting transfers between devices, shards(): at_diag = lax.ppermute(diag_start, AXES, route(1, -1))  1.66 us
  transfers between devices with their start and end apart: 12, of which 6 were waited for; matrix products, arithmetic and copies ran while one was open for 0% of the time, Pallas kernels for 12%

profile of v5, /device:TPU:0, one launch (start us, length us, event | category | flops | bytes accessed | tf_op | source)
XLA Modules:
  0.0 39.6 jit_solution(5777285081543551164)
XLA Ops:
  0.6 0.0 copy-start
  0.6 1.1 %pack.1 = (bf16[72,512]{1,0:T(8,128)(2,1)S(1)}, bf16[72,512]{1,0:T(8,128)(2,1)S(1)}, bf16[72,512]{1,0:T(8,128)(2,1)S(1)}, bf16[72,512]{1,0:T(8,128)(2,1)S(1)}, f32[16,529]{1,0:T(8,128)S(1)}) custom-call(bf16[12,12,512]{2,1,0:T(8,128)(2,1)} %tokens_hbm.1, bf16[12,12,512]{2,1,0:T(8,128)(2,1)} %grad_hbm.1, f32[16,529]{1,0:T(8,128)} %table_hbm.1), custom_call_target="tpu_custom_call" | custom-call | bytes 1048576 | tf_op jit(solution)/shard_map/pack/pallas_call | solution.py:60
  1.8 3.0 %collective-permute-start = (bf16[72,512]{1,0:T(8,128)(2,1)S(1)}, bf16[72,512]{1,0:T(8,128)(2,1)S(1)}, u32[]{:S(2)}, u32[]{:S(2)}) collective-permute-start(bf16[72,512]{1,0:T(8,128)(2,1)S(1)} %get-tuple-element.24), channel_id=1, source_target_pairs={{0,4},{1,5},{2,6},{3,7},{4,8},{5,9},{6,10},{7,11},{8,12},{9,13},{1... | collective-permute-start | bytes 221192 | tf_op jit(solution)/shard_map/ppermute | solution.py:409
  4.8 1.7 %collective-permute-start.1 = (bf16[72,512]{1,0:T(8,128)(2,1)S(1)}, bf16[72,512]{1,0:T(8,128)(2,1)S(1)}, u32[]{:S(2)}, u32[]{:S(2)}) collective-permute-start(bf16[72,512]{1,0:T(8,128)(2,1)S(1)} %get-tuple-element.25), channel_id=1, source_target_pairs={{0,7},{1,4},{2,5},{3,6},{4,11},{5,8},{6,9},{7,10},{8,15},{9,12},{1... | collective-permute-start | bytes 221192 | tf_op jit(solution)/shard_map/ppermute | solution.py:410
  6.4 1.1 %collective-permute-start.2 = (bf16[72,512]{1,0:T(8,128)(2,1)S(1)}, bf16[72,512]{1,0:T(8,128)(2,1)S(1)}, u32[]{:S(2)}, u32[]{:S(2)}) collective-permute-start(bf16[72,512]{1,0:T(8,128)(2,1)S(1)} %get-tuple-element.26), channel_id=1, source_target_pairs={{0,3},{1,0},{2,1},{3,2},{4,7},{5,4},{6,5},{7,6},{8,11},{9,8},{10,9... | collective-permute-start | bytes 221192 | tf_op jit(solution)/shard_map/ppermute | solution.py:411
  7.6 3.4 %relative_bias.1 = (f32[2304,128]{1,0:T(8,128)S(1)}, f32[2304,128]{1,0:T(8,128)S(1)}, bf16[512,1536]{1,0:T(8,128)(2,1)S(1)}, bf16[512,512]{1,0:T(8,128)(2,1)S(1)}) custom-call(s32[1]{0:T(128)} %bitcast.2.flag_ref, f32[16,529]{1,0:T(8,128)S(1)} %get-tuple-element.27.table_ref, bf16[512,1536]{1,0:T(8,128)(2,1)} %weight_hbm.1, bf16[512,512]{1,0:T(8,128)(2,1)} %proj_hbm.1), custom_call_target="tpu_custom_call" | custom-call | flops 283115520 | bytes 6291456 | tf_op jit(solution)/shard_map/relative_bias/pallas_call | solution.py:134
  10.9 0.0 collective-permute-done.lon_ref
  11.0 0.4 %collective-permute-done.1.diag_ref = bf16[72,512]{1,0:T(8,128)(2,1)S(1)} collective-permute-done((bf16[72,512]{1,0:T(8,128)(2,1)S(1)}, bf16[72,512]{1,0:T(8,128)(2,1)S(1)}, u32[]{:S(2)}, u32[]{:S(2)}) %collective-permute-start.1) | collective-permute-done | bytes 73760 | tf_op jit(solution)/shard_map/ppermute | solution.py:410
  11.4 0.0 collective-permute-done.2.lat_ref
  11.4 0.0 copy-done
  11.4 3.8 %window_backward.1 = (bf16[144,1536]{1,0:T(8,128)(2,1)S(1)}, f32[144,512]{1,0:T(8,128)S(1)}, f32[144,128]{1,0:T(8,128)S(1)}, f32[144,512]{1,0:T(8,128)S(1)}, bf1...) custom-call(s32[1]{0:T(128)} %bitcast.order_ref, bf16[72,512]{1,0:T(8,128)(2,1)S(1)} %get-tuple-element.23.own_ref, ...), custom_call_target="tpu_custom_call" | custom-call | flops 528482304 | bytes 6291456 | tf_op jit(solution)/shard_map/window_backward/pallas_call | solution.py:298
  15.2 1.2 %collective-permute-start.5 = (bf16[4,4,48,512]{3,2,1,0:T(8,128)(2,1)S(1)}, bf16[4,4,48,512]{3,2,1,0:T(8,128)(2,1)S(1)}, u32[]{:S(2)}, u32[]{:S(2)}) collective-permute-start(bf16[4,4,48,512]{3,2,1,0:T(8,128)(2,1)S(1)} %bitcast.36), channel_id=1, source_target_pairs={{0,1},{1,0},{2,3},{3,2},{4,5},{5,4},{6,7},{7,6},{8,9},{9,8},{10,11... | collective-permute-start | bytes 2359304 | tf_op jit(solution)/shard_map/ppermute | solution.py:381
  16.4 0.8 %norm_backward.1 = (bf16[36,512]{1,0:T(8,128)(2,1)S(1)}, bf16[36,512]{1,0:T(8,128)(2,1)S(1)}, bf16[2,36,512]{2,1,0:T(8,128)(2,1)S(1)}) custom-call(bf16[144,1536]{1,0:T(8,128)(2,1)S(1)} %get-tuple-element.33.qkv_ref, bf16[512,1536]{1,0:T(8,128)(2,1)S(1)} %get-tuple-element.28.weight_ref, f32[1,512]{1,0:T(1,128)S(1)} %bitcast.35, ...), custom_call_target="tpu_custom_call" | custom-call | flops 226492416 | bytes 3145728 | tf_op jit(solution)/shard_map/norm_backward/pallas_call | solution.py:341
  17.2 1.1 %collective-permute-done.5 = bf16[4,4,48,512]{3,2,1,0:T(8,128)(2,1)S(1)} collective-permute-done((bf16[4,4,48,512]{3,2,1,0:T(8,128)(2,1)S(1)}, bf16[4,4,48,512]{3,2,1,0:T(8,128)(2,1)S(1)}, u32[]{:S(2)}, u32[]{:S(2)}) %collective-permute-start.5) | collective-permute-done | bytes 786464 | tf_op jit(solution)/shard_map/ppermute | solution.py:381
  18.3 0.2 fusion
  18.6 0.4 collective-permute-start.6
  19.0 2.4 %collective-permute-start.8 = (bf16[4,48,512]{2,1,0:T(8,128)(2,1)S(1)}, bf16[4,48,512]{2,1,0:T(8,128)(2,1)S(1)}, u32[]{:S(2)}, u32[]{:S(2)}) collective-permute-start(bf16[4,48,512]{2,1,0:T(8,128)(2,1)S(1)} %get-tuple-element.45), channel_id=1, source_target_pairs={{0,6},{1,7},{2,4},{3,5},{4,2},{5,3},{6,0},{7,1},{8,14},{9,15},{10,... | collective-permute-start | bytes 589832 | tf_op jit(solution)/shard_map/ppermute | solution.py:381
  21.4 0.8 %collective-permute-start.7 = (bf16[4,48,512]{2,1,0:T(8,128)(2,1)S(1)}, bf16[4,48,512]{2,1,0:T(8,128)(2,1)S(1)}, u32[]{:S(2)}, u32[]{:S(2)}) collective-permute-start(bf16[4,48,512]{2,1,0:T(8,128)(2,1)S(1)} %get-tuple-element.46), channel_id=1, source_target_pairs={{0,2},{1,5},{2,0},{3,7},{4,6},{5,1},{6,4},{7,3},{8,10},{9,13},{10,... | collective-permute-start | bytes 589832 | tf_op jit(solution)/shard_map/ppermute | solution.py:381
  22.2 0.0 collective-permute-start.3
  22.2 7.0 %collective-permute-done.3.side_ref = bf16[2,36,512]{2,1,0:T(8,128)(2,1)S(1)} collective-permute-done((bf16[2,36,512]{2,1,0:T(8,128)(2,1)S(1)}, bf16[2,36,512]{2,1,0:T(8,128)(2,1)S(1)}, u32[]{:S(2)}, u32[]{:S(2)}) %collective-permute-start.3) | collective-permute-done | bytes 73760 | tf_op jit(solution)/shard_map/ppermute | solution.py:453
  29.2 2.6 %collective-permute-start.4 = (bf16[2,36,512]{2,1,0:T(8,128)(2,1)S(1)}, bf16[2,36,512]{2,1,0:T(8,128)(2,1)S(1)}, u32[]{:S(2)}, u32[]{:S(2)}) collective-permute-start(bf16[2,36,512]{2,1,0:T(8,128)(2,1)S(1)} %pad_maximum_fusion), channel_id=1, source_target_pairs={{0,28},{1,29},{2,30},{3,31},{4,0},{5,1},{6,2},{7,3},{8,4},{9,5},{1... | collective-permute-start | bytes 221192 | tf_op jit(solution)/shard_map/ppermute | solution.py:454
  31.8 0.0 collective-permute-done.6
  31.8 0.0 collective-permute-done.8
  31.8 0.0 collective-permute-done.7
  31.8 0.1 fusion.3
  31.9 0.8 %collective-permute-start.9 = (bf16[48,512]{1,0:T(8,128)(2,1)S(1)}, bf16[48,512]{1,0:T(8,128)(2,1)S(1)}, u32[]{:S(2)}, u32[]{:S(2)}) collective-permute-start(bf16[48,512]{1,0:T(8,128)(2,1)S(1)} %get-tuple-element.47), channel_id=1, source_target_pairs={{0,16},{1,17},{2,18},{3,19},{4,20},{5,21},{6,22},{7,23},{8,24},{9,... | collective-permute-start | bytes 147464 | tf_op jit(solution)/shard_map/ppermute | solution.py:381
  32.7 1.3 %collective-permute-start.11 = (bf16[48,512]{1,0:T(8,128)(2,1)S(1)}, bf16[48,512]{1,0:T(8,128)(2,1)S(1)}, u32[]{:S(2)}, u32[]{:S(2)}) collective-permute-start(bf16[48,512]{1,0:T(8,128)(2,1)S(1)} %get-tuple-element.48), channel_id=1, source_target_pairs={{0,24},{1,25},{2,26},{3,27},{4,28},{5,29},{6,30},{7,31},{8,16},{9,... | collective-permute-start | bytes 147464 | tf_op jit(solution)/shard_map/ppermute | solution.py:381
  34.0 1.4 %collective-permute-start.10 = (bf16[48,512]{1,0:T(8,128)(2,1)S(1)}, bf16[48,512]{1,0:T(8,128)(2,1)S(1)}, u32[]{:S(2)}, u32[]{:S(2)}) collective-permute-start(bf16[48,512]{1,0:T(8,128)(2,1)S(1)} %get-tuple-element.49), channel_id=1, source_target_pairs={{0,8},{1,9},{2,10},{3,11},{4,12},{5,13},{6,14},{7,15},{8,0},{9,1},... | collective-permute-start | bytes 147464 | tf_op jit(solution)/shard_map/ppermute | solution.py:381
  35.5 0.0 collective-permute-done.4.lon_ref
  35.5 0.7 %unpack.1 = bf16[12,12,512]{2,1,0:T(8,128)(2,1)} custom-call(bf16[2,36,512]{2,1,0:T(8,128)(2,1)S(1)} %collective-permute-done.4.lon_ref, bf16[2,36,512]{2,1,0:T(8,128)(2,1)S(1)} %collective-permute-done.3.side_ref, bf16[36,512]{1,0:T(8,128)(2,1)S(1)} %get-tuple-element.41.own_ref), custom_call_target="tpu_custom_call" | custom-call | bytes 524288 | tf_op jit(solution)/shard_map/unpack/pallas_call | solution.py:367
  36.2 1.6 %collective-permute-done.9 = bf16[48,512]{1,0:T(8,128)(2,1)S(1)} collective-permute-done((bf16[48,512]{1,0:T(8,128)(2,1)S(1)}, bf16[48,512]{1,0:T(8,128)(2,1)S(1)}, u32[]{:S(2)}, u32[]{:S(2)}) %collective-permute-start.9) | collective-permute-done | bytes 49184 | tf_op jit(solution)/shard_map/ppermute | solution.py:381
  37.8 0.9 %collective-permute-done.11 = bf16[48,512]{1,0:T(8,128)(2,1)S(1)} collective-permute-done((bf16[48,512]{1,0:T(8,128)(2,1)S(1)}, bf16[48,512]{1,0:T(8,128)(2,1)S(1)}, u32[]{:S(2)}, u32[]{:S(2)}) %collective-permute-start.11) | collective-permute-done | bytes 49184 | tf_op jit(solution)/shard_map/ppermute | solution.py:381
  38.7 0.1 collective-permute-done.10
  38.9 0.7 %copy.8 = f32[6,4,8,128]{3,1,2,0:T(4,128)} copy(f32[6,4,8,128]{3,2,1,0:T(8,128)S(1)} %fusion.7) | data formatting | bytes 196608
  (5 shorter events, 0.1 us)
Async XLA Ops:
  0.6 10.8 %copy-start = (f32[512]{0:T(512)S(1)}, f32[512]{0:T(512)}, u32[]{:S(2)}) copy-start(f32[512]{0:T(512)} %param.7) | copy-start | bytes 6148
  1.8 9.2 %collective-permute-start = (bf16[72,512]{1,0:T(8,128)(2,1)S(1)}, bf16[72,512]{1,0:T(8,128)(2,1)S(1)}, u32[]{:S(2)}, u32[]{:S(2)}) collective-permute-start(bf16[72,512]{1,0:T(8,128)(2,1)S(1)} %get-tuple-element.24), channel_id=1, source_target_pairs={{0,4},{1,5},{2,6},{3,7},{4,8},{5,9},{6,10},{7,11},{8,12},{9,13},{1... | collective-permute-start | bytes 221192 | tf_op jit(solution)/shard_map/ppermute | solution.py:409
  4.8 6.6 %collective-permute-start.1 = (bf16[72,512]{1,0:T(8,128)(2,1)S(1)}, bf16[72,512]{1,0:T(8,128)(2,1)S(1)}, u32[]{:S(2)}, u32[]{:S(2)}) collective-permute-start(bf16[72,512]{1,0:T(8,128)(2,1)S(1)} %get-tuple-element.25), channel_id=1, source_target_pairs={{0,7},{1,4},{2,5},{3,6},{4,11},{5,8},{6,9},{7,10},{8,15},{9,12},{1... | collective-permute-start | bytes 221192 | tf_op jit(solution)/shard_map/ppermute | solution.py:410
  6.4 5.0 %collective-permute-start.2 = (bf16[72,512]{1,0:T(8,128)(2,1)S(1)}, bf16[72,512]{1,0:T(8,128)(2,1)S(1)}, u32[]{:S(2)}, u32[]{:S(2)}) collective-permute-start(bf16[72,512]{1,0:T(8,128)(2,1)S(1)} %get-tuple-element.26), channel_id=1, source_target_pairs={{0,3},{1,0},{2,1},{3,2},{4,7},{5,4},{6,5},{7,6},{8,11},{9,8},{10,9... | collective-permute-start | bytes 221192 | tf_op jit(solution)/shard_map/ppermute | solution.py:411
  15.2 3.2 %collective-permute-start.5 = (bf16[4,4,48,512]{3,2,1,0:T(8,128)(2,1)S(1)}, bf16[4,4,48,512]{3,2,1,0:T(8,128)(2,1)S(1)}, u32[]{:S(2)}, u32[]{:S(2)}) collective-permute-start(bf16[4,4,48,512]{3,2,1,0:T(8,128)(2,1)S(1)} %bitcast.36), channel_id=1, source_target_pairs={{0,1},{1,0},{2,3},{3,2},{4,5},{5,4},{6,7},{7,6},{8,9},{9,8},{10,11... | collective-permute-start | bytes 2359304 | tf_op jit(solution)/shard_map/ppermute | solution.py:381
  18.6 13.1 %collective-permute-start.6 = (bf16[4,48,512]{2,1,0:T(8,128)(2,1)S(1)}, bf16[4,48,512]{2,1,0:T(8,128)(2,1)S(1)}, u32[]{:S(2)}, u32[]{:S(2)}) collective-permute-start(bf16[4,48,512]{2,1,0:T(8,128)(2,1)S(1)} %get-tuple-element.44), channel_id=1, source_target_pairs={{0,4},{1,3},{2,6},{3,1},{4,0},{5,7},{6,2},{7,5},{8,12},{9,11},{10,... | collective-permute-start | bytes 589832 | tf_op jit(solution)/shard_map/ppermute | solution.py:381
  19.0 12.8 %collective-permute-start.8 = (bf16[4,48,512]{2,1,0:T(8,128)(2,1)S(1)}, bf16[4,48,512]{2,1,0:T(8,128)(2,1)S(1)}, u32[]{:S(2)}, u32[]{:S(2)}) collective-permute-start(bf16[4,48,512]{2,1,0:T(8,128)(2,1)S(1)} %get-tuple-element.45), channel_id=1, source_target_pairs={{0,6},{1,7},{2,4},{3,5},{4,2},{5,3},{6,0},{7,1},{8,14},{9,15},{10,... | collective-permute-start | bytes 589832 | tf_op jit(solution)/shard_map/ppermute | solution.py:381
  21.4 10.4 %collective-permute-start.7 = (bf16[4,48,512]{2,1,0:T(8,128)(2,1)S(1)}, bf16[4,48,512]{2,1,0:T(8,128)(2,1)S(1)}, u32[]{:S(2)}, u32[]{:S(2)}) collective-permute-start(bf16[4,48,512]{2,1,0:T(8,128)(2,1)S(1)} %get-tuple-element.46), channel_id=1, source_target_pairs={{0,2},{1,5},{2,0},{3,7},{4,6},{5,1},{6,4},{7,3},{8,10},{9,13},{10,... | collective-permute-start | bytes 589832 | tf_op jit(solution)/shard_map/ppermute | solution.py:381
  22.2 7.0 %collective-permute-start.3 = (bf16[2,36,512]{2,1,0:T(8,128)(2,1)S(1)}, bf16[2,36,512]{2,1,0:T(8,128)(2,1)S(1)}, u32[]{:S(2)}, u32[]{:S(2)}) collective-permute-start(bf16[2,36,512]{2,1,0:T(8,128)(2,1)S(1)} %get-tuple-element.40), channel_id=1, source_target_pairs={{0,1},{1,2},{2,3},{3,0},{4,5},{5,6},{6,7},{7,4},{8,9},{9,10},{10,1... | collective-permute-start | bytes 221192 | tf_op jit(solution)/shard_map/ppermute | solution.py:453
  29.2 6.3 %collective-permute-start.4 = (bf16[2,36,512]{2,1,0:T(8,128)(2,1)S(1)}, bf16[2,36,512]{2,1,0:T(8,128)(2,1)S(1)}, u32[]{:S(2)}, u32[]{:S(2)}) collective-permute-start(bf16[2,36,512]{2,1,0:T(8,128)(2,1)S(1)} %pad_maximum_fusion), channel_id=1, source_target_pairs={{0,28},{1,29},{2,30},{3,31},{4,0},{5,1},{6,2},{7,3},{8,4},{9,5},{1... | collective-permute-start | bytes 221192 | tf_op jit(solution)/shard_map/ppermute | solution.py:454
  31.9 5.9 %collective-permute-start.9 = (bf16[48,512]{1,0:T(8,128)(2,1)S(1)}, bf16[48,512]{1,0:T(8,128)(2,1)S(1)}, u32[]{:S(2)}, u32[]{:S(2)}) collective-permute-start(bf16[48,512]{1,0:T(8,128)(2,1)S(1)} %get-tuple-element.47), channel_id=1, source_target_pairs={{0,16},{1,17},{2,18},{3,19},{4,20},{5,21},{6,22},{7,23},{8,24},{9,... | collective-permute-start | bytes 147464 | tf_op jit(solution)/shard_map/ppermute | solution.py:381
  32.7 6.0 %collective-permute-start.11 = (bf16[48,512]{1,0:T(8,128)(2,1)S(1)}, bf16[48,512]{1,0:T(8,128)(2,1)S(1)}, u32[]{:S(2)}, u32[]{:S(2)}) collective-permute-start(bf16[48,512]{1,0:T(8,128)(2,1)S(1)} %get-tuple-element.48), channel_id=1, source_target_pairs={{0,24},{1,25},{2,26},{3,27},{4,28},{5,29},{6,30},{7,31},{8,16},{9,... | collective-permute-start | bytes 147464 | tf_op jit(solution)/shard_map/ppermute | solution.py:381
  34.0 4.8 %collective-permute-start.10 = (bf16[48,512]{1,0:T(8,128)(2,1)S(1)}, bf16[48,512]{1,0:T(8,128)(2,1)S(1)}, u32[]{:S(2)}, u32[]{:S(2)}) collective-permute-start(bf16[48,512]{1,0:T(8,128)(2,1)S(1)} %get-tuple-element.49), channel_id=1, source_target_pairs={{0,8},{1,9},{2,10},{3,11},{4,12},{5,13},{6,14},{7,15},{8,0},{9,1},... | collective-permute-start | bytes 147464 | tf_op jit(solution)/shard_map/ppermute | solution.py:381

commit v6 on v5

--- a/solution.py
+++ b/solution.py
@@ -16,6 +16,7 @@
 LANES = 128
 F32 = jnp.float32
 BF16 = jnp.bfloat16
+ROOM = 8
 AXES = ("lon", "lat")
 PLANE = (0, 2, 1, 3)
 
@@ -48,7 +49,7 @@
             stage_ref[2 if early else 3, row : row + EDGE, :] = line[:EDGE]
             stage_ref[0 if early else 1, row : row + EDGE, :] = line[EDGE:]
     for n, out in enumerate((own_ref, lon_ref, lat_ref, diag_ref)):
-        out[...] = stage_ref[n].astype(BF16)
+        out[...] = stage_ref[n, : 2 * QUARTER, :].astype(BF16)
     copies[2].wait()
 
 
@@ -64,7 +65,7 @@
         out_specs=(vmem,) * 5,
         scratch_shapes=[
             pltpu.VMEM((2,) + tokens.shape, BF16),
-            pltpu.VMEM((4, 2 * QUARTER, width), F32),
+            pltpu.VMEM((4, 2 * QUARTER + ROOM, width), F32),
             pltpu.SemaphoreType.DMA((3,)),
         ],
         compiler_params=pltpu.CompilerParams(vmem_limit_bytes=8 << 20),
@@ -179,7 +180,7 @@
         both = ref[...].astype(F32)
         token_ref[QUARTER * k : QUARTER * (k + 1), :] = both[:QUARTER]
         grad_ref[QUARTER * k : QUARTER * (k + 1), :] = both[QUARTER:]
-    inputs = token_ref[...]
+    inputs = token_ref[:AREA, :]
     gain = gain_ref[...]
     centred = inputs - jnp.mean(inputs, axis=-1, keepdims=True)
     inverse = lax.rsqrt(jnp.mean(centred * centred, axis=-1, keepdims=True) + 1e-05)
@@ -188,7 +189,7 @@
     inverse_ref[...] = jnp.broadcast_to(inverse, inverse_ref.shape)
     normed = (unit * gain).astype(BF16)
     qkv_ref[...] = dot(normed, weight_ref[...], 1, 0).astype(BF16)
-    upstream = dot(grad_ref[...].astype(BF16), proj_ref[...], 1, 1).astype(BF16)
+    upstream = dot(grad_ref[:AREA, :].astype(BF16), proj_ref[...], 1, 1).astype(BF16)
     lane = lax.broadcasted_iota(jnp.int32, (AREA, LANES), 1)
     zero = jnp.zeros((AREA, LANES), BF16)
     here = [(lane >= size * n) & (lane < size * (n + 1)) for n in range(group)]
@@ -276,16 +277,18 @@
     if blocks is None:
         weight_outs[0][...] = dot(turned_ref[...], normed, 1, 0)
     else:
+        send_ref, kept_ref, normed_ref = weight_outs
         rows = 3 * width // len(blocks)
+        half = 3 * width // 2
         place = order_ref[0]
         odd = place % 2 == 1
         for slot, (even_offset, odd_offset) in enumerate(blocks):
             offset = jnp.where(odd, odd_offset, even_offset)
             start = pl.multiple_of((place ^ offset) * rows, rows)
-            placed_ref[slot * rows : (slot + 1) * rows, :] = turned_ref[pl.ds(start, rows), :]
-        total = 3 * width // len(weight_outs)
-        for k, ref in enumerate(weight_outs):
-            ref[...] = dot(placed_ref[total * k : total * (k + 1), :], normed, 1, 0).astype(BF16)
+            target, first = (kept_ref, slot * rows) if slot * rows < half else (placed_ref, slot * rows - half)
+            target[first : first + rows, :] = turned_ref[pl.ds(start, rows), :]
+        send_ref[...] = dot(placed_ref[...], normed, 1, 0).astype(BF16)
+        normed_ref[...] = normed
 
 
 def window_backward(order, quarters, gain, weight, proj, low, high, blocks):
@@ -293,7 +296,11 @@
     if blocks is None:
         weight_shapes = (jax.ShapeDtypeStruct((3 * width, width), F32),)
     else:
-        weight_shapes = (jax.ShapeDtypeStruct((3 * width // 2, width), BF16),) * 2
+        weight_shapes = (
+            jax.ShapeDtypeStruct((3 * width // 2, width), BF16),
+            jax.ShapeDtypeStruct((3 * width // 2, AREA), BF16),
+            jax.ShapeDtypeStruct((AREA, width), BF16),
+        )
     vmem = pl.BlockSpec(memory_space=pltpu.VMEM)
     return pl.pallas_call(
         functools.partial(window_kernel, blocks),
@@ -301,15 +308,15 @@
             jax.ShapeDtypeStruct((AREA, 3 * width), BF16),
             jax.ShapeDtypeStruct((AREA, width), F32),
             jax.ShapeDtypeStruct((AREA, LANES), F32),
-            jax.ShapeDtypeStruct((AREA, width), F32),
+            jax.ShapeDtypeStruct((AREA + ROOM, width), F32),
         )
         + weight_shapes,
         in_specs=[pl.BlockSpec(memory_space=pltpu.SMEM)] + [vmem] * 9,
         out_specs=(vmem,) * (4 + len(weight_shapes)),
         scratch_shapes=[
-            pltpu.VMEM((AREA, width), F32),
+            pltpu.VMEM((AREA + ROOM, width), F32),
             pltpu.VMEM((3 * width, AREA), BF16),
-            pltpu.VMEM((3 * width, AREA), BF16),
+            pltpu.VMEM((3 * width // 2, AREA), BF16),
         ],
         compiler_params=pltpu.CompilerParams(vmem_limit_bytes=32 << 20),
         cost_estimate=pl.CostEstimate(
@@ -320,36 +327,42 @@
 
 
 def norm_kernel(
-    qkv_ref, weight_ref, gain_ref, unit_ref, inverse_ref, grad_ref, own_out, lon_out, side_out, token_ref
+    qkv_ref, weight_ref, gain_ref, unit_ref, inverse_ref, grad_ref, *rest
 ):
+    if len(rest) > 4:
+        kept_ref, normed_ref, *rest = rest
+        keep_out = rest.pop(3)
+        keep_out[...] = dot(kept_ref[...], normed_ref[...], 1, 0).astype(BF16)
+    own_out, lon_out, side_out, token_ref = rest
     unit = unit_ref[...]
     scaled = dot(qkv_ref[...], weight_ref[...], 1, 1) * gain_ref[...]
-    result = grad_ref[...] + inverse_ref[:, :1] * (
+    result = grad_ref[:AREA, :] + inverse_ref[:, :1] * (
         scaled
         - jnp.mean(scaled, axis=-1, keepdims=True)
         - unit * jnp.mean(scaled * unit, axis=-1, keepdims=True)
     )
-    token_ref[...] = result
+    token_ref[:AREA, :] = result
     for k, ref in enumerate((lon_out, own_out, side_out.at[1], side_out.at[0])):
         ref[...] = token_ref[QUARTER * k : QUARTER * (k + 1), :].astype(BF16)
 
 
-def norm_backward(qkv, weight, gain, unit, inverse, grad):
+def norm_backward(qkv, weight, gain, unit, inverse, grad, kept):
     width = unit.shape[1]
     piece = jax.ShapeDtypeStruct((QUARTER, width), BF16)
+    keep = (jax.ShapeDtypeStruct((3 * width // 2, width), BF16),) if kept else ()
     vmem = pl.BlockSpec(memory_space=pltpu.VMEM)
     return pl.pallas_call(
         norm_kernel,
-        out_shape=(piece, piece, jax.ShapeDtypeStruct((2, QUARTER, width), BF16)),
-        in_specs=[vmem] * 6,
-        out_specs=(vmem,) * 3,
-        scratch_shapes=[pltpu.VMEM((AREA, width), F32)],
+        out_shape=(piece, piece, jax.ShapeDtypeStruct((2, QUARTER, width), BF16)) + keep,
+        in_specs=[vmem] * (6 + len(kept)),
+        out_specs=(vmem,) * (3 + len(keep)),
+        scratch_shapes=[pltpu.VMEM((AREA + ROOM, width), F32)],
         compiler_params=pltpu.CompilerParams(vmem_limit_bytes=16 << 20),
         cost_estimate=pl.CostEstimate(
             flops=6 * AREA * width * width, bytes_accessed=3 << 20, transcendentals=0
         ),
         name="norm_backward",
-    )(qkv, weight, gain, unit, inverse, grad)
+    )(qkv, weight, gain, unit, inverse, grad, *kept)
 
 
 def unpack_kernel(lon_ref, side_ref, own_ref, out_ref, line_ref):
@@ -357,8 +370,8 @@
         left, right = (side_ref[0], own_ref[...]) if u < EDGE else (lon_ref[1], lon_ref[0])
         rows = slice(u % EDGE * EDGE, u % EDGE * EDGE + EDGE)
         line_ref[u, :EDGE, :] = left.astype(F32)[rows]
-        line_ref[u, EDGE:, :] = right.astype(F32)[rows]
-    out_ref[...] = line_ref[...].astype(BF16)
+        line_ref[u, EDGE:WIN, :] = right.astype(F32)[rows]
+    out_ref[...] = line_ref[:, :WIN, :].astype(BF16)
 
 
 def unpack(lon, side, own):
@@ -369,7 +382,7 @@
         out_shape=jax.ShapeDtypeStruct((WIN, WIN, width), BF16),
         in_specs=[vmem] * 3,
         out_specs=vmem,
-        scratch_shapes=[pltpu.VMEM((WIN, WIN, width), F32)],
+        scratch_shapes=[pltpu.VMEM((WIN, 2 * ROOM, width), F32)],
         compiler_params=pltpu.CompilerParams(vmem_limit_bytes=8 << 20),
         cost_estimate=pl.CostEstimate(flops=0, bytes_accessed=1 << 19, transcendentals=0),
         name="unpack",
@@ -435,11 +448,12 @@
         high,
         blocks,
     )
-    own, to_lon, to_side = norm_backward(grad_qkv, weight, gain, unit, inverse, grad)
+    own, to_lon, to_side, *keep = norm_backward(
+        grad_qkv, weight, gain, unit, inverse, grad, weight_grads[1:]
+    )
     factor = 1.0 / math.sqrt(span_lon * lons * span_lat * lats)
     if staged:
-        keep, send = weight_grads
-        keep, to_lon, to_side = lax.optimization_barrier((keep, to_lon, to_side))
+        send, keep = weight_grads[0], keep[0]
         shape = (4, far, rows, width)
         pair = add_slots(keep.reshape(shape), [exchange(send.reshape(shape), 1, 1, total)]).astype(BF16)
         planes = [(2 * PLANE[k], 2 * k) for k in range(1, 4)]

time: 39.7 us -> 39.5 us (level)
  transfers between devices with their start and end apart: 12 -> 12, of which waited for: 6 -> 6; matrix products, arithmetic and copies ran while one was open for 0% -> 0% of each run, Pallas kernels for 12% -> 13%
where the time goes in v6:
time: 39.5 us; the launch traced here: 39.3 us
  starting transfers between devices  16.7 us (42%)
  waiting for transfers between devices  11 us (28%)
  Pallas kernels  9.76 us (25%)
  local copies, waits for them, and re-layouts  0.73 us (2%)
  between operations  0.73 us (2%)
    ppermute x7, starting transfers between devices, exchange(): return lax.ppermute(block, AXES, pairs)  8.36 us
    ppermute x1, waiting for transfers between devices, shards(): from_side = lax.ppermute(to_side, AXES, route(0, 1))  7 us
    ppermute x7, waiting for transfers between devices, exchange(): return lax.ppermute(block, AXES, pairs)  3.6 us
    pallas_call x1, Pallas kernels, window_backward(): pl.pallas_call(functools.partial(window_kernel, blocks), out_shape=(jax.S...  3.58 us
    pallas_call x1, Pallas kernels, relative_bias(): pl.pallas_call(bias_kernel, out_shape=(shape, shape, jax.ShapeDtypeStruct...  3.38 us
    ppermute x1, starting transfers between devices, shards(): at_lon = lax.ppermute(lon_start, AXES, route(1, 0))  2.99 us
    ppermute x1, starting transfers between devices, shards(): lax.ppermute(jnp.stack([to_lon, from_side[1]]), AXES, route(-1, 0))  2.57 us
    ppermute x1, starting transfers between devices, shards(): at_diag = lax.ppermute(diag_start, AXES, route(1, -1))  1.66 us
  transfers between devices with their start and end apart: 12, of which 6 were waited for; matrix products, arithmetic and copies ran while one was open for 0% of the time, Pallas kernels for 13%

profile of v6, /device:TPU:0, one launch (start us, length us, event | category | flops | bytes accessed | tf_op | source)
XLA Modules:
  0.0 39.3 jit_solution(2111236060586112552)
XLA Ops:
  0.6 0.0 copy-start
  0.6 1.1 %pack.1 = (bf16[72,512]{1,0:T(8,128)(2,1)S(1)}, bf16[72,512]{1,0:T(8,128)(2,1)S(1)}, bf16[72,512]{1,0:T(8,128)(2,1)S(1)}, bf16[72,512]{1,0:T(8,128)(2,1)S(1)}, f32[16,529]{1,0:T(8,128)S(1)}) custom-call(bf16[12,12,512]{2,1,0:T(8,128)(2,1)} %tokens_hbm.1, bf16[12,12,512]{2,1,0:T(8,128)(2,1)} %grad_hbm.1, f32[16,529]{1,0:T(8,128)} %table_hbm.1), custom_call_target="tpu_custom_call" | custom-call | bytes 1048576 | tf_op jit(solution)/shard_map/pack/pallas_call | solution.py:61
  1.8 3.0 %collective-permute-start = (bf16[72,512]{1,0:T(8,128)(2,1)S(1)}, bf16[72,512]{1,0:T(8,128)(2,1)S(1)}, u32[]{:S(2)}, u32[]{:S(2)}) collective-permute-start(bf16[72,512]{1,0:T(8,128)(2,1)S(1)} %get-tuple-element.23), channel_id=1, source_target_pairs={{0,4},{1,5},{2,6},{3,7},{4,8},{5,9},{6,10},{7,11},{8,12},{9,13},{1... | collective-permute-start | bytes 221192 | tf_op jit(solution)/shard_map/ppermute | solution.py:422
  4.8 1.7 %collective-permute-start.1 = (bf16[72,512]{1,0:T(8,128)(2,1)S(1)}, bf16[72,512]{1,0:T(8,128)(2,1)S(1)}, u32[]{:S(2)}, u32[]{:S(2)}) collective-permute-start(bf16[72,512]{1,0:T(8,128)(2,1)S(1)} %get-tuple-element.24), channel_id=1, source_target_pairs={{0,7},{1,4},{2,5},{3,6},{4,11},{5,8},{6,9},{7,10},{8,15},{9,12},{1... | collective-permute-start | bytes 221192 | tf_op jit(solution)/shard_map/ppermute | solution.py:423
  6.4 1.1 %collective-permute-start.2 = (bf16[72,512]{1,0:T(8,128)(2,1)S(1)}, bf16[72,512]{1,0:T(8,128)(2,1)S(1)}, u32[]{:S(2)}, u32[]{:S(2)}) collective-permute-start(bf16[72,512]{1,0:T(8,128)(2,1)S(1)} %get-tuple-element.25), channel_id=1, source_target_pairs={{0,3},{1,0},{2,1},{3,2},{4,7},{5,4},{6,5},{7,6},{8,11},{9,8},{10,9... | collective-permute-start | bytes 221192 | tf_op jit(solution)/shard_map/ppermute | solution.py:424
  7.6 3.4 %relative_bias.1 = (f32[2304,128]{1,0:T(8,128)S(1)}, f32[2304,128]{1,0:T(8,128)S(1)}, bf16[512,1536]{1,0:T(8,128)(2,1)S(1)}, bf16[512,512]{1,0:T(8,128)(2,1)S(1)}) custom-call(s32[1]{0:T(128)} %bitcast.2.flag_ref, f32[16,529]{1,0:T(8,128)S(1)} %get-tuple-element.26.table_ref, bf16[512,1536]{1,0:T(8,128)(2,1)} %weight_hbm.1, bf16[512,512]{1,0:T(8,128)(2,1)} %proj_hbm.1), custom_call_target="tpu_custom_call" | custom-call | flops 283115520 | bytes 6291456 | tf_op jit(solution)/shard_map/relative_bias/pallas_call | solution.py:135
  10.9 0.0 collective-permute-done.lon_ref
  11.0 0.4 %collective-permute-done.1.diag_ref = bf16[72,512]{1,0:T(8,128)(2,1)S(1)} collective-permute-done((bf16[72,512]{1,0:T(8,128)(2,1)S(1)}, bf16[72,512]{1,0:T(8,128)(2,1)S(1)}, u32[]{:S(2)}, u32[]{:S(2)}) %collective-permute-start.1) | collective-permute-done | bytes 73760 | tf_op jit(solution)/shard_map/ppermute | solution.py:423
  11.4 0.0 collective-permute-done.2.lat_ref
  11.4 0.0 copy-done
  11.4 3.6 %window_backward.1 = (bf16[144,1536]{1,0:T(8,128)(2,1)S(1)}, f32[144,512]{1,0:T(8,128)S(1)}, f32[144,128]{1,0:T(8,128)S(1)}, f32[152,512]{1,0:T(8,128)S(1)}, bf1...) custom-call(s32[1]{0:T(128)} %bitcast.order_ref, ...), custom_call_target="tpu_custom_call" | custom-call | flops 528482304 | bytes 6291456 | tf_op jit(solution)/shard_map/window_backward/pallas_call | solution.py:305
  15.0 1.3 %collective-permute-start.5 = (bf16[4,4,48,512]{3,2,1,0:T(8,128)(2,1)S(1)}, bf16[4,4,48,512]{3,2,1,0:T(8,128)(2,1)S(1)}, u32[]{:S(2)}, u32[]{:S(2)}) collective-permute-start(bf16[4,4,48,512]{3,2,1,0:T(8,128)(2,1)S(1)} %bitcast.36), channel_id=1, source_target_pairs={{0,1},{1,0},{2,3},{3,2},{4,5},{5,4},{6,7},{7,6},{8,9},{9,8},{10,11... | collective-permute-start | bytes 2359304 | tf_op jit(solution)/shard_map/ppermute | solution.py:394
  16.2 0.9 %norm_backward.1 = (bf16[36,512]{1,0:T(8,128)(2,1)S(1)}, bf16[36,512]{1,0:T(8,128)(2,1)S(1)}, bf16[2,36,512]{2,1,0:T(8,128)(2,1)S(1)}, bf16[768,512]{1,0:T(8,128)(2,1)S(1)}) custom-call(bf16[144,1536]{1,0:T(8,128)(2,1)S(1)} %get-tuple-element.31.qkv_ref, bf16[512,1536]{1,0:T(8,128)(2,1)S(1)} %get-tuple-element.27.weight_ref, f32[1,512]{1,0:T(1,128)S(1)} %bitcast.35, ...), custom_call_target="tpu_custom_call" | custom-call | flops 226492416 | bytes 3145728 | tf_op jit(solution)/shard_map/norm_backward/pallas_call | solution.py:354
  17.2 1.0 %collective-permute-done.5 = bf16[4,4,48,512]{3,2,1,0:T(8,128)(2,1)S(1)} collective-permute-done((bf16[4,4,48,512]{3,2,1,0:T(8,128)(2,1)S(1)}, bf16[4,4,48,512]{3,2,1,0:T(8,128)(2,1)S(1)}, u32[]{:S(2)}, u32[]{:S(2)}) %collective-permute-start.5) | collective-permute-done | bytes 786464 | tf_op jit(solution)/shard_map/ppermute | solution.py:394
  18.1 0.2 fusion
  18.4 0.4 collective-permute-start.6
  18.8 2.4 %collective-permute-start.8 = (bf16[4,48,512]{2,1,0:T(8,128)(2,1)S(1)}, bf16[4,48,512]{2,1,0:T(8,128)(2,1)S(1)}, u32[]{:S(2)}, u32[]{:S(2)}) collective-permute-start(bf16[4,48,512]{2,1,0:T(8,128)(2,1)S(1)} %get-tuple-element.43), channel_id=1, source_target_pairs={{0,6},{1,7},{2,4},{3,5},{4,2},{5,3},{6,0},{7,1},{8,14},{9,15},{10,... | collective-permute-start | bytes 589832 | tf_op jit(solution)/shard_map/ppermute | solution.py:394
  21.2 0.8 %collective-permute-start.7 = (bf16[4,48,512]{2,1,0:T(8,128)(2,1)S(1)}, bf16[4,48,512]{2,1,0:T(8,128)(2,1)S(1)}, u32[]{:S(2)}, u32[]{:S(2)}) collective-permute-start(bf16[4,48,512]{2,1,0:T(8,128)(2,1)S(1)} %get-tuple-element.44), channel_id=1, source_target_pairs={{0,2},{1,5},{2,0},{3,7},{4,6},{5,1},{6,4},{7,3},{8,10},{9,13},{10,... | collective-permute-start | bytes 589832 | tf_op jit(solution)/shard_map/ppermute | solution.py:394
  22.0 0.0 collective-permute-start.3
  22.0 7.0 %collective-permute-done.3.side_ref = bf16[2,36,512]{2,1,0:T(8,128)(2,1)S(1)} collective-permute-done((bf16[2,36,512]{2,1,0:T(8,128)(2,1)S(1)}, bf16[2,36,512]{2,1,0:T(8,128)(2,1)S(1)}, u32[]{:S(2)}, u32[]{:S(2)}) %collective-permute-start.3) | collective-permute-done | bytes 73760 | tf_op jit(solution)/shard_map/ppermute | solution.py:467
  29.0 2.6 %collective-permute-start.4 = (bf16[2,36,512]{2,1,0:T(8,128)(2,1)S(1)}, bf16[2,36,512]{2,1,0:T(8,128)(2,1)S(1)}, u32[]{:S(2)}, u32[]{:S(2)}) collective-permute-start(bf16[2,36,512]{2,1,0:T(8,128)(2,1)S(1)} %pad_maximum_fusion), channel_id=1, source_target_pairs={{0,28},{1,29},{2,30},{3,31},{4,0},{5,1},{6,2},{7,3},{8,4},{9,5},{1... | collective-permute-start | bytes 221192 | tf_op jit(solution)/shard_map/ppermute | solution.py:468
  31.6 0.0 collective-permute-done.6
  31.6 0.0 collective-permute-done.8
  31.6 0.0 collective-permute-done.7
  31.6 0.1 fusion.3
  31.7 0.8 %collective-permute-start.9 = (bf16[48,512]{1,0:T(8,128)(2,1)S(1)}, bf16[48,512]{1,0:T(8,128)(2,1)S(1)}, u32[]{:S(2)}, u32[]{:S(2)}) collective-permute-start(bf16[48,512]{1,0:T(8,128)(2,1)S(1)} %get-tuple-element.45), channel_id=1, source_target_pairs={{0,16},{1,17},{2,18},{3,19},{4,20},{5,21},{6,22},{7,23},{8,24},{9,... | collective-permute-start | bytes 147464 | tf_op jit(solution)/shard_map/ppermute | solution.py:394
  32.5 1.4 %collective-permute-start.11 = (bf16[48,512]{1,0:T(8,128)(2,1)S(1)}, bf16[48,512]{1,0:T(8,128)(2,1)S(1)}, u32[]{:S(2)}, u32[]{:S(2)}) collective-permute-start(bf16[48,512]{1,0:T(8,128)(2,1)S(1)} %get-tuple-element.46), channel_id=1, source_target_pairs={{0,24},{1,25},{2,26},{3,27},{4,28},{5,29},{6,30},{7,31},{8,16},{9,... | collective-permute-start | bytes 147464 | tf_op jit(solution)/shard_map/ppermute | solution.py:394
  33.8 1.4 %collective-permute-start.10 = (bf16[48,512]{1,0:T(8,128)(2,1)S(1)}, bf16[48,512]{1,0:T(8,128)(2,1)S(1)}, u32[]{:S(2)}, u32[]{:S(2)}) collective-permute-start(bf16[48,512]{1,0:T(8,128)(2,1)S(1)} %get-tuple-element.47), channel_id=1, source_target_pairs={{0,8},{1,9},{2,10},{3,11},{4,12},{5,13},{6,14},{7,15},{8,0},{9,1},... | collective-permute-start | bytes 147464 | tf_op jit(solution)/shard_map/ppermute | solution.py:394
  35.3 0.0 collective-permute-done.4.lon_ref
  35.3 0.7 %unpack.1 = bf16[12,12,512]{2,1,0:T(8,128)(2,1)} custom-call(bf16[2,36,512]{2,1,0:T(8,128)(2,1)S(1)} %collective-permute-done.4.lon_ref, bf16[2,36,512]{2,1,0:T(8,128)(2,1)S(1)} %collective-permute-done.3.side_ref, bf16[36,512]{1,0:T(8,128)(2,1)S(1)} %get-tuple-element.39.own_ref), custom_call_target="tpu_custom_call" | custom-call | bytes 524288 | tf_op jit(solution)/shard_map/unpack/pallas_call | solution.py:380
  36.0 1.6 %collective-permute-done.9 = bf16[48,512]{1,0:T(8,128)(2,1)S(1)} collective-permute-done((bf16[48,512]{1,0:T(8,128)(2,1)S(1)}, bf16[48,512]{1,0:T(8,128)(2,1)S(1)}, u32[]{:S(2)}, u32[]{:S(2)}) %collective-permute-start.9) | collective-permute-done | bytes 49184 | tf_op jit(solution)/shard_map/ppermute | solution.py:394
  37.6 0.9 %collective-permute-done.11 = bf16[48,512]{1,0:T(8,128)(2,1)S(1)} collective-permute-done((bf16[48,512]{1,0:T(8,128)(2,1)S(1)}, bf16[48,512]{1,0:T(8,128)(2,1)S(1)}, u32[]{:S(2)}, u32[]{:S(2)}) %collective-permute-start.11) | collective-permute-done | bytes 49184 | tf_op jit(solution)/shard_map/ppermute | solution.py:394
  38.5 0.1 collective-permute-done.10
  38.7 0.7 %copy.8 = f32[6,4,8,128]{3,1,2,0:T(4,128)} copy(f32[6,4,8,128]{3,2,1,0:T(8,128)S(1)} %fusion.7) | data formatting | bytes 196608
  (5 shorter events, 0.1 us)
Async XLA Ops:
  0.6 10.8 %copy-start = (f32[512]{0:T(512)S(1)}, f32[512]{0:T(512)}, u32[]{:S(2)}) copy-start(f32[512]{0:T(512)} %param.7) | copy-start | bytes 6148
  1.8 9.2 %collective-permute-start = (bf16[72,512]{1,0:T(8,128)(2,1)S(1)}, bf16[72,512]{1,0:T(8,128)(2,1)S(1)}, u32[]{:S(2)}, u32[]{:S(2)}) collective-permute-start(bf16[72,512]{1,0:T(8,128)(2,1)S(1)} %get-tuple-element.23), channel_id=1, source_target_pairs={{0,4},{1,5},{2,6},{3,7},{4,8},{5,9},{6,10},{7,11},{8,12},{9,13},{1... | collective-permute-start | bytes 221192 | tf_op jit(solution)/shard_map/ppermute | solution.py:422
  4.8 6.6 %collective-permute-start.1 = (bf16[72,512]{1,0:T(8,128)(2,1)S(1)}, bf16[72,512]{1,0:T(8,128)(2,1)S(1)}, u32[]{:S(2)}, u32[]{:S(2)}) collective-permute-start(bf16[72,512]{1,0:T(8,128)(2,1)S(1)} %get-tuple-element.24), channel_id=1, source_target_pairs={{0,7},{1,4},{2,5},{3,6},{4,11},{5,8},{6,9},{7,10},{8,15},{9,12},{1... | collective-permute-start | bytes 221192 | tf_op jit(solution)/shard_map/ppermute | solution.py:423
  6.4 5.0 %collective-permute-start.2 = (bf16[72,512]{1,0:T(8,128)(2,1)S(1)}, bf16[72,512]{1,0:T(8,128)(2,1)S(1)}, u32[]{:S(2)}, u32[]{:S(2)}) collective-permute-start(bf16[72,512]{1,0:T(8,128)(2,1)S(1)} %get-tuple-element.25), channel_id=1, source_target_pairs={{0,3},{1,0},{2,1},{3,2},{4,7},{5,4},{6,5},{7,6},{8,11},{9,8},{10,9... | collective-permute-start | bytes 221192 | tf_op jit(solution)/shard_map/ppermute | solution.py:424
  15.0 3.2 %collective-permute-start.5 = (bf16[4,4,48,512]{3,2,1,0:T(8,128)(2,1)S(1)}, bf16[4,4,48,512]{3,2,1,0:T(8,128)(2,1)S(1)}, u32[]{:S(2)}, u32[]{:S(2)}) collective-permute-start(bf16[4,4,48,512]{3,2,1,0:T(8,128)(2,1)S(1)} %bitcast.36), channel_id=1, source_target_pairs={{0,1},{1,0},{2,3},{3,2},{4,5},{5,4},{6,7},{7,6},{8,9},{9,8},{10,11... | collective-permute-start | bytes 2359304 | tf_op jit(solution)/shard_map/ppermute | solution.py:394
  18.4 13.2 %collective-permute-start.6 = (bf16[4,48,512]{2,1,0:T(8,128)(2,1)S(1)}, bf16[4,48,512]{2,1,0:T(8,128)(2,1)S(1)}, u32[]{:S(2)}, u32[]{:S(2)}) collective-permute-start(bf16[4,48,512]{2,1,0:T(8,128)(2,1)S(1)} %get-tuple-element.42), channel_id=1, source_target_pairs={{0,4},{1,3},{2,6},{3,1},{4,0},{5,7},{6,2},{7,5},{8,12},{9,11},{10,... | collective-permute-start | bytes 589832 | tf_op jit(solution)/shard_map/ppermute | solution.py:394
  18.8 12.8 %collective-permute-start.8 = (bf16[4,48,512]{2,1,0:T(8,128)(2,1)S(1)}, bf16[4,48,512]{2,1,0:T(8,128)(2,1)S(1)}, u32[]{:S(2)}, u32[]{:S(2)}) collective-permute-start(bf16[4,48,512]{2,1,0:T(8,128)(2,1)S(1)} %get-tuple-element.43), channel_id=1, source_target_pairs={{0,6},{1,7},{2,4},{3,5},{4,2},{5,3},{6,0},{7,1},{8,14},{9,15},{10,... | collective-permute-start | bytes 589832 | tf_op jit(solution)/shard_map/ppermute | solution.py:394
  21.2 10.4 %collective-permute-start.7 = (bf16[4,48,512]{2,1,0:T(8,128)(2,1)S(1)}, bf16[4,48,512]{2,1,0:T(8,128)(2,1)S(1)}, u32[]{:S(2)}, u32[]{:S(2)}) collective-permute-start(bf16[4,48,512]{2,1,0:T(8,128)(2,1)S(1)} %get-tuple-element.44), channel_id=1, source_target_pairs={{0,2},{1,5},{2,0},{3,7},{4,6},{5,1},{6,4},{7,3},{8,10},{9,13},{10,... | collective-permute-start | bytes 589832 | tf_op jit(solution)/shard_map/ppermute | solution.py:394
  22.0 7.0 %collective-permute-start.3 = (bf16[2,36,512]{2,1,0:T(8,128)(2,1)S(1)}, bf16[2,36,512]{2,1,0:T(8,128)(2,1)S(1)}, u32[]{:S(2)}, u32[]{:S(2)}) collective-permute-start(bf16[2,36,512]{2,1,0:T(8,128)(2,1)S(1)} %get-tuple-element.38), channel_id=1, source_target_pairs={{0,1},{1,2},{2,3},{3,0},{4,5},{5,6},{6,7},{7,4},{8,9},{9,10},{10,1... | collective-permute-start | bytes 221192 | tf_op jit(solution)/shard_map/ppermute | solution.py:467
  29.0 6.3 %collective-permute-start.4 = (bf16[2,36,512]{2,1,0:T(8,128)(2,1)S(1)}, bf16[2,36,512]{2,1,0:T(8,128)(2,1)S(1)}, u32[]{:S(2)}, u32[]{:S(2)}) collective-permute-start(bf16[2,36,512]{2,1,0:T(8,128)(2,1)S(1)} %pad_maximum_fusion), channel_id=1, source_target_pairs={{0,28},{1,29},{2,30},{3,31},{4,0},{5,1},{6,2},{7,3},{8,4},{9,5},{1... | collective-permute-start | bytes 221192 | tf_op jit(solution)/shard_map/ppermute | solution.py:468
  31.7 5.9 %collective-permute-start.9 = (bf16[48,512]{1,0:T(8,128)(2,1)S(1)}, bf16[48,512]{1,0:T(8,128)(2,1)S(1)}, u32[]{:S(2)}, u32[]{:S(2)}) collective-permute-start(bf16[48,512]{1,0:T(8,128)(2,1)S(1)} %get-tuple-element.45), channel_id=1, source_target_pairs={{0,16},{1,17},{2,18},{3,19},{4,20},{5,21},{6,22},{7,23},{8,24},{9,... | collective-permute-start | bytes 147464 | tf_op jit(solution)/shard_map/ppermute | solution.py:394
  32.5 6.0 %collective-permute-start.11 = (bf16[48,512]{1,0:T(8,128)(2,1)S(1)}, bf16[48,512]{1,0:T(8,128)(2,1)S(1)}, u32[]{:S(2)}, u32[]{:S(2)}) collective-permute-start(bf16[48,512]{1,0:T(8,128)(2,1)S(1)} %get-tuple-element.46), channel_id=1, source_target_pairs={{0,24},{1,25},{2,26},{3,27},{4,28},{5,29},{6,30},{7,31},{8,16},{9,... | collective-permute-start | bytes 147464 | tf_op jit(solution)/shard_map/ppermute | solution.py:394
  33.8 4.8 %collective-permute-start.10 = (bf16[48,512]{1,0:T(8,128)(2,1)S(1)}, bf16[48,512]{1,0:T(8,128)(2,1)S(1)}, u32[]{:S(2)}, u32[]{:S(2)}) collective-permute-start(bf16[48,512]{1,0:T(8,128)(2,1)S(1)} %get-tuple-element.47), channel_id=1, source_target_pairs={{0,8},{1,9},{2,10},{3,11},{4,12},{5,13},{6,14},{7,15},{8,0},{9,1},... | collective-permute-start | bytes 147464 | tf_op jit(solution)/shard_map/ppermute | solution.py:394

commit v7 on v6

--- a/solution.py
+++ b/solution.py
@@ -155,8 +155,8 @@
     blocks,
     order_ref,
     own_ref,
+    diag_ref,
     lon_ref,
-    diag_ref,
     lat_ref,
     gain_ref,
     weight_ref,
@@ -422,7 +422,7 @@
     at_lon = lax.ppermute(lon_start, AXES, route(1, 0))
     at_diag = lax.ppermute(diag_start, AXES, route(1, -1))
     at_lat = lax.ppermute(lat_start, AXES, route(0, -1))
-    quarters = [own, at_lon, at_diag, at_lat]
+    quarters = [own, at_diag, at_lon, at_lat]
     flag = (lax.axis_index("lat") == lats - 1).astype(jnp.int32).reshape(1)
     low, high, weight, proj = relative_bias(flag, table, qkv_weight, proj_weight)
     rows = 3 * width // total

time: 39.5 us -> 39.2 us (level)
  starting transfers between devices: 16.7 us -> 14.4 us
  waiting for transfers between devices: 11 us -> 13.1 us
    ppermute x1, starting transfers between devices: 1.66 us -> 3.39 us  [shards(): at_diag = lax.ppermute(diag_start, AXES, route(1, -1))]
    ppermute x1, waiting for transfers between devices: 0.01 us -> 1.62 us  [shards(): at_lon = lax.ppermute(lon_start, AXES, route(1, 0))]
    ppermute x1, starting transfers between devices: 2.99 us -> 1.55 us  [shards(): at_lon = lax.ppermute(lon_start, AXES, route(1, 0))]
    ppermute x7, starting transfers between devices: 8.36 us -> 7.17 us  [exchange(): return lax.ppermute(block, AXES, pairs)]
    ppermute x1, starting transfers between devices: 2.57 us -> 1.69 us  [shards(): lax.ppermute(jnp.stack([to_lon, from_side[1]]), AXES, route(-1, 0))]
    ppermute x7, waiting for transfers between devices: 3.6 us -> 4.47 us  [exchange(): return lax.ppermute(block, AXES, pairs)]
    ppermute x1, starting transfers between devices: 1.12 us -> 0.56 us  [shards(): at_lat = lax.ppermute(lat_start, AXES, route(0, -1))]
    ppermute x1, waiting for transfers between devices: 0.43 us -> 0.01 us  [shards(): at_diag = lax.ppermute(diag_start, AXES, route(1, -1))]
  transfers between devices with their start and end apart: 12 -> 12, of which waited for: 6 -> 8; matrix products, arithmetic and copies ran while one was open for 0% -> 0% of each run, Pallas kernels for 13% -> 13%
where the time goes in v7:
time: 39.2 us; the launch traced here: 39.1 us
  starting transfers between devices  14.4 us (37%)
  waiting for transfers between devices  13.1 us (33%)
  Pallas kernels  9.77 us (25%)
  between operations  0.74 us (2%)
  local copies, waits for them, and re-layouts  0.73 us (2%)
    ppermute x7, starting transfers between devices, exchange(): return lax.ppermute(block, AXES, pairs)  7.17 us
    ppermute x1, waiting for transfers between devices, shards(): from_side = lax.ppermute(to_side, AXES, route(0, 1))  7 us
    ppermute x7, waiting for transfers between devices, exchange(): return lax.ppermute(block, AXES, pairs)  4.47 us
    pallas_call x1, Pallas kernels, window_backward(): pl.pallas_call(functools.partial(window_kernel, blocks), out_shape=(jax.S...  3.59 us
    ppermute x1, starting transfers between devices, shards(): at_diag = lax.ppermute(diag_start, AXES, route(1, -1))  3.39 us
    pallas_call x1, Pallas kernels, relative_bias(): pl.pallas_call(bias_kernel, out_shape=(shape, shape, jax.ShapeDtypeStruct...  3.38 us
    ppermute x1, starting transfers between devices, shards(): lax.ppermute(jnp.stack([to_lon, from_side[1]]), AXES, route(-1, 0))  1.69 us
    ppermute x1, waiting for transfers between devices, shards(): at_lon = lax.ppermute(lon_start, AXES, route(1, 0))  1.62 us
  transfers between devices with their start and end apart: 12, of which 8 were waited for; matrix products, arithmetic and copies ran while one was open for 0% of the time, Pallas kernels for 13%

profile of v7, /device:TPU:0, one launch (start us, length us, event | category | flops | bytes accessed | tf_op | source)
XLA Modules:
  0.0 39.1 jit_solution(14158940521682893625)
XLA Ops:
  0.6 0.0 copy-start
  0.6 1.1 %pack.1 = (bf16[72,512]{1,0:T(8,128)(2,1)S(1)}, bf16[72,512]{1,0:T(8,128)(2,1)S(1)}, bf16[72,512]{1,0:T(8,128)(2,1)S(1)}, bf16[72,512]{1,0:T(8,128)(2,1)S(1)}, f32[16,529]{1,0:T(8,128)S(1)}) custom-call(bf16[12,12,512]{2,1,0:T(8,128)(2,1)} %tokens_hbm.1, bf16[12,12,512]{2,1,0:T(8,128)(2,1)} %grad_hbm.1, f32[16,529]{1,0:T(8,128)} %table_hbm.1), custom_call_target="tpu_custom_call" | custom-call | bytes 1048576 | tf_op jit(solution)/shard_map/pack/pallas_call | solution.py:61
  1.8 3.4 %collective-permute-start = (bf16[72,512]{1,0:T(8,128)(2,1)S(1)}, bf16[72,512]{1,0:T(8,128)(2,1)S(1)}, u32[]{:S(2)}, u32[]{:S(2)}) collective-permute-start(bf16[72,512]{1,0:T(8,128)(2,1)S(1)} %get-tuple-element.23), channel_id=1, source_target_pairs={{0,7},{1,4},{2,5},{3,6},{4,11},{5,8},{6,9},{7,10},{8,15},{9,12},{1... | collective-permute-start | bytes 221192 | tf_op jit(solution)/shard_map/ppermute | solution.py:423
  5.2 1.5 %collective-permute-start.1 = (bf16[72,512]{1,0:T(8,128)(2,1)S(1)}, bf16[72,512]{1,0:T(8,128)(2,1)S(1)}, u32[]{:S(2)}, u32[]{:S(2)}) collective-permute-start(bf16[72,512]{1,0:T(8,128)(2,1)S(1)} %get-tuple-element.24), channel_id=1, source_target_pairs={{0,4},{1,5},{2,6},{3,7},{4,8},{5,9},{6,10},{7,11},{8,12},{9,13},{1... | collective-permute-start | bytes 221192 | tf_op jit(solution)/shard_map/ppermute | solution.py:422
  6.7 0.6 %collective-permute-start.2 = (bf16[72,512]{1,0:T(8,128)(2,1)S(1)}, bf16[72,512]{1,0:T(8,128)(2,1)S(1)}, u32[]{:S(2)}, u32[]{:S(2)}) collective-permute-start(bf16[72,512]{1,0:T(8,128)(2,1)S(1)} %get-tuple-element.25), channel_id=1, source_target_pairs={{0,3},{1,0},{2,1},{3,2},{4,7},{5,4},{6,5},{7,6},{8,11},{9,8},{10,9... | collective-permute-start | bytes 221192 | tf_op jit(solution)/shard_map/ppermute | solution.py:424
  7.3 3.4 %relative_bias.1 = (f32[2304,128]{1,0:T(8,128)S(1)}, f32[2304,128]{1,0:T(8,128)S(1)}, bf16[512,1536]{1,0:T(8,128)(2,1)S(1)}, bf16[512,512]{1,0:T(8,128)(2,1)S(1)}) custom-call(s32[1]{0:T(128)} %bitcast.2.flag_ref, f32[16,529]{1,0:T(8,128)S(1)} %get-tuple-element.26.table_ref, bf16[512,1536]{1,0:T(8,128)(2,1)} %weight_hbm.1, bf16[512,512]{1,0:T(8,128)(2,1)} %proj_hbm.1), custom_call_target="tpu_custom_call" | custom-call | flops 283115520 | bytes 6291456 | tf_op jit(solution)/shard_map/relative_bias/pallas_call | solution.py:135
  10.7 0.0 collective-permute-done.diag_ref
  10.7 1.6 %collective-permute-done.1.lon_ref = bf16[72,512]{1,0:T(8,128)(2,1)S(1)} collective-permute-done((bf16[72,512]{1,0:T(8,128)(2,1)S(1)}, bf16[72,512]{1,0:T(8,128)(2,1)S(1)}, u32[]{:S(2)}, u32[]{:S(2)}) %collective-permute-start.1) | collective-permute-done | bytes 73760 | tf_op jit(solution)/shard_map/ppermute | solution.py:422
  12.3 0.0 collective-permute-done.2.lat_ref
  12.3 0.0 copy-done
  12.3 3.6 %window_backward.1 = (bf16[144,1536]{1,0:T(8,128)(2,1)S(1)}, f32[144,512]{1,0:T(8,128)S(1)}, f32[144,128]{1,0:T(8,128)S(1)}, f32[152,512]{1,0:T(8,128)S(1)}, bf1...) custom-call(s32[1]{0:T(128)} %bitcast.order_ref, ...), custom_call_target="tpu_custom_call" | custom-call | flops 528482304 | bytes 6291456 | tf_op jit(solution)/shard_map/window_backward/pallas_call | solution.py:305
  15.9 0.1 collective-permute-start.5
  16.0 0.9 %norm_backward.1 = (bf16[36,512]{1,0:T(8,128)(2,1)S(1)}, bf16[36,512]{1,0:T(8,128)(2,1)S(1)}, bf16[2,36,512]{2,1,0:T(8,128)(2,1)S(1)}, bf16[768,512]{1,0:T(8,128)(2,1)S(1)}) custom-call(bf16[144,1536]{1,0:T(8,128)(2,1)S(1)} %get-tuple-element.31.qkv_ref, bf16[512,1536]{1,0:T(8,128)(2,1)S(1)} %get-tuple-element.27.weight_ref, f32[1,512]{1,0:T(1,128)S(1)} %bitcast.35, ...), custom_call_target="tpu_custom_call" | custom-call | flops 226492416 | bytes 3145728 | tf_op jit(solution)/shard_map/norm_backward/pallas_call | solution.py:354
  16.9 1.3 %collective-permute-done.5 = bf16[4,4,48,512]{3,2,1,0:T(8,128)(2,1)S(1)} collective-permute-done((bf16[4,4,48,512]{3,2,1,0:T(8,128)(2,1)S(1)}, bf16[4,4,48,512]{3,2,1,0:T(8,128)(2,1)S(1)}, u32[]{:S(2)}, u32[]{:S(2)}) %collective-permute-start.5) | collective-permute-done | bytes 786464 | tf_op jit(solution)/shard_map/ppermute | solution.py:394
  18.3 0.2 fusion
  18.6 0.1 collective-permute-start.6
  18.6 2.8 %collective-permute-start.8 = (bf16[4,48,512]{2,1,0:T(8,128)(2,1)S(1)}, bf16[4,48,512]{2,1,0:T(8,128)(2,1)S(1)}, u32[]{:S(2)}, u32[]{:S(2)}) collective-permute-start(bf16[4,48,512]{2,1,0:T(8,128)(2,1)S(1)} %get-tuple-element.43), channel_id=1, source_target_pairs={{0,6},{1,7},{2,4},{3,5},{4,2},{5,3},{6,0},{7,1},{8,14},{9,15},{10,... | collective-permute-start | bytes 589832 | tf_op jit(solution)/shard_map/ppermute | solution.py:394
  21.4 0.7 %collective-permute-start.7 = (bf16[4,48,512]{2,1,0:T(8,128)(2,1)S(1)}, bf16[4,48,512]{2,1,0:T(8,128)(2,1)S(1)}, u32[]{:S(2)}, u32[]{:S(2)}) collective-permute-start(bf16[4,48,512]{2,1,0:T(8,128)(2,1)S(1)} %get-tuple-element.44), channel_id=1, source_target_pairs={{0,2},{1,5},{2,0},{3,7},{4,6},{5,1},{6,4},{7,3},{8,10},{9,13},{10,... | collective-permute-start | bytes 589832 | tf_op jit(solution)/shard_map/ppermute | solution.py:394
  22.1 0.0 collective-permute-start.3
  22.1 7.0 %collective-permute-done.3.side_ref = bf16[2,36,512]{2,1,0:T(8,128)(2,1)S(1)} collective-permute-done((bf16[2,36,512]{2,1,0:T(8,128)(2,1)S(1)}, bf16[2,36,512]{2,1,0:T(8,128)(2,1)S(1)}, u32[]{:S(2)}, u32[]{:S(2)}) %collective-permute-start.3) | collective-permute-done | bytes 73760 | tf_op jit(solution)/shard_map/ppermute | solution.py:467
  29.1 1.7 %collective-permute-start.4 = (bf16[2,36,512]{2,1,0:T(8,128)(2,1)S(1)}, bf16[2,36,512]{2,1,0:T(8,128)(2,1)S(1)}, u32[]{:S(2)}, u32[]{:S(2)}) collective-permute-start(bf16[2,36,512]{2,1,0:T(8,128)(2,1)S(1)} %pad_maximum_fusion), channel_id=1, source_target_pairs={{0,28},{1,29},{2,30},{3,31},{4,0},{5,1},{6,2},{7,3},{8,4},{9,5},{1... | collective-permute-start | bytes 221192 | tf_op jit(solution)/shard_map/ppermute | solution.py:468
  30.8 0.0 collective-permute-done.6
  30.8 0.3 collective-permute-done.8
  31.1 0.2 collective-permute-done.7
  31.3 0.1 fusion.3
  31.4 0.8 %collective-permute-start.9 = (bf16[48,512]{1,0:T(8,128)(2,1)S(1)}, bf16[48,512]{1,0:T(8,128)(2,1)S(1)}, u32[]{:S(2)}, u32[]{:S(2)}) collective-permute-start(bf16[48,512]{1,0:T(8,128)(2,1)S(1)} %get-tuple-element.45), channel_id=1, source_target_pairs={{0,16},{1,17},{2,18},{3,19},{4,20},{5,21},{6,22},{7,23},{8,24},{9,... | collective-permute-start | bytes 147464 | tf_op jit(solution)/shard_map/ppermute | solution.py:394
  32.2 1.3 %collective-permute-start.11 = (bf16[48,512]{1,0:T(8,128)(2,1)S(1)}, bf16[48,512]{1,0:T(8,128)(2,1)S(1)}, u32[]{:S(2)}, u32[]{:S(2)}) collective-permute-start(bf16[48,512]{1,0:T(8,128)(2,1)S(1)} %get-tuple-element.46), channel_id=1, source_target_pairs={{0,24},{1,25},{2,26},{3,27},{4,28},{5,29},{6,30},{7,31},{8,16},{9,... | collective-permute-start | bytes 147464 | tf_op jit(solution)/shard_map/ppermute | solution.py:394
  33.5 1.4 %collective-permute-start.10 = (bf16[48,512]{1,0:T(8,128)(2,1)S(1)}, bf16[48,512]{1,0:T(8,128)(2,1)S(1)}, u32[]{:S(2)}, u32[]{:S(2)}) collective-permute-start(bf16[48,512]{1,0:T(8,128)(2,1)S(1)} %get-tuple-element.47), channel_id=1, source_target_pairs={{0,8},{1,9},{2,10},{3,11},{4,12},{5,13},{6,14},{7,15},{8,0},{9,1},... | collective-permute-start | bytes 147464 | tf_op jit(solution)/shard_map/ppermute | solution.py:394
  35.0 0.0 collective-permute-done.4.lon_ref
  35.0 0.7 %unpack.1 = bf16[12,12,512]{2,1,0:T(8,128)(2,1)} custom-call(bf16[2,36,512]{2,1,0:T(8,128)(2,1)S(1)} %collective-permute-done.4.lon_ref, bf16[2,36,512]{2,1,0:T(8,128)(2,1)S(1)} %collective-permute-done.3.side_ref, bf16[36,512]{1,0:T(8,128)(2,1)S(1)} %get-tuple-element.39.own_ref), custom_call_target="tpu_custom_call" | custom-call | bytes 524288 | tf_op jit(solution)/shard_map/unpack/pallas_call | solution.py:380
  35.7 1.6 %collective-permute-done.9 = bf16[48,512]{1,0:T(8,128)(2,1)S(1)} collective-permute-done((bf16[48,512]{1,0:T(8,128)(2,1)S(1)}, bf16[48,512]{1,0:T(8,128)(2,1)S(1)}, u32[]{:S(2)}, u32[]{:S(2)}) %collective-permute-start.9) | collective-permute-done | bytes 49184 | tf_op jit(solution)/shard_map/ppermute | solution.py:394
  37.3 0.9 %collective-permute-done.11 = bf16[48,512]{1,0:T(8,128)(2,1)S(1)} collective-permute-done((bf16[48,512]{1,0:T(8,128)(2,1)S(1)}, bf16[48,512]{1,0:T(8,128)(2,1)S(1)}, u32[]{:S(2)}, u32[]{:S(2)}) %collective-permute-start.11) | collective-permute-done | bytes 49184 | tf_op jit(solution)/shard_map/ppermute | solution.py:394
  38.2 0.1 collective-permute-done.10
  38.4 0.7 %copy.8 = f32[6,4,8,128]{3,1,2,0:T(4,128)} copy(f32[6,4,8,128]{3,2,1,0:T(8,128)S(1)} %fusion.7) | data formatting | bytes 196608
  (5 shorter events, 0.1 us)
Async XLA Ops:
  0.6 11.7 %copy-start = (f32[512]{0:T(512)S(1)}, f32[512]{0:T(512)}, u32[]{:S(2)}) copy-start(f32[512]{0:T(512)} %param.7) | copy-start | bytes 6148
  1.8 8.9 %collective-permute-start = (bf16[72,512]{1,0:T(8,128)(2,1)S(1)}, bf16[72,512]{1,0:T(8,128)(2,1)S(1)}, u32[]{:S(2)}, u32[]{:S(2)}) collective-permute-start(bf16[72,512]{1,0:T(8,128)(2,1)S(1)} %get-tuple-element.23), channel_id=1, source_target_pairs={{0,7},{1,4},{2,5},{3,6},{4,11},{5,8},{6,9},{7,10},{8,15},{9,12},{1... | collective-permute-start | bytes 221192 | tf_op jit(solution)/shard_map/ppermute | solution.py:423
  5.2 7.1 %collective-permute-start.1 = (bf16[72,512]{1,0:T(8,128)(2,1)S(1)}, bf16[72,512]{1,0:T(8,128)(2,1)S(1)}, u32[]{:S(2)}, u32[]{:S(2)}) collective-permute-start(bf16[72,512]{1,0:T(8,128)(2,1)S(1)} %get-tuple-element.24), channel_id=1, source_target_pairs={{0,4},{1,5},{2,6},{3,7},{4,8},{5,9},{6,10},{7,11},{8,12},{9,13},{1... | collective-permute-start | bytes 221192 | tf_op jit(solution)/shard_map/ppermute | solution.py:422
  6.7 5.6 %collective-permute-start.2 = (bf16[72,512]{1,0:T(8,128)(2,1)S(1)}, bf16[72,512]{1,0:T(8,128)(2,1)S(1)}, u32[]{:S(2)}, u32[]{:S(2)}) collective-permute-start(bf16[72,512]{1,0:T(8,128)(2,1)S(1)} %get-tuple-element.25), channel_id=1, source_target_pairs={{0,3},{1,0},{2,1},{3,2},{4,7},{5,4},{6,5},{7,6},{8,11},{9,8},{10,9... | collective-permute-start | bytes 221192 | tf_op jit(solution)/shard_map/ppermute | solution.py:424
  15.9 2.4 %collective-permute-start.5 = (bf16[4,4,48,512]{3,2,1,0:T(8,128)(2,1)S(1)}, bf16[4,4,48,512]{3,2,1,0:T(8,128)(2,1)S(1)}, u32[]{:S(2)}, u32[]{:S(2)}) collective-permute-start(bf16[4,4,48,512]{3,2,1,0:T(8,128)(2,1)S(1)} %bitcast.36), channel_id=1, source_target_pairs={{0,1},{1,0},{2,3},{3,2},{4,5},{5,4},{6,7},{7,6},{8,9},{9,8},{10,11... | collective-permute-start | bytes 2359304 | tf_op jit(solution)/shard_map/ppermute | solution.py:394
  18.6 12.3 %collective-permute-start.6 = (bf16[4,48,512]{2,1,0:T(8,128)(2,1)S(1)}, bf16[4,48,512]{2,1,0:T(8,128)(2,1)S(1)}, u32[]{:S(2)}, u32[]{:S(2)}) collective-permute-start(bf16[4,48,512]{2,1,0:T(8,128)(2,1)S(1)} %get-tuple-element.42), channel_id=1, source_target_pairs={{0,4},{1,3},{2,6},{3,1},{4,0},{5,7},{6,2},{7,5},{8,12},{9,11},{10,... | collective-permute-start | bytes 589832 | tf_op jit(solution)/shard_map/ppermute | solution.py:394
  18.6 12.5 %collective-permute-start.8 = (bf16[4,48,512]{2,1,0:T(8,128)(2,1)S(1)}, bf16[4,48,512]{2,1,0:T(8,128)(2,1)S(1)}, u32[]{:S(2)}, u32[]{:S(2)}) collective-permute-start(bf16[4,48,512]{2,1,0:T(8,128)(2,1)S(1)} %get-tuple-element.43), channel_id=1, source_target_pairs={{0,6},{1,7},{2,4},{3,5},{4,2},{5,3},{6,0},{7,1},{8,14},{9,15},{10,... | collective-permute-start | bytes 589832 | tf_op jit(solution)/shard_map/ppermute | solution.py:394
  21.4 9.9 %collective-permute-start.7 = (bf16[4,48,512]{2,1,0:T(8,128)(2,1)S(1)}, bf16[4,48,512]{2,1,0:T(8,128)(2,1)S(1)}, u32[]{:S(2)}, u32[]{:S(2)}) collective-permute-start(bf16[4,48,512]{2,1,0:T(8,128)(2,1)S(1)} %get-tuple-element.44), channel_id=1, source_target_pairs={{0,2},{1,5},{2,0},{3,7},{4,6},{5,1},{6,4},{7,3},{8,10},{9,13},{10,... | collective-permute-start | bytes 589832 | tf_op jit(solution)/shard_map/ppermute | solution.py:394
  22.1 7.0 %collective-permute-start.3 = (bf16[2,36,512]{2,1,0:T(8,128)(2,1)S(1)}, bf16[2,36,512]{2,1,0:T(8,128)(2,1)S(1)}, u32[]{:S(2)}, u32[]{:S(2)}) collective-permute-start(bf16[2,36,512]{2,1,0:T(8,128)(2,1)S(1)} %get-tuple-element.38), channel_id=1, source_target_pairs={{0,1},{1,2},{2,3},{3,0},{4,5},{5,6},{6,7},{7,4},{8,9},{9,10},{10,1... | collective-permute-start | bytes 221192 | tf_op jit(solution)/shard_map/ppermute | solution.py:467
  29.1 5.8 %collective-permute-start.4 = (bf16[2,36,512]{2,1,0:T(8,128)(2,1)S(1)}, bf16[2,36,512]{2,1,0:T(8,128)(2,1)S(1)}, u32[]{:S(2)}, u32[]{:S(2)}) collective-permute-start(bf16[2,36,512]{2,1,0:T(8,128)(2,1)S(1)} %pad_maximum_fusion), channel_id=1, source_target_pairs={{0,28},{1,29},{2,30},{3,31},{4,0},{5,1},{6,2},{7,3},{8,4},{9,5},{1... | collective-permute-start | bytes 221192 | tf_op jit(solution)/shard_map/ppermute | solution.py:468
  31.4 5.9 %collective-permute-start.9 = (bf16[48,512]{1,0:T(8,128)(2,1)S(1)}, bf16[48,512]{1,0:T(8,128)(2,1)S(1)}, u32[]{:S(2)}, u32[]{:S(2)}) collective-permute-start(bf16[48,512]{1,0:T(8,128)(2,1)S(1)} %get-tuple-element.45), channel_id=1, source_target_pairs={{0,16},{1,17},{2,18},{3,19},{4,20},{5,21},{6,22},{7,23},{8,24},{9,... | collective-permute-start | bytes 147464 | tf_op jit(solution)/shard_map/ppermute | solution.py:394
  32.2 6.0 %collective-permute-start.11 = (bf16[48,512]{1,0:T(8,128)(2,1)S(1)}, bf16[48,512]{1,0:T(8,128)(2,1)S(1)}, u32[]{:S(2)}, u32[]{:S(2)}) collective-permute-start(bf16[48,512]{1,0:T(8,128)(2,1)S(1)} %get-tuple-element.46), channel_id=1, source_target_pairs={{0,24},{1,25},{2,26},{3,27},{4,28},{5,29},{6,30},{7,31},{8,16},{9,... | collective-permute-start | bytes 147464 | tf_op jit(solution)/shard_map/ppermute | solution.py:394
  33.5 4.8 %collective-permute-start.10 = (bf16[48,512]{1,0:T(8,128)(2,1)S(1)}, bf16[48,512]{1,0:T(8,128)(2,1)S(1)}, u32[]{:S(2)}, u32[]{:S(2)}) collective-permute-start(bf16[48,512]{1,0:T(8,128)(2,1)S(1)} %get-tuple-element.47), channel_id=1, source_target_pairs={{0,8},{1,9},{2,10},{3,11},{4,12},{5,13},{6,14},{7,15},{8,0},{9,1},... | collective-permute-start | bytes 147464 | tf_op jit(solution)/shard_map/ppermute | solution.py:394
